TPU v7x, 128 devices: a whole 4x4x4 slice. The times are simulated.
128 devices in a mesh: dp: 8 (over z, y_hi), ctx: 16 (over x, y_lo, core).
Axes of the slice: x: 4, y: 4 (y_hi: 2, y_lo: 2; y = y_hi * 2 + y_lo), z: 4, core: 2. Of those that a mesh axis runs over, the one named last changes fastest.
Arguments:
- tokens: bfloat16 [8, 8192, 1024], P('dp', 'ctx'), may hold values from -60 to 60
- kept: int32 [8, 4096], P('dp', 'ctx'), may hold values from 0 to 8191, as said below
- gain_attn: float32 [1024], replicated, may hold values from 0.25 to 1.75
- gain_ffn: float32 [1024], replicated, may hold values from 0.25 to 1.75
- w_query: bfloat16 [1024, 1024], P(None, 'ctx'), may hold values from -4 to 4
- w_key: bfloat16 [1024, 1024], P(None, 'ctx'), may hold values from -4 to 4
- w_value: bfloat16 [1024, 1024], P(None, 'ctx'), may hold values from -0.1875 to 0.1875
- w_out: bfloat16 [1024, 1024], P('ctx'), may hold values from -0.1875 to 0.1875
- expert_ids: int32 [8, 4096, 1], P('dp', 'ctx'), may hold values from 0 to 127; in each aligned block of 256 rows (0 to 255, 256 to 511, ..., all dimensions but the last counted through in order) at most 4 rows name the same one
- w_in: bfloat16 [128, 1024, 2816], P(('dp', 'ctx')), may hold values from -0.1875 to 0.1875
- w_back: bfloat16 [128, 2816, 1024], P(('dp', 'ctx')), may hold values from -0.109375 to 0.109375
Outputs:
- blended: bfloat16 [8, 8192, 1024], P('dp', 'ctx')
Inputs may be any that keep to these rules, and one draw needn't show every extreme that they name: `kept`: in each document row, entries j * 256 to (j + 1) * 256 - 1 are strictly increasing positions from j * 512 to (j + 1) * 512 - 1. `expert_ids`: in each aligned block of 256 rows (the kept positions of one block b) no expert is named more than 4 times.
All inputs are finite; a program needn't handle non-finite values.
Results may differ from a plain program's by a relative error of at most 0.007.
Values may be sent and summed in bfloat16 or wider, within the bound.
No kernel may reach another device: no remote copies, remote signals or barrier semaphores. Data moves between devices by JAX's collectives and lax.ppermute only.
A program may use at most 64 MiB of HBM per device.

v0:
```python
import math

import jax
import jax.numpy as jnp
from jax import lax
from jax.sharding import PartitionSpec as P

HS = 64


eps_norm = 1e-06
score_gain = 2.5


def rms_scale(values, gain):
    values = values.astype(jnp.float32)
    power = jnp.mean(values * values, axis=-1, keepdims=True)
    return values * lax.rsqrt(power + eps_norm) * gain


def attend(queries, keys, values):
    count, heads_here, width = queries.shape
    block = 512
    scale = score_gain / math.sqrt(width)
    blocks = queries.reshape(count // block, block, heads_here, width)

    def one_block(block_rows):
        scores = (
            jnp.einsum("qhd,khd->hqk", block_rows, keys, preferred_element_type=jnp.float32) * scale
        )
        top = jnp.max(scores, axis=-1, keepdims=True)
        weights = jnp.exp(scores - top)
        probs = (weights / jnp.sum(weights, axis=-1, keepdims=True)).astype(jnp.bfloat16)
        mixed = jnp.einsum("hqk,khd->qhd", probs, values, preferred_element_type=jnp.float32)
        return mixed.astype(jnp.bfloat16)

    return lax.map(one_block, blocks).reshape(count, heads_here, width)


def body(
    tokens, kept, gain_attn, gain_ffn, w_query, w_key, w_value, w_out, expert_ids, w_in, w_back
):
    document = tokens[0]
    shard_len, width_model = document.shape
    ctx_count = lax.axis_size("ctx")
    dp_count = lax.axis_size("dp")
    local = kept[0] - lax.axis_index("ctx") * shard_len
    rows = jnp.take(document, local, axis=0)
    keep_here = rows.shape[0]
    normed = rms_scale(rows, gain_attn).astype(jnp.bfloat16)
    head_width = HS
    heads_here = w_query.shape[1] // head_width
    stacked = jnp.stack([w_query, w_key, w_value], axis=1)
    triple = jnp.einsum(
        "td,dcf->tcf",
        lax.all_gather(normed, "ctx", axis=0, tiled=True),
        stacked,
        preferred_element_type=jnp.float32,
    ).astype(jnp.bfloat16)
    triple = triple.reshape(triple.shape[0], 3, heads_here, head_width)
    mixed = attend(triple[:, 0], triple[:, 1], triple[:, 2])
    flat_mixed = mixed.reshape(mixed.shape[0], heads_here * head_width)
    attn = lax.psum_scatter(
        jnp.dot(flat_mixed, w_out, preferred_element_type=jnp.float32).astype(jnp.bfloat16),
        "ctx",
        scatter_dimension=0,
        tiled=True,
    ).astype(jnp.float32)
    first = rows.astype(jnp.float32) + attn
    ffn_in = rms_scale(first, gain_ffn).astype(jnp.bfloat16)
    expert_here = w_in.shape[0]
    owners = dp_count * ctx_count
    experts_all = expert_here * owners
    capacity = 2 * keep_here // experts_all
    labels = expert_ids[0, :, 0]
    choose = (labels[:, None] == jnp.arange(experts_all, dtype=jnp.int32)[None, :]).astype(
        jnp.float32
    )
    order = jnp.arange(keep_here, dtype=jnp.int32)
    earlier = (order[None, :] < order[:, None]).astype(jnp.float32)
    before = jnp.dot(earlier, choose, precision=lax.Precision.HIGHEST)
    slots = jnp.sum(before * choose, axis=1).astype(jnp.int32)
    place = labels * capacity + slots
    spots = (place[None, :] == jnp.arange(experts_all * capacity, dtype=jnp.int32)[:, None]).astype(
        jnp.bfloat16
    )
    buffer = jnp.dot(spots, ffn_in, preferred_element_type=jnp.float32).astype(jnp.bfloat16)
    buffer = buffer.reshape(experts_all, capacity, width_model)
    received = lax.all_to_all(buffer, ("dp", "ctx"), split_axis=0, concat_axis=0, tiled=True)
    items = received.shape[1]
    grouped = received.reshape(owners, expert_here, items, width_model)
    hidden = jnp.einsum("sgid,gdf->sgif", grouped, w_in, preferred_element_type=jnp.float32)
    hidden = jnp.maximum(hidden, 0.0).astype(jnp.bfloat16)
    answer = jnp.einsum("sgif,gfd->sgid", hidden, w_back, preferred_element_type=jnp.float32)
    answered = answer.astype(jnp.bfloat16).reshape(owners * expert_here, items, width_model)
    back = lax.all_to_all(answered, ("dp", "ctx"), split_axis=0, concat_axis=0, tiled=True)
    answers = back.reshape(experts_all * capacity, width_model)
    taken = jnp.take(answers, place, axis=0)
    second = (first + taken.astype(jnp.float32)).astype(jnp.bfloat16)
    blended = document.at[local].set(second)
    return blended[None]


def solution(mesh):
    return jax.shard_map(
        body,
        mesh=mesh,
        in_specs=(
            P("dp", "ctx", None),
            P("dp", "ctx"),
            P(),
            P(),
            P(None, "ctx"),
            P(None, "ctx"),
            P(None, "ctx"),
            P("ctx", None),
            P("dp", "ctx", None),
            P(("dp", "ctx"), None, None),
            P(("dp", "ctx"), None, None),
        ),
        out_specs=P("dp", "ctx", None),
        check_vma=False,
    )
```

profile of v0, /device:TPU:1, one launch (start us, length us, event | category | flops | bytes accessed | tf_op | source)
XLA Modules:
  0.0 304.4 jit_solution(5685941121041606233)
XLA Ops:
  10.1 1.8 fusion.24
  12.0 55.7 %all-gather.2.cloned.1.call-done = bf16[4096,1024]{1,0:T(8,128)(2,1)} async-done(((bf16[256,1024]{1,0:T(8,128)(2,1)}), bf16[4096,1024]{1,0:T(8,128)(2,1)}) %all-gather.2.cloned.1.call-update) | async-done | bytes 8388624 | tf_op jit(solution)/shard_map/all_gather | solution.py:56
  67.7 6.3 %fusion.40 = f32[4096,192]{0,1:S(1)} fusion(bf16[4096,1024]{1,0:T(8,128)(2,1)} %all-gather.2.cloned.1.call-done, bf16[1024,192]{0,1:T(8,128)(2,1)S(1)} %bitcast.86), kind=kOutput, calls=%fused_computation.67 | convolution fusion | flops 1610612736 | bytes 11927552
  75.4 41.4 %while.10 = (s32[]{:T(128)}, bf16[8,512,1,64]{1,3,2,0:T(8,128)(2,1)S(1)}, bf16[8,512,1,64]{1,3,2,0:T(8,128)(2,1)S(1)}, bf16[4096,1,64]{0,2,1:T(8,128)(2,1)S(1)}, bf16[4096,1,64]{0,2,1:T(8,128)(2,1)}, /*index=5*/s32[]{:T(128)}) while((s32[]{:T(128)}, bf16[8,512,1,64]{1,3,2,0:T(8,128)(2,1)S(1)}, bf16[8,512,1,64]{1,3,2,0:T(8,128)(2,1)S(1)}, ...), condition=%wide.region_4.6_spmd, body=%wide.region_1.5_spmd.sunk | while | flops 555777024 | bytes 28452968 | solution.py:37
  76.8 1.5 fusion.49
  78.4 2.3 fusion.50
  82.0 1.5 fusion.49
  83.5 2.3 fusion.50
  88.7 2.3 fusion.50
  93.9 2.3 fusion.50
  99.1 2.3 fusion.50
  104.2 2.3 fusion.50
  107.9 1.5 fusion.49
  109.4 2.3 fusion.50
  114.6 2.3 fusion.50
  117.0 5.6 %convolution_convert_fusion = bf16[4096,1024]{1,0:T(8,128)(2,1)} fusion(bf16[4096,64]{0,1:T(8,128)(2,1)S(1)} %bitcast.83, bf16[64,1024]{1,0:T(8,128)(2,1)S(1)} %copy-done), kind=kOutput, calls=%fused_computation.18 | convolution fusion | flops 541065216 | bytes 9043968 | tf_op jit(solution)/shard_map/dot_general | solution.py:64
  122.9 97.2 %reduce-scatter.2.cloned.1.call-done = bf16[256,1024]{1,0:T(8,128)(2,1)} async-done(((bf16[4096,1024]{1,0:T(8,128)(2,1)}), bf16[256,1024]{1,0:T(8,128)(2,1)}) %reduce-scatter.2.cloned.1.call-update) | async-done | bytes 524304 | tf_op jit(solution)/shard_map/reduce_scatter | solution.py:63
  221.5 2.7 convolution_convert_fusion.1
  225.7 28.1 %all_to_all.10 = bf16[128,4,1024]{2,1,0:T(4,128)(2,1)} all-to-all(bf16[128,4,1024]{2,1,0:T(4,128)(2,1)S(1)} %reshape.113), channel_id=1, replica_groups=mesh['dp'=8,'ctx'=16] {'dp','ctx'}, dimensions={0} | all-to-all | bytes 2097152 | tf_op jit(solution)/shard_map/all_to_all | solution.py:89
  253.8 11.2 %fusion.18 = bf16[128,4,1024]{2,0,1:T(8,128)(2,1)S(1)} fusion(bf16[1,2816,1024]{2,1,0:T(8,128)(2,1)} %param.25, bf16[1,1024,2816]{2,1,0:T(8,128)(2,1)} %param.24, bf16[128,4,1024]{2,1,0:T(4,128)(2,1)} %all_to_all.10), kind=kOutput, calls=%fused_computation.28 | convolution fusion | flops 5908987904 | bytes 13631488 | tf_op jit(solution)/shard_map/sgif,gfd->sgid/dot_general | solution.py:94
  265.0 1.8 copy.25
  266.8 5.1 %all-to-all-start.1 = ((bf16[128,4,1024]{2,1,0:T(4,128)(2,1)}), bf16[128,4,1024]{2,1,0:T(4,128)(2,1)}, u32[]{:S(2)}, u32[]{:S(2)}) async-start(bf16[128,4,1024]{2,1,0:T(4,128)(2,1)} %copy.25), calls=%async_computation.2 | async-start | bytes 2097152 | tf_op jit(solution)/shard_map/all_to_all | solution.py:96
  271.9 19.1 %all-to-all-done.1 = bf16[128,4,1024]{2,1,0:T(4,128)(2,1)} async-done(((bf16[128,4,1024]{2,1,0:T(4,128)(2,1)}), bf16[128,4,1024]{2,1,0:T(4,128)(2,1)}, u32[]{:S(2)}, u32[]{:S(2)}) %all-to-all-start.1) | async-done | bytes 1048608 | tf_op jit(solution)/shard_map/all_to_all | solution.py:96
  292.4 4.2 %scatter_custom_fusion = bf16[512,1024]{1,0:T(8,128)(2,1)S(1)} fusion(bf16[512,1024]{1,0:T(8,128)(2,1)S(1)} %bitcast.81, s32[256]{0:T(256)S(1)} %bitcast.93, bf16[256,1024]{1,0:T(8,128)(2,1)S(1)} %copy-done.2, pred[256]{0:T(512)(128)(4,1)S(1)} %compare_and_fusion, bf16[]{:T(256)} %constant.10.clone.2, bf16[512,1024]{1,0:T(8,128)(2,1)S(1)} %reshape.116, ...), kind=kCustom, calls=%fused_computation.39 | custom fusion | flops 2097152 | bytes 3150850 | tf_op jit(solution)/shard_map/scatter | solution.py:100
  (72 shorter events, 29.1 us)
Async XLA Ops:
  6.5 110.4 %copy-start = (bf16[64,1024]{1,0:T(8,128)(2,1)S(1)}, bf16[64,1024]{1,0:T(8,128)(2,1)}, u32[]{:S(2)}) copy-start(bf16[64,1024]{1,0:T(8,128)(2,1)} %param.22) | copy-start | bytes 393220
  6.5 5.4 %copy-start.6 = (bf16[1024,64]{0,1:T(8,128)(2,1)S(1)}, bf16[1024,64]{0,1:T(8,128)(2,1)}, u32[]{:S(2)}) copy-start(bf16[1024,64]{0,1:T(8,128)(2,1)} %param.19) | copy-start | bytes 393220
  6.5 5.4 %copy-start.5 = (bf16[1024,64]{0,1:T(8,128)(2,1)S(1)}, bf16[1024,64]{0,1:T(8,128)(2,1)}, u32[]{:S(2)}) copy-start(bf16[1024,64]{0,1:T(8,128)(2,1)} %param.20) | copy-start | bytes 393220
  6.5 5.4 %copy-start.4 = (bf16[1024,64]{0,1:T(8,128)(2,1)S(1)}, bf16[1024,64]{0,1:T(8,128)(2,1)}, u32[]{:S(2)}) copy-start(bf16[1024,64]{0,1:T(8,128)(2,1)} %param.21) | copy-start | bytes 393220
  6.5 61.2 %all-gather.2.cloned.1.call-start = ((), (), s32[]{:S(2)}) async-start(), calls=%async_computation.3 | async-start | bytes 8912896 | tf_op jit(solution)/shard_map/all_gather | solution.py:56
  11.8 208.2 %reduce-scatter.2.cloned.1.call-start = ((), (), s32[]{:S(2)}) async-start(), calls=%async_computation.4 | async-start | bytes 8912896 | tf_op jit(solution)/shard_map/reduce_scatter | solution.py:63
  75.5 2.9 copy-start.3
  80.6 2.9 copy-start.3
  85.8 2.9 copy-start.3
  91.0 2.9 copy-start.3
  96.2 2.9 copy-start.3
  101.4 2.9 copy-start.3
  106.5 2.9 copy-start.3
  111.7 2.9 copy-start.3
  116.9 5.7 %copy-start.7 = (s32[1,256,1]{1,2,0:T(1,128)S(1)}, s32[1,256,1]{1,2,0:T(1,128)}, u32[]{:S(2)}) copy-start(s32[1,256,1]{1,2,0:T(1,128)} %param.23) | copy-start | bytes 3076
  117.0 104.6 %copy-start.8 = (f32[1024]{0:T(1024)S(1)}, f32[1024]{0:T(1024)}, u32[]{:S(2)}) copy-start(f32[1024]{0:T(1024)} %param.18) | copy-start | bytes 12292
  253.8 38.5 %copy-start.2 = (bf16[256,1024]{1,0:T(8,128)(2,1)S(1)}, bf16[256,1024]{1,0:T(8,128)(2,1)}, u32[]{:S(2)}) copy-start(bf16[256,1024]{1,0:T(8,128)(2,1)} %reduce-scatter.2.cloned.1.call-done) | copy-start | bytes 1572868
  266.8 24.2 %all-to-all-start.1 = ((bf16[128,4,1024]{2,1,0:T(4,128)(2,1)}), bf16[128,4,1024]{2,1,0:T(4,128)(2,1)}, u32[]{:S(2)}, u32[]{:S(2)}) async-start(bf16[128,4,1024]{2,1,0:T(4,128)(2,1)} %copy.25), calls=%async_computation.2 | async-start | bytes 2097152 | tf_op jit(solution)/shard_map/all_to_all | solution.py:96
  296.6 1.0 copy-start.1
Sparse Core Ops, SparseCore 0:
  12.0 55.7 all-gather.1
  122.7 97.3 reduce-scatter.1
where the time goes:
time: 305 us; the launch traced here: 304 us
  waiting for transfers between devices  172 us (56%)
  matrix products  55 us (18%)
  blocking collectives  28.1 us (9%)
  other arithmetic  20.7 us (7%)
  between operations  13.6 us (4%)
  local copies, waits for them, and re-layouts  9.36 us (3%)
  starting transfers between devices  5.16 us (2%)
    reduce_scatter x1, waiting for transfers between devices, body(): lax.psum_scatter(jnp.dot(flat_mixed, w_out, preferred_element_type=jnp.fl...  97.2 us
    all_gather x1, waiting for transfers between devices, body(): lax.all_gather(normed, 'ctx', axis=0, tiled=True)  55.7 us
    all_to_all x1, blocking collectives, body(): lax.all_to_all(buffer, ('dp', 'ctx'), split_axis=0, concat_axis=0, tiled=...  28.1 us
    all_to_all x1, waiting for transfers between devices, body(): lax.all_to_all(answered, ('dp', 'ctx'), split_axis=0, concat_axis=0, tile...  19.1 us
    dot_general x8, matrix products, one_block(): jnp.einsum('hqk,khd->qhd', probs, values, preferred_element_type=jnp.floa...  18.1 us
    reduce_sum x8, other arithmetic, one_block(): jnp.sum(weights, axis=-1, keepdims=True)  12 us
    dot_general x1, matrix products, body(): jnp.einsum('sgif,gfd->sgid', hidden, w_back, preferred_element_type=jnp.f...  11.2 us
    dot_general x8, matrix products, one_block(): jnp.einsum('qhd,khd->hqk', block_rows, keys, preferred_element_type=jnp.f...  10.9 us
  transfers between devices with their start and end apart: 3, of which 3 were waited for; matrix products, arithmetic and copies ran while one was open for 0% of the time, Pallas kernels for 0%

commit v1 on v0

--- a/solution.py
+++ b/solution.py
@@ -51,21 +51,27 @@
     head_width = HS
     heads_here = w_query.shape[1] // head_width
     stacked = jnp.stack([w_query, w_key, w_value], axis=1)
+    gathered = lax.all_gather(normed, "ctx", axis=0, tiled=True)
     triple = jnp.einsum(
         "td,dcf->tcf",
-        lax.all_gather(normed, "ctx", axis=0, tiled=True),
+        gathered,
         stacked,
         preferred_element_type=jnp.float32,
     ).astype(jnp.bfloat16)
     triple = triple.reshape(triple.shape[0], 3, heads_here, head_width)
     mixed = attend(triple[:, 0], triple[:, 1], triple[:, 2])
     flat_mixed = mixed.reshape(mixed.shape[0], heads_here * head_width)
-    attn = lax.psum_scatter(
-        jnp.dot(flat_mixed, w_out, preferred_element_type=jnp.float32).astype(jnp.bfloat16),
+    parts = lax.all_to_all(
+        flat_mixed.reshape(ctx_count, keep_here, heads_here * head_width),
         "ctx",
-        scatter_dimension=0,
+        split_axis=0,
+        concat_axis=0,
         tiled=True,
-    ).astype(jnp.float32)
+    )
+    w_rows, _ = lax.optimization_barrier((w_out, gathered))
+    w_all = lax.all_gather(w_rows, "ctx", axis=0, tiled=True)
+    mine = jnp.transpose(parts, (1, 0, 2)).reshape(keep_here, -1)
+    attn = jnp.dot(mine, w_all, preferred_element_type=jnp.float32)
     first = rows.astype(jnp.float32) + attn
     ffn_in = rms_scale(first, gain_ffn).astype(jnp.bfloat16)
     expert_here = w_in.shape[0]

time: 305 us -> 223 us (0.73)
  waiting for transfers between devices: 172 us -> 84.2 us
  starting transfers between devices: 5.16 us -> 10.3 us
  local copies, waits for them, and re-layouts: 9.36 us -> 12.8 us
    reduce_scatter x1 -> x0, waiting for transfers between devices: 97.2 us -> none  [body(): lax.psum_scatter(jnp.dot(flat_mixed, w_out, preferred_element_type=jnp.fl...]
    all_to_all x0 -> x1, waiting for transfers between devices: none -> 9.38 us  [body(): lax.all_to_all(flat_mixed.reshape(ctx_count, keep_here, heads_here * head...]
    all_to_all x0 -> x1, starting transfers between devices: none -> 5.14 us  [body(): lax.all_to_all(flat_mixed.reshape(ctx_count, keep_here, heads_here * head...]
    dot_general x8, matrix products: 18.1 us -> 23.2 us  [one_block(): jnp.einsum('hqk,khd->qhd', probs, values, preferred_element_type=jnp.floa...]
    dot_general x1, matrix products: 5.61 us -> 2.42 us  [body(): attn = jnp.dot(mine, w_all, preferred_element_type=jnp.float32)]
    all_gather x1 -> x2, waiting for transfers between devices: 55.7 us -> 55.7 us  [the longest x1 55.7 us: body(): gathered = lax.all_gather(normed, 'ctx', axis=0, tiled=True)]
  transfers between devices with their start and end apart: 3 -> 4, of which waited for: 3 -> 3; matrix products, arithmetic and copies ran while one was open for 0% -> 25% of each run, Pallas kernels for 0% -> 0%
where the time goes in v1:
time: 223 us; the launch traced here: 222 us
  waiting for transfers between devices  84.2 us (38%)
  matrix products  55.4 us (25%)
  blocking collectives  27.3 us (12%)
  other arithmetic  18.5 us (8%)
  between operations  13.6 us (6%)
  local copies, waits for them, and re-layouts  12.8 us (6%)
  starting transfers between devices  10.3 us (5%)
    all_gather x1, waiting for transfers between devices, body(): gathered = lax.all_gather(normed, 'ctx', axis=0, tiled=True)  55.7 us
    all_to_all x1, blocking collectives, body(): lax.all_to_all(buffer, ('dp', 'ctx'), split_axis=0, concat_axis=0, tiled=...  27.3 us
    dot_general x8, matrix products, one_block(): jnp.einsum('hqk,khd->qhd', probs, values, preferred_element_type=jnp.floa...  23.2 us
    all_to_all x1, waiting for transfers between devices, body(): lax.all_to_all(answered, ('dp', 'ctx'), split_axis=0, concat_axis=0, tile...  19.1 us
    reduce_sum x8, other arithmetic, one_block(): jnp.sum(weights, axis=-1, keepdims=True)  12 us
    dot_general x1, matrix products, body(): jnp.einsum('sgif,gfd->sgid', hidden, w_back, preferred_element_type=jnp.f...  11.8 us
    dot_general x8, matrix products, one_block(): jnp.einsum('qhd,khd->hqk', block_rows, keys, preferred_element_type=jnp.f...  10.9 us
    all_to_all x1, waiting for transfers between devices, body(): lax.all_to_all(flat_mixed.reshape(ctx_count, keep_here, heads_here * head...  9.38 us
  transfers between devices with their start and end apart: 4, of which 3 were waited for; matrix products, arithmetic and copies ran while one was open for 25% of the time, Pallas kernels for 0%

profile of v1, /device:TPU:1, one launch (start us, length us, event | category | flops | bytes accessed | tf_op | source)
XLA Modules:
  0.0 222.2 jit_solution(10503088453496204175)
XLA Ops:
  11.4 55.7 %all-gather.3.cloned.1.call-done = bf16[4096,1024]{1,0:T(8,128)(2,1)} async-done(((bf16[256,1024]{1,0:T(8,128)(2,1)}), bf16[4096,1024]{1,0:T(8,128)(2,1)}) %all-gather.3.cloned.1.call-update) | async-done | bytes 8388624 | tf_op jit(solution)/shard_map/all_gather | solution.py:54
  67.1 6.3 %fusion.40 = f32[4096,192]{0,1:S(1)} fusion(bf16[4096,1024]{1,0:T(8,128)(2,1)} %all-gather.3.cloned.1.call-done, bf16[1024,192]{0,1:T(8,128)(2,1)S(1)} %bitcast.88), kind=kOutput, calls=%fused_computation.66 | convolution fusion | flops 1610612736 | bytes 11927552
  74.9 46.2 %while.10 = (s32[]{:T(128)}, bf16[8,512,1,64]{1,3,2,0:T(8,128)(2,1)}, bf16[8,512,1,64]{1,3,2,0:T(8,128)(2,1)S(1)}, bf16[4096,1,64]{0,2,1:T(8,128)(2,1)S(1)}, bf16[4096,1,64]{0,2,1:T(8,128)(2,1)}, /*index=5*/s32[]{:T(128)}) while((s32[]{:T(128)}, bf16[8,512,1,64]{1,3,2,0:T(8,128)(2,1)}, bf16[8,512,1,64]{1,3,2,0:T(8,128)(2,1)S(1)}, ...), condition=%wide.region_4.6_spmd, body=%wide.region_1.5_spmd.sunk | while | flops 555777024 | bytes 28452976 | solution.py:37
  76.2 1.5 fusion.49
  77.7 2.9 %fusion.50 = bf16[8,512,1,64]{1,3,2,0:T(8,128)(2,1)} fusion(bf16[8,512,1,64]{1,3,2,0:T(8,128)(2,1)} %get-tuple-element.119, s32[]{:T(128)S(6)} %copy.37, f32[512,4096]{1,0:T(8,128)S(1)} %get-tuple-element.110, f32[512]{0:T(512)S(1)} %fusion.49, f32[512]{0:T(512)S(1)} %get-tuple-element.111, bf16[4096,1,64]{0,2,1:T(8,128)(2,1)S(1)} %copy-done.1), kind=kOutput, calls=%fused_computation.10.clone.1 | convolution fusion | flops 276856832 | bytes 8982532 | tf_op jit(solution)/shard_map/while/body/eval_jaxpr/hqk,khd->qhd/dot_general | solution.py:34
  82.0 1.5 fusion.49
  83.5 2.9 %fusion.50 = bf16[8,512,1,64]{1,3,2,0:T(8,128)(2,1)} fusion(bf16[8,512,1,64]{1,3,2,0:T(8,128)(2,1)} %get-tuple-element.119, s32[]{:T(128)S(6)} %copy.37, f32[512,4096]{1,0:T(8,128)S(1)} %get-tuple-element.110, f32[512]{0:T(512)S(1)} %fusion.49, f32[512]{0:T(512)S(1)} %get-tuple-element.111, bf16[4096,1,64]{0,2,1:T(8,128)(2,1)S(1)} %copy-done.1), kind=kOutput, calls=%fused_computation.10.clone.1 | convolution fusion | flops 276856832 | bytes 8982532 | tf_op jit(solution)/shard_map/while/body/eval_jaxpr/hqk,khd->qhd/dot_general | solution.py:34
  87.8 1.5 fusion.49
  89.3 2.9 %fusion.50 = bf16[8,512,1,64]{1,3,2,0:T(8,128)(2,1)} fusion(bf16[8,512,1,64]{1,3,2,0:T(8,128)(2,1)} %get-tuple-element.119, s32[]{:T(128)S(6)} %copy.37, f32[512,4096]{1,0:T(8,128)S(1)} %get-tuple-element.110, f32[512]{0:T(512)S(1)} %fusion.49, f32[512]{0:T(512)S(1)} %get-tuple-element.111, bf16[4096,1,64]{0,2,1:T(8,128)(2,1)S(1)} %copy-done.1), kind=kOutput, calls=%fused_computation.10.clone.1 | convolution fusion | flops 276856832 | bytes 8982532 | tf_op jit(solution)/shard_map/while/body/eval_jaxpr/hqk,khd->qhd/dot_general | solution.py:34
  93.6 1.5 fusion.49
  95.1 2.9 %fusion.50 = bf16[8,512,1,64]{1,3,2,0:T(8,128)(2,1)} fusion(bf16[8,512,1,64]{1,3,2,0:T(8,128)(2,1)} %get-tuple-element.119, s32[]{:T(128)S(6)} %copy.37, f32[512,4096]{1,0:T(8,128)S(1)} %get-tuple-element.110, f32[512]{0:T(512)S(1)} %fusion.49, f32[512]{0:T(512)S(1)} %get-tuple-element.111, bf16[4096,1,64]{0,2,1:T(8,128)(2,1)S(1)} %copy-done.1), kind=kOutput, calls=%fused_computation.10.clone.1 | convolution fusion | flops 276856832 | bytes 8982532 | tf_op jit(solution)/shard_map/while/body/eval_jaxpr/hqk,khd->qhd/dot_general | solution.py:34
  100.9 2.9 %fusion.50 = bf16[8,512,1,64]{1,3,2,0:T(8,128)(2,1)} fusion(bf16[8,512,1,64]{1,3,2,0:T(8,128)(2,1)} %get-tuple-element.119, s32[]{:T(128)S(6)} %copy.37, f32[512,4096]{1,0:T(8,128)S(1)} %get-tuple-element.110, f32[512]{0:T(512)S(1)} %fusion.49, f32[512]{0:T(512)S(1)} %get-tuple-element.111, bf16[4096,1,64]{0,2,1:T(8,128)(2,1)S(1)} %copy-done.1), kind=kOutput, calls=%fused_computation.10.clone.1 | convolution fusion | flops 276856832 | bytes 8982532 | tf_op jit(solution)/shard_map/while/body/eval_jaxpr/hqk,khd->qhd/dot_general | solution.py:34
  106.6 2.9 %fusion.50 = bf16[8,512,1,64]{1,3,2,0:T(8,128)(2,1)} fusion(bf16[8,512,1,64]{1,3,2,0:T(8,128)(2,1)} %get-tuple-element.119, s32[]{:T(128)S(6)} %copy.37, f32[512,4096]{1,0:T(8,128)S(1)} %get-tuple-element.110, f32[512]{0:T(512)S(1)} %fusion.49, f32[512]{0:T(512)S(1)} %get-tuple-element.111, bf16[4096,1,64]{0,2,1:T(8,128)(2,1)S(1)} %copy-done.1), kind=kOutput, calls=%fused_computation.10.clone.1 | convolution fusion | flops 276856832 | bytes 8982532 | tf_op jit(solution)/shard_map/while/body/eval_jaxpr/hqk,khd->qhd/dot_general | solution.py:34
  112.4 2.9 %fusion.50 = bf16[8,512,1,64]{1,3,2,0:T(8,128)(2,1)} fusion(bf16[8,512,1,64]{1,3,2,0:T(8,128)(2,1)} %get-tuple-element.119, s32[]{:T(128)S(6)} %copy.37, f32[512,4096]{1,0:T(8,128)S(1)} %get-tuple-element.110, f32[512]{0:T(512)S(1)} %fusion.49, f32[512]{0:T(512)S(1)} %get-tuple-element.111, bf16[4096,1,64]{0,2,1:T(8,128)(2,1)S(1)} %copy-done.1), kind=kOutput, calls=%fused_computation.10.clone.1 | convolution fusion | flops 276856832 | bytes 8982532 | tf_op jit(solution)/shard_map/while/body/eval_jaxpr/hqk,khd->qhd/dot_general | solution.py:34
  118.2 2.9 %fusion.50 = bf16[8,512,1,64]{1,3,2,0:T(8,128)(2,1)} fusion(bf16[8,512,1,64]{1,3,2,0:T(8,128)(2,1)} %get-tuple-element.119, s32[]{:T(128)S(6)} %copy.37, f32[512,4096]{1,0:T(8,128)S(1)} %get-tuple-element.110, f32[512]{0:T(512)S(1)} %fusion.49, f32[512]{0:T(512)S(1)} %get-tuple-element.111, bf16[4096,1,64]{0,2,1:T(8,128)(2,1)S(1)} %copy-done.1), kind=kOutput, calls=%fused_computation.10.clone.1 | convolution fusion | flops 276856832 | bytes 8982532 | tf_op jit(solution)/shard_map/while/body/eval_jaxpr/hqk,khd->qhd/dot_general | solution.py:34
  123.6 5.1 %all-to-all-start = ((bf16[16,256,64]{1,2,0:T(8,128)(2,1)}), bf16[16,256,64]{1,2,0:T(8,128)(2,1)S(1)}, u32[]{:S(2)}, u32[]{:S(2)}) async-start(bf16[16,256,64]{1,2,0:T(8,128)(2,1)} %copy.26), calls=%async_computation | async-start | bytes 1048576 | tf_op jit(solution)/shard_map/all_to_all | solution.py:64
  129.0 9.4 %all-to-all-done = bf16[16,256,64]{1,2,0:T(8,128)(2,1)S(1)} async-done(((bf16[16,256,64]{1,2,0:T(8,128)(2,1)}), bf16[16,256,64]{1,2,0:T(8,128)(2,1)S(1)}, u32[]{:S(2)}, u32[]{:S(2)}) %all-to-all-start) | async-done | bytes 524320 | tf_op jit(solution)/shard_map/all_to_all | solution.py:64
  138.3 2.4 %multiply_reduce_fusion.1 = (f32[256]{0:T(256)S(1)}, f32[256,1024]{1,0:T(8,128)S(1)}) fusion(bf16[256,1024]{0,1:T(8,128)(2,1)S(1)} %bitcast.85, bf16[1024,1024]{1,0:T(8,128)(2,1)} %all-gather.5.cloned.1.call-done, bf16[256,1024]{1,0:T(8,128)(2,1)S(1)} %gather_fusion, pred[256]{0:T(512)(128)(4,1)S(1)} %compare_and_fusion.1), kind=kOutput, calls=%fused_computation.37 | convolution fusion | flops 538181376 | bytes 4195584 | tf_op jit(solution)/shard_map/dot_general | solution.py:74
  142.5 27.3 %all_to_all.15 = bf16[128,4,1024]{2,1,0:T(4,128)(2,1)S(1)} all-to-all(bf16[128,4,1024]{2,1,0:T(4,128)(2,1)} %reshape.117), channel_id=1, replica_groups=mesh['dp'=8,'ctx'=16] {'dp','ctx'}, dimensions={0} | all-to-all | bytes 2097152 | tf_op jit(solution)/shard_map/all_to_all | solution.py:95
  169.8 11.8 %fusion.18 = bf16[128,4,1024]{2,0,1:T(8,128)(2,1)} fusion(bf16[1,2816,1024]{2,1,0:T(8,128)(2,1)} %param.25, bf16[1,1024,2816]{2,1,0:T(8,128)(2,1)} %param.24, bf16[128,4,1024]{2,1,0:T(4,128)(2,1)S(1)} %all_to_all.15), kind=kOutput, calls=%fused_computation.27 | convolution fusion | flops 5908987904 | bytes 13631488 | tf_op jit(solution)/shard_map/sgif,gfd->sgid/dot_general | solution.py:100
  181.6 3.1 %copy.28 = bf16[128,4,1024]{2,1,0:T(4,128)(2,1)} copy(bf16[128,4,1024]{2,0,1:T(8,128)(2,1)} %fusion.18) | data formatting | bytes 2097152 | tf_op jit(solution)/shard_map/convert_element_type | solution.py:101
  184.7 5.1 %all-to-all-start.2 = ((bf16[128,4,1024]{2,1,0:T(4,128)(2,1)}), bf16[128,4,1024]{2,1,0:T(4,128)(2,1)}, u32[]{:S(2)}, u32[]{:S(2)}) async-start(bf16[128,4,1024]{2,1,0:T(4,128)(2,1)} %copy.28), calls=%async_computation.2 | async-start | bytes 2097152 | tf_op jit(solution)/shard_map/all_to_all | solution.py:102
  189.8 19.1 %all-to-all-done.2 = bf16[128,4,1024]{2,1,0:T(4,128)(2,1)} async-done(((bf16[128,4,1024]{2,1,0:T(4,128)(2,1)}), bf16[128,4,1024]{2,1,0:T(4,128)(2,1)}, u32[]{:S(2)}, u32[]{:S(2)}) %all-to-all-start.2) | async-done | bytes 1048608 | tf_op jit(solution)/shard_map/all_to_all | solution.py:102
  210.2 4.1 %scatter_custom_fusion = bf16[512,1024]{1,0:T(8,128)(2,1)S(1)} fusion(bf16[512,1024]{1,0:T(8,128)(2,1)S(1)} %bitcast.83, s32[256]{0:T(256)S(1)} %bitcast.94, f32[256,1024]{1,0:T(8,128)S(1)} %get-tuple-element.76, pred[256]{0:T(512)(128)(4,1)S(1)} %compare_and_fusion, bf16[]{:T(256)} %constant.10.clone.2, bf16[512,1024]{1,0:T(8,128)(2,1)S(1)} %reshape.120, ...), kind=kCustom, calls=%fused_computation.38 | custom fusion | flops 1048576 | bytes 3150338 | tf_op jit(solution)/shard_map/scatter | solution.py:106
  (73 shorter events, 29.9 us)
Async XLA Ops:
  6.5 3.5 %copy-start.5 = (f32[1024]{0:T(1024)S(1)}, f32[1024]{0:T(1024)}, u32[]{:S(2)}) copy-start(f32[1024]{0:T(1024)} %param.17) | copy-start | bytes 12292
  6.5 4.7 %copy-start.4 = (bf16[1024,64]{0,1:T(8,128)(2,1)S(1)}, bf16[1024,64]{0,1:T(8,128)(2,1)}, u32[]{:S(2)}) copy-start(bf16[1024,64]{0,1:T(8,128)(2,1)} %param.19) | copy-start | bytes 393220
  6.5 4.7 %copy-start.3 = (bf16[1024,64]{0,1:T(8,128)(2,1)S(1)}, bf16[1024,64]{0,1:T(8,128)(2,1)}, u32[]{:S(2)}) copy-start(bf16[1024,64]{0,1:T(8,128)(2,1)} %param.20) | copy-start | bytes 393220
  6.5 4.8 %copy-start.2 = (bf16[1024,64]{0,1:T(8,128)(2,1)S(1)}, bf16[1024,64]{0,1:T(8,128)(2,1)}, u32[]{:S(2)}) copy-start(bf16[1024,64]{0,1:T(8,128)(2,1)} %param.21) | copy-start | bytes 393220
  6.5 60.5 %all-gather.3.cloned.1.call-start = ((), (), s32[]{:S(2)}) async-start(), calls=%async_computation.3 | async-start | bytes 8912896 | tf_op jit(solution)/shard_map/all_gather | solution.py:54
  11.2 127.1 %all-gather.5.cloned.1.call-start = ((), (), s32[]{:S(2)}) async-start(), calls=%async_computation.4 | async-start | bytes 2228224 | tf_op jit(solution)/shard_map/all_gather | solution.py:72
  74.8 53.9 %copy-start.7 = (s32[1,256,1]{1,2,0:T(1,128)S(1)}, s32[1,256,1]{1,2,0:T(1,128)}, u32[]{:S(2)}) copy-start(s32[1,256,1]{1,2,0:T(1,128)} %param.23) | copy-start | bytes 3076
  76.2 1.5 copy-start.1
  82.0 1.5 copy-start.1
  87.8 1.5 copy-start.1
  93.6 1.5 copy-start.1
  99.3 1.5 copy-start.1
  105.1 1.5 copy-start.1
  110.9 1.5 copy-start.1
  116.7 1.5 copy-start.1
  121.1 19.7 %copy-start.6 = (f32[1024]{0:T(1024)S(1)}, f32[1024]{0:T(1024)}, u32[]{:S(2)}) copy-start(f32[1024]{0:T(1024)} %param.18) | copy-start | bytes 12292
  123.6 14.8 %all-to-all-start = ((bf16[16,256,64]{1,2,0:T(8,128)(2,1)}), bf16[16,256,64]{1,2,0:T(8,128)(2,1)S(1)}, u32[]{:S(2)}, u32[]{:S(2)}) async-start(bf16[16,256,64]{1,2,0:T(8,128)(2,1)} %copy.26), calls=%async_computation | async-start | bytes 1048576 | tf_op jit(solution)/shard_map/all_to_all | solution.py:64
  184.7 24.2 %all-to-all-start.2 = ((bf16[128,4,1024]{2,1,0:T(4,128)(2,1)}), bf16[128,4,1024]{2,1,0:T(4,128)(2,1)}, u32[]{:S(2)}, u32[]{:S(2)}) async-start(bf16[128,4,1024]{2,1,0:T(4,128)(2,1)} %copy.28), calls=%async_computation.2 | async-start | bytes 2097152 | tf_op jit(solution)/shard_map/all_to_all | solution.py:102
  214.4 1.0 copy-start
Sparse Core Ops, SparseCore 0:
  11.3 55.7 all-gather.2
  68.8 34.8 all-gather.4

commit v2 on v0

v2 whole, which is shorter than its diff:
```python
import functools
import math

import jax
import jax.numpy as jnp
from jax import lax
from jax.experimental import pallas as pl
from jax.experimental.pallas import tpu as pltpu
from jax.sharding import PartitionSpec as P

HS = 64
LANES = 128
HALF = 128
SLOTS = 4
eps_norm = 1e-06
score_gain = 2.5
SCALE2 = score_gain / math.sqrt(HS) * math.log2(math.e)

A0, A1, A2, A3 = (0, 0), (1, 0), (2, 0), (3, 0)
B0, B1, B2, B3 = (0, 1), (1, 1), (2, 1), (3, 1)
UNITS = (
    [(c, h) for c in (A0, A3, A1, B0) for h in (0, 1)]
    + [(A2, 0), (B3, 0), (A2, 1), (B1, 0), (B1, 1), (B3, 1)]
    + [(B2, 0), (B2, 1)]
)


def params(limit=48):
    return pltpu.CompilerParams(vmem_limit_bytes=limit << 20)


def cost(flops, moved, exps=0):
    return pl.CostEstimate(flops=int(flops), bytes_accessed=int(moved), transcendentals=int(exps))


def dot32(a, b):
    return jnp.dot(a, b, preferred_element_type=jnp.float32)


def dot_first(a, b):
    return lax.dot_general(a, b, (((0,), (0,)), ((), ())), preferred_element_type=jnp.float32)


def iota(shape, axis):
    return lax.broadcasted_iota(jnp.int32, shape, axis)


def one_hot(flag):
    return jnp.where(flag, 1.0, 0.0).astype(jnp.bfloat16)


def rms_scale(values, gain):
    power = jnp.mean(values * values, axis=-1, keepdims=True)
    return values * lax.rsqrt(power + eps_norm) * gain


def gather_kernel(local_ref, doc_ref, gain_ref, rows_ref, normed_ref):
    local = local_ref[...]
    spread = one_hot(iota((doc_ref.shape[0], local.shape[1]), 0) == local)
    rows = dot_first(spread, doc_ref[...])
    rows_ref[...] = rows.astype(jnp.bfloat16)
    normed_ref[...] = rms_scale(rows, gain_ref[...]).astype(jnp.bfloat16)


def gather_rows(local, document, gain):
    keep, (_, width) = local.shape[1], document.shape
    shape = jax.ShapeDtypeStruct((keep, width), jnp.bfloat16)
    return pl.pallas_call(
        gather_kernel,
        out_shape=(shape, shape),
        compiler_params=params(),
        cost_estimate=cost(2 * keep * document.size, 2 * (document.size + 2 * keep * width)),
        name="gather_rows",
    )(local, document, gain)


def project_kernel(*refs):
    *blocks, own_w, other_w, own_ref, other_ref = refs
    at = 0
    for block in blocks:
        here = pl.ds(at, block.shape[0])
        value = block[...]
        own_ref[here, :] = dot32(value, own_w[...]).astype(jnp.bfloat16)
        other_ref[here, :] = dot32(value, other_w[...]).astype(jnp.bfloat16)
        at += block.shape[0]


def project(blocks, own_w, other_w):
    count = sum(block.shape[0] for block in blocks)
    shape = jax.ShapeDtypeStruct((count, own_w.shape[1]), jnp.bfloat16)
    depth = own_w.shape[0]
    return pl.pallas_call(
        project_kernel,
        out_shape=(shape, shape),
        compiler_params=params(),
        cost_estimate=cost(4 * count * own_w.size, 2 * (count * depth + 2 * own_w.size)),
        name="project_rows",
    )(*blocks, own_w, other_w)


def attend_kernel(where_ref, *refs, pieces, chunk, span):
    packed, (out_ref, keys, values, queries, mixed) = refs[:pieces], refs[pieces:]
    step = pl.program_id(0)
    total = keys.shape[1]

    @pl.when(step == 0)
    def _():
        at = 0
        for piece in packed:
            count = piece.shape[0]
            here = pl.ds(at, count)
            pair = piece[:, :LANES].astype(jnp.float32)
            lane = iota((count, LANES), 1)
            twice = jnp.where(lane < HS, pair, pltpu.roll(pair, HS, 1)) * SCALE2
            high = twice.astype(jnp.bfloat16).astype(jnp.float32)
            queries[here, :] = jnp.where(lane < HS, high, twice - high).astype(jnp.bfloat16)
            turned = pair.T[HS:, :].astype(jnp.bfloat16)
            keys[:HS, here] = turned
            keys[HS:, here] = turned
            ones = jnp.where(lane == HS, 1.0, 0.0)
            values[here, :] = (piece[:, LANES:].astype(jnp.float32) + ones).astype(jnp.bfloat16)
            at += count

    query = queries[pl.ds(pl.multiple_of(step * span, span), span), :]
    top = jnp.full((span, 1), -1e30, jnp.float32)
    held = jnp.zeros((span, LANES), jnp.float32)
    for j in range(total // chunk):
        here = pl.ds(j * chunk, chunk)
        scores = dot32(query, keys[:, here])
        newer = jnp.maximum(top, jnp.max(scores, axis=1, keepdims=True))
        weights = jnp.exp2(scores - newer).astype(jnp.bfloat16)
        held = held * jnp.exp2(top - newer) + dot32(weights, values[here, :])
        top = newer
    mixed[...] = held.T
    result = (mixed[:HS, :] / mixed[HS : HS + 1, :]).astype(jnp.bfloat16)
    units = span // HALF
    for first in range(total // span):

        @pl.when(step == first)
        def _():
            for k in range(units):
                unit = first * units + k
                half = UNITS[unit % len(UNITS)][1]
                out_ref[where_ref[unit], :, half * HALF : (half + 1) * HALF] = result[
                    :, k * HALF : (k + 1) * HALF
                ]


def attend(where, packed, blocks):
    total = sum(piece.shape[0] for piece in packed)
    span, chunk = 1024, 512
    return pl.pallas_call(
        functools.partial(attend_kernel, pieces=len(packed), chunk=chunk, span=span),
        grid_spec=pltpu.PrefetchScalarGridSpec(
            num_scalar_prefetch=1,
            grid=(total // span,),
            in_specs=[pl.BlockSpec(piece.shape, lambda i, w: (0, 0)) for piece in packed],
            out_specs=pl.BlockSpec((blocks, HS, 2 * HALF), lambda i, w: (0, 0, 0)),
            scratch_shapes=[
                pltpu.VMEM((LANES, total), jnp.bfloat16),
                pltpu.VMEM((total, LANES), jnp.bfloat16),
                pltpu.VMEM((total, LANES), jnp.bfloat16),
                pltpu.VMEM((LANES, span), jnp.float32),
            ],
        ),
        out_shape=jax.ShapeDtypeStruct((blocks, HS, 2 * HALF), jnp.bfloat16),
        compiler_params=params(),
        cost_estimate=cost(4 * total * total * LANES, 6 * total * LANES, total * total),
        name="attend_heads",
    )(where, *packed)


def dispatch_kernel(mixed_ref, w_ref, rows_ref, gain_ref, label_ref, first_ref, send_ref, place_ref):
    first = rows_ref[...].astype(jnp.float32) + dot_first(mixed_ref[...], w_ref[...])
    first_ref[...] = first
    entry = rms_scale(first, gain_ref[...]).astype(jnp.bfloat16)
    keep, width = first.shape
    label = label_ref[...].astype(jnp.float32)
    across = jnp.broadcast_to(label, (keep, keep))
    same = (across == across.T) & (iota((keep, keep), 0) < iota((keep, keep), 1))
    slot = jnp.sum(jnp.where(same, 1.0, 0.0), axis=0, keepdims=True)
    place = (label * (2 * SLOTS) + slot).astype(jnp.int32)
    place_ref[...] = place
    places = send_ref.shape[0]
    half = width // 2
    row = iota((places, keep), 0)
    send = dot32(one_hot(row == place), entry[:, :half])
    send = send + dot32(one_hot(row == place + SLOTS), entry[:, half:])
    send_ref[...] = send.astype(jnp.bfloat16)


def dispatch(mixed, w_all, rows, gain, label, experts):
    keep, width = rows.shape
    places = experts * 2 * SLOTS
    return pl.pallas_call(
        dispatch_kernel,
        out_shape=(
            jax.ShapeDtypeStruct((keep, width), jnp.float32),
            jax.ShapeDtypeStruct((places, width // 2), jnp.bfloat16),
            jax.ShapeDtypeStruct((1, keep), jnp.int32),
        ),
        compiler_params=params(),
        cost_estimate=cost(4 * keep * w_all.size, 2 * w_all.size + 10 * keep * width),
        name="dispatch_rows",
    )(mixed, w_all, rows, gain, label)


def expert_kernel(slots_ref, w_in_ref, w_back_ref, out_ref, entry, total):
    step = pl.program_id(0)
    count, half = slots_ref.shape
    pairs = count // 16

    @pl.when(step == 0)
    def _():
        got = slots_ref[...].astype(jnp.float32).reshape(pairs, 2, 8, half)
        even, odd = got[:, 0], got[:, 1]
        low_side = iota((pairs, 8, half), 1) < SLOTS
        low = jnp.where(low_side, even, pltpu.roll(odd, SLOTS, 1))
        high = jnp.where(low_side, pltpu.roll(even, SLOTS, 1), odd)
        entry[:, :half] = low.reshape(count // 2, half).astype(jnp.bfloat16)
        entry[:, half:] = high.reshape(count // 2, half).astype(jnp.bfloat16)

    hidden = jnp.maximum(dot32(entry[...], w_in_ref[...]), 0.0).astype(jnp.bfloat16)
    part = dot32(hidden, w_back_ref[...])

    @pl.when(step == 0)
    def _():
        total[...] = part

    @pl.when(step > 0)
    def _():
        total[...] += part

    @pl.when(step == pl.num_programs(0) - 1)
    def _():
        low = total[:, :half].reshape(pairs, 8, half)
        high = total[:, half:].reshape(pairs, 8, half)
        low_side = iota((pairs, 8, half), 1) < SLOTS
        even = jnp.where(low_side, low, pltpu.roll(high, SLOTS, 1))
        odd = jnp.where(low_side, pltpu.roll(low, SLOTS, 1), high)
        both = jnp.concatenate([even[:, None], odd[:, None]], axis=1)
        out_ref[...] = both.reshape(count, half).astype(jnp.bfloat16)


def run_expert(slots, w_in, w_back):
    count, half = slots.shape
    width, inner = w_in.shape
    tile = 256
    return pl.pallas_call(
        expert_kernel,
        grid=(inner // tile,),
        in_specs=[
            pl.BlockSpec((count, half), lambda i: (0, 0)),
            pl.BlockSpec((width, tile), lambda i: (0, i)),
            pl.BlockSpec((tile, width), lambda i: (i, 0)),
        ],
        out_specs=pl.BlockSpec((count, half), lambda i: (0, 0)),
        out_shape=jax.ShapeDtypeStruct((count, half), jnp.bfloat16),
        scratch_shapes=[
            pltpu.VMEM((count // 2, width), jnp.bfloat16),
            pltpu.VMEM((count // 2, width), jnp.float32),
        ],
        compiler_params=params(),
        cost_estimate=cost(2 * count * w_in.size, 4 * w_in.size + 4 * slots.size),
        name="run_expert",
    )(slots, w_in, w_back)


def combine_kernel(back_ref, place_ref, first_ref, local_ref, doc_ref, out_ref):
    back = back_ref[...]
    places, half = back.shape
    place = place_ref[...]
    keep = place.shape[1]
    row = iota((places, keep), 0)
    low = dot_first(one_hot(row == place), back)
    high = dot_first(one_hot(row == place + SLOTS), back)
    taken = jnp.concatenate([low, high], axis=1)
    second = (first_ref[...] + taken).astype(jnp.bfloat16)
    spread = iota((doc_ref.shape[0], keep), 0) == local_ref[...]
    fresh = dot32(one_hot(spread), second).astype(jnp.bfloat16)
    hit = jnp.max(jnp.where(spread, 1.0, 0.0), axis=1, keepdims=True) > 0.5
    out_ref[...] = jnp.where(hit, fresh, doc_ref[...])


def combine(back, place, first, local, document):
    keep, width = first.shape
    return pl.pallas_call(
        combine_kernel,
        out_shape=jax.ShapeDtypeStruct(document.shape, document.dtype),
        compiler_params=params(),
        cost_estimate=cost(2 * keep * (2 * back.size + document.size), 6 * document.size),
        name="combine_rows",
    )(back, place, first, local, document)


def body(
    tokens, kept, gain_attn, gain_ffn, w_query, w_key, w_value, w_out, expert_ids, w_in, w_back
):
    document = tokens[0]
    shard_len, width = document.shape
    ctx_count = lax.axis_size("ctx")
    experts = lax.axis_size("dp") * ctx_count
    me = lax.axis_index("ctx")
    keep = kept.shape[1]
    local = kept - me * shard_len

    def along(value, step):
        pairs = [(i, (i // 4 + step) % 4 * 4 + i % 4) for i in range(ctx_count)]
        return lax.ppermute(value, "ctx", pairs)

    def flip(value, bit):
        return lax.ppermute(value, "ctx", [(i, i ^ bit) for i in range(ctx_count)])

    own_w = jnp.concatenate([w_query, w_key, w_value, jnp.zeros_like(w_value)], axis=1)
    other_w = flip(own_w, 1)
    w_all = lax.all_gather(w_out, "ctx", axis=0, tiled=True)
    rows, normed = gather_rows(local, document, gain_attn[None])

    a3, a1, b0 = along(normed, 1), along(normed, 3), flip(normed, 2)
    r1 = along(jnp.concatenate([a3[:HALF], b0[:HALF]]), 1)
    r2 = along(jnp.concatenate([a1[HALF:], b0[:HALF]]), 3)
    r3 = flip(jnp.concatenate([a1[HALF:], a3[HALF:]]), 2)
    b2 = flip(jnp.concatenate([r1[:HALF], r2[:HALF]]), 2)
    stages = [[normed], [a3, a1, b0], [r1, r2, r3], [b2]]
    own, other = [], []
    for blocks in stages:
        mine, theirs = project(blocks, own_w, other_w)
        own.append(mine)
        other.append(flip(theirs, 1))

    def places(core):
        found = []
        for (dx, dy), _ in UNITS:
            x, y = (me // 4 + dx) % 4, (me // 2 % 2) ^ dy
            found.append(x * 4 + y * 2 + core)
        return found

    core = me % 2
    where = jnp.stack(places(core) + places(1 - core)).astype(jnp.int32)
    mixed = attend(where, own + other, ctx_count)
    parts = lax.all_to_all(mixed, "ctx", split_axis=0, concat_axis=0, tiled=True)

    label = expert_ids[:, :, 0]
    first, send, place = dispatch(
        parts.reshape(-1, keep), w_all, rows, gain_ffn[None], label, experts
    )
    names = ("dp", "ctx")
    send = send.reshape(experts, 2 * SLOTS, width // 2)
    got = lax.all_to_all(send, names, split_axis=0, concat_axis=0, tiled=True)
    answer = run_expert(got.reshape(-1, width // 2), w_in[0], w_back[0])
    answer = answer.reshape(experts, 2 * SLOTS, width // 2)
    back = lax.all_to_all(answer, names, split_axis=0, concat_axis=0, tiled=True)
    return combine(back.reshape(-1, width // 2), place, first, local, document)[None]


def solution(mesh):
    return jax.shard_map(
        body,
        mesh=mesh,
        in_specs=(
            P("dp", "ctx", None),
            P("dp", "ctx"),
            P(),
            P(),
            P(None, "ctx"),
            P(None, "ctx"),
            P(None, "ctx"),
            P("ctx", None),
            P("dp", "ctx", None),
            P(("dp", "ctx"), None, None),
            P(("dp", "ctx"), None, None),
        ),
        out_specs=P("dp", "ctx", None),
        check_vma=False,
    )
```

time: 305 us -> 189 us (0.62)
  waiting for transfers between devices: 172 us -> 31.9 us
  matrix products: 55 us -> 0 us
  Pallas kernels: 0 us -> 45.7 us
  blocking collectives: 28.1 us -> 65.8 us
  other arithmetic: 20.7 us -> 3.3 us
  starting transfers between devices: 5.16 us -> 17.2 us
    reduce_scatter x1 -> x0, waiting for transfers between devices: 97.2 us -> none  [body(): lax.psum_scatter(jnp.dot(flat_mixed, w_out, preferred_element_type=jnp.fl...]
    all_gather x1, waiting for transfers between devices: 55.7 us -> 0.01 us  [body(): w_all = lax.all_gather(w_out, 'ctx', axis=0, tiled=True)]
    dot_general x20 -> x0, matrix products: 48.8 us -> none  [the longest x8 18.1 us: one_block(): jnp.einsum('hqk,khd->qhd', probs, values, preferred_element_type=jnp.floa...]
    pallas_call x0 -> x9, Pallas kernels: none -> 45.7 us  [the longest x1 21.2 us: attend(): pl.pallas_call(functools.partial(attend_kernel, pieces=len(packed), chunk...]
    all_to_all x1 -> x3, blocking collectives: 28.1 us -> 65.8 us  [the longest x1 28.8 us: body(): got = lax.all_to_all(send, names, split_axis=0, concat_axis=0, tiled=True)]
    ppermute x0 -> x12, waiting for transfers between devices: none -> 31.2 us  [the longest x8 15.8 us: flip(): return lax.ppermute(value, 'ctx', [(i, i ^ bit) for i in range(ctx_count)])]
    all_to_all x1 -> x0, waiting for transfers between devices: 19.1 us -> none  [body(): lax.all_to_all(answered, ('dp', 'ctx'), split_axis=0, concat_axis=0, tile...]
    ppermute x0 -> x12, starting transfers between devices: none -> 17.2 us  [the longest x8 11.7 us: flip(): return lax.ppermute(value, 'ctx', [(i, i ^ bit) for i in range(ctx_count)])]
  transfers between devices with their start and end apart: 3 -> 13, of which waited for: 3 -> 6; matrix products, arithmetic and copies ran while one was open for 0% -> 4% of each run, Pallas kernels for 0% -> 13%
where the time goes in v2:
time: 189 us
  blocking collectives  65.8 us (35%)
  Pallas kernels  45.7 us (24%)
  waiting for transfers between devices  31.9 us (17%)
  starting transfers between devices  17.2 us (9%)
  between operations  13.6 us (7%)
  local copies, waits for them, and re-layouts  11 us (6%)
  other arithmetic  3.3 us (2%)
    all_to_all x1, blocking collectives, body(): got = lax.all_to_all(send, names, split_axis=0, concat_axis=0, tiled=True)  28.8 us
    all_to_all x1, blocking collectives, body(): lax.all_to_all(answer, names, split_axis=0, concat_axis=0, tiled=True)  23.1 us
    pallas_call x1, Pallas kernels, attend(): pl.pallas_call(functools.partial(attend_kernel, pieces=len(packed), chunk...  21.2 us
    pallas_call x1, Pallas kernels, run_expert(): pl.pallas_call(expert_kernel, grid=(inner // tile,), in_specs=[pl.BlockSp...  17.6 us
    ppermute x8, waiting for transfers between devices, flip(): return lax.ppermute(value, 'ctx', [(i, i ^ bit) for i in range(ctx_count)])  15.8 us
    ppermute x4, waiting for transfers between devices, along(): return lax.ppermute(value, 'ctx', pairs)  15.4 us
    all_to_all x1, blocking collectives, body(): lax.all_to_all(mixed, 'ctx', split_axis=0, concat_axis=0, tiled=True)  14 us
    ppermute x8, starting transfers between devices, flip(): return lax.ppermute(value, 'ctx', [(i, i ^ bit) for i in range(ctx_count)])  11.7 us
  transfers between devices with their start and end apart: 13, of which 6 were waited for; matrix products, arithmetic and copies ran while one was open for 4% of the time, Pallas kernels for 13%

profile of v2, /device:TPU:1, one launch (start us, length us, event | category | flops | bytes accessed | tf_op | source)
XLA Modules:
  0.0 188.6 jit_solution(17710600323139639982)
XLA Ops:
  7.9 1.2 copy-done
  11.3 3.3 %collective-permute-start.2 = (bf16[256,1024]{1,0:T(8,128)(2,1)S(1)}, bf16[256,1024]{1,0:T(8,128)(2,1)S(1)}, u32[]{:S(2)}, u32[]{:S(2)}) collective-permute-start(bf16[256,1024]{1,0:T(8,128)(2,1)S(1)} %get-tuple-element.18.refs_0_), channel_id=1, source_target_pairs={{0,12},{1,13},{2,14},{3,15},{4,0},{5,1},{6,2},{7,3},{8,4},{9,5},{1... | collective-permute-start | bytes 1572872 | tf_op jit(solution)/shard_map/ppermute | solution.py:309
  14.6 1.3 collective-permute-start.3
  15.9 9.4 %collective-permute-done.2.refs_1_ = bf16[256,1024]{1,0:T(8,128)(2,1)S(1)} collective-permute-done((bf16[256,1024]{1,0:T(8,128)(2,1)S(1)}, bf16[256,1024]{1,0:T(8,128)(2,1)S(1)}, u32[]{:S(2)}, u32[]{:S(2)}) %collective-permute-start.2) | collective-permute-done | bytes 524320 | tf_op jit(solution)/shard_map/ppermute | solution.py:309
  25.3 4.2 %collective-permute-done.3.refs_2_ = bf16[256,1024]{1,0:T(8,128)(2,1)S(1)} collective-permute-done((bf16[256,1024]{1,0:T(8,128)(2,1)S(1)}, bf16[256,1024]{1,0:T(8,128)(2,1)S(1)}, u32[]{:S(2)}, u32[]{:S(2)}) %collective-permute-start.3) | collective-permute-done | bytes 524320 | tf_op jit(solution)/shard_map/ppermute | solution.py:312
  29.5 1.3 pad_maximum_fusion.2
  30.8 2.2 %collective-permute-start.5 = (bf16[256,1024]{1,0:T(8,128)(2,1)}, bf16[256,1024]{1,0:T(8,128)(2,1)S(1)}, u32[]{:S(2)}, u32[]{:S(2)}) collective-permute-start(bf16[256,1024]{1,0:T(8,128)(2,1)} %get-tuple-element.34), channel_id=1, source_target_pairs={{0,12},{1,13},{2,14},{3,15},{4,0},{5,1},{6,2},{7,3},{8,4},{9,5},{1... | collective-permute-start | bytes 1572872 | tf_op jit(solution)/shard_map/ppermute | solution.py:309
  33.2 1.7 copy.13
  34.9 1.8 copy.12
  36.8 1.3 maximum_maximum_fusion.refs_1_.refs_3_
  38.1 3.7 %collective-permute-start = (bf16[1024,256]{1,0:T(8,128)(2,1)S(1)}, bf16[1024,256]{1,0:T(8,128)(2,1)S(1)}, u32[]{:S(2)}, u32[]{:S(2)}) collective-permute-start(bf16[1024,256]{1,0:T(8,128)(2,1)S(1)} %maximum_maximum_fusion.refs_1_.refs_3_), channel_id=1, source_target_pairs={{0,1},{1,0},{2,3},{3,2},{4,5},{5,4},{6,7},{7,6},{8,9},{9,8},{10,11... | collective-permute-start | bytes 1572872 | tf_op jit(solution)/shard_map/ppermute | solution.py:312
  41.8 1.0 collective-permute-start.6
  42.9 6.1 %collective-permute-done.5.refs_1_ = bf16[256,1024]{1,0:T(8,128)(2,1)S(1)} collective-permute-done((bf16[256,1024]{1,0:T(8,128)(2,1)}, bf16[256,1024]{1,0:T(8,128)(2,1)S(1)}, u32[]{:S(2)}, u32[]{:S(2)}) %collective-permute-start.5) | collective-permute-done | bytes 524320 | tf_op jit(solution)/shard_map/ppermute | solution.py:309
  50.9 2.8 %collective-permute-start.9 = (bf16[768,256]{1,0:T(8,128)(2,1)S(1)}, bf16[768,256]{1,0:T(8,128)(2,1)S(1)}, u32[]{:S(2)}, u32[]{:S(2)}) collective-permute-start(bf16[768,256]{1,0:T(8,128)(2,1)S(1)} %get-tuple-element.24), channel_id=1, source_target_pairs={{0,1},{1,0},{2,3},{3,2},{4,5},{5,4},{6,7},{7,6},{8,9},{9,8},{10,11... | collective-permute-start | bytes 1179656 | tf_op jit(solution)/shard_map/ppermute | solution.py:312
  53.6 2.8 %collective-permute-done.6.refs_2_ = bf16[256,1024]{1,0:T(8,128)(2,1)S(1)} collective-permute-done((bf16[256,1024]{1,0:T(8,128)(2,1)}, bf16[256,1024]{1,0:T(8,128)(2,1)S(1)}, u32[]{:S(2)}, u32[]{:S(2)}) %collective-permute-start.6) | collective-permute-done | bytes 524320 | tf_op jit(solution)/shard_map/ppermute | solution.py:312
  59.7 8.0 %collective-permute-done.7.refs_0_ = bf16[256,1024]{1,0:T(8,128)(2,1)S(1)} collective-permute-done((bf16[256,1024]{1,0:T(8,128)(2,1)S(1)}, bf16[256,1024]{1,0:T(8,128)(2,1)S(1)}, u32[]{:S(2)}, u32[]{:S(2)}) %collective-permute-start.7) | collective-permute-done | bytes 524320 | tf_op jit(solution)/shard_map/ppermute | solution.py:312
  72.0 21.2 %attend_heads.1 = bf16[16,64,256]{2,1,0:T(8,128)(2,1)S(1)} custom-call(s32[32]{0:T(128)S(1)} %stack.83.where_ref, bf16[256,256]{1,0:T(8,128)(2,1)S(1)} %get-tuple-element.19.refs_0_, bf16[768,256]{1,0:T(8,128)(2,1)S(1)} %copy-done.9, bf16[768,256]{1,0:T(8,128)(2,1)S(1)} %copy-done.11, bf16[256,256]{1,0:T(8,128)(2,1)S(1)} %get-tuple-element.22.refs_3_, ...), custom_call_target="tpu_custom_call" | custom-call | flops 8589934592 | bytes 3145728 | tf_op jit(solution)/shard_map/attend_heads/pallas_call | solution.py:152
  93.2 14.0 %all_to_all.15 = bf16[16,64,256]{2,1,0:T(8,128)(2,1)S(1)} all-to-all(bf16[16,64,256]{2,1,0:T(8,128)(2,1)S(1)} %attend_heads.1), channel_id=1, replica_groups=mesh['dp'=8,'ctx'=16] {'ctx'}, dimensions={0} | all-to-all | bytes 1048576 | tf_op jit(solution)/shard_map/all_to_all | solution.py:341
  107.2 1.6 copy-done.3
  108.7 1.6 dispatch_rows.1
  110.3 28.8 %all_to_all.16 = bf16[128,8,512]{2,1,0:T(8,128)(2,1)S(1)} all-to-all(bf16[128,8,512]{2,1,0:T(8,128)(2,1)S(1)} %bitcast.31), channel_id=1, replica_groups=mesh['dp'=8,'ctx'=16] {'dp','ctx'}, dimensions={0} | all-to-all | bytes 2097152 | tf_op jit(solution)/shard_map/all_to_all | solution.py:349
  139.1 17.6 %run_expert.1 = bf16[1024,512]{1,0:T(8,128)(2,1)S(1)} custom-call(bf16[1024,512]{1,0:T(8,128)(2,1)S(1)} %bitcast.32, bf16[1024,2816]{1,0:T(8,128)(2,1)} %bitcast.38, bf16[2816,1024]{1,0:T(8,128)(2,1)} %bitcast.39), custom_call_target="tpu_custom_call" | custom-call | flops 5905580032 | bytes 13631488 | tf_op jit(solution)/shard_map/run_expert/pallas_call | solution.py:249
  156.7 23.1 %all_to_all.17 = bf16[128,8,512]{2,1,0:T(8,128)(2,1)S(1)} all-to-all(bf16[128,8,512]{2,1,0:T(8,128)(2,1)S(1)} %bitcast.33), channel_id=1, replica_groups=mesh['dp'=8,'ctx'=16] {'dp','ctx'}, dimensions={0} | all-to-all | bytes 2097152 | tf_op jit(solution)/shard_map/all_to_all | solution.py:352
  179.8 2.0 %combine_rows.1 = bf16[512,1024]{1,0:T(8,128)(2,1)} custom-call(bf16[1024,512]{1,0:T(8,128)(2,1)S(1)} %bitcast.30, s32[1,256]{1,0:T(1,128)S(1)} %get-tuple-element.29.place_ref, f32[256,1024]{1,0:T(8,128)S(1)} %get-tuple-element.30.first_ref, s32[1,256]{1,0:T(1,128)S(1)} %broadcast_subtract_fusion.local_ref, bf16[512,1024]{1,0:T(8,128)(2,1)S(1)} %bitcast.29), custom_call_target="tpu_custom_call" | custom-call | flops 805306368 | bytes 3145728 | tf_op jit(solution)/shard_map/combine_rows/pallas_call | solution.py:287
  (56 shorter events, 13.3 us)
Async XLA Ops:
  6.5 26.5 %copy-start.12 = (bf16[1024,64]{0,1:T(8,128)(2,1)S(1)}, bf16[1024,64]{0,1:T(8,128)(2,1)}, u32[]{:S(2)}) copy-start(bf16[1024,64]{0,1:T(8,128)(2,1)} %param.17) | copy-start | bytes 393220
  6.5 100.6 %all-gather.2.cloned.1.call-start = ((), (), s32[]{:S(2)}) async-start(), calls=%async_computation.3 | async-start | bytes 2228224 | tf_op jit(solution)/shard_map/all_gather | solution.py:316
  7.9 1.2 copy-start
  10.5 0.8 copy-start.4
  11.3 14.0 %collective-permute-start.2 = (bf16[256,1024]{1,0:T(8,128)(2,1)S(1)}, bf16[256,1024]{1,0:T(8,128)(2,1)S(1)}, u32[]{:S(2)}, u32[]{:S(2)}) collective-permute-start(bf16[256,1024]{1,0:T(8,128)(2,1)S(1)} %get-tuple-element.18.refs_0_), channel_id=1, source_target_pairs={{0,12},{1,13},{2,14},{3,15},{4,0},{5,1},{6,2},{7,3},{8,4},{9,5},{1... | collective-permute-start | bytes 1572872 | tf_op jit(solution)/shard_map/ppermute | solution.py:309
  14.6 14.9 %collective-permute-start.3 = (bf16[256,1024]{1,0:T(8,128)(2,1)S(1)}, bf16[256,1024]{1,0:T(8,128)(2,1)S(1)}, u32[]{:S(2)}, u32[]{:S(2)}) collective-permute-start(bf16[256,1024]{1,0:T(8,128)(2,1)S(1)} %get-tuple-element.18.refs_0_), channel_id=1, source_target_pairs={{0,2},{1,3},{2,0},{3,1},{4,6},{5,7},{6,4},{7,5},{8,10},{9,11},{10,... | collective-permute-start | bytes 1572872 | tf_op jit(solution)/shard_map/ppermute | solution.py:312
  15.9 13.6 %collective-permute-start.1 = (bf16[256,1024]{1,0:T(8,128)(2,1)S(1)}, bf16[256,1024]{1,0:T(8,128)(2,1)S(1)}, u32[]{:S(2)}, u32[]{:S(2)}) collective-permute-start(bf16[256,1024]{1,0:T(8,128)(2,1)S(1)} %get-tuple-element.18.refs_0_), channel_id=1, source_target_pairs={{0,4},{1,5},{2,6},{3,7},{4,8},{5,9},{6,10},{7,11},{8,12},{9,13},{1... | collective-permute-start | bytes 1572872 | tf_op jit(solution)/shard_map/ppermute | solution.py:309
  30.8 18.1 %collective-permute-start.5 = (bf16[256,1024]{1,0:T(8,128)(2,1)}, bf16[256,1024]{1,0:T(8,128)(2,1)S(1)}, u32[]{:S(2)}, u32[]{:S(2)}) collective-permute-start(bf16[256,1024]{1,0:T(8,128)(2,1)} %get-tuple-element.34), channel_id=1, source_target_pairs={{0,12},{1,13},{2,14},{3,15},{4,0},{5,1},{6,2},{7,3},{8,4},{9,5},{1... | collective-permute-start | bytes 1572872 | tf_op jit(solution)/shard_map/ppermute | solution.py:309
  33.0 15.9 %collective-permute-start.4 = (bf16[256,1024]{1,0:T(8,128)(2,1)}, bf16[256,1024]{1,0:T(8,128)(2,1)S(1)}, u32[]{:S(2)}, u32[]{:S(2)}) collective-permute-start(bf16[256,1024]{1,0:T(8,128)(2,1)} %get-tuple-element.35), channel_id=1, source_target_pairs={{0,4},{1,5},{2,6},{3,7},{4,8},{5,9},{6,10},{7,11},{8,12},{9,13},{1... | collective-permute-start | bytes 1572872 | tf_op jit(solution)/shard_map/ppermute | solution.py:309
  38.1 11.8 %collective-permute-start = (bf16[1024,256]{1,0:T(8,128)(2,1)S(1)}, bf16[1024,256]{1,0:T(8,128)(2,1)S(1)}, u32[]{:S(2)}, u32[]{:S(2)}) collective-permute-start(bf16[1024,256]{1,0:T(8,128)(2,1)S(1)} %maximum_maximum_fusion.refs_1_.refs_3_), channel_id=1, source_target_pairs={{0,1},{1,0},{2,3},{3,2},{4,5},{5,4},{6,7},{7,6},{8,9},{9,8},{10,11... | collective-permute-start | bytes 1572872 | tf_op jit(solution)/shard_map/ppermute | solution.py:312
  41.8 14.6 %collective-permute-start.6 = (bf16[256,1024]{1,0:T(8,128)(2,1)}, bf16[256,1024]{1,0:T(8,128)(2,1)S(1)}, u32[]{:S(2)}, u32[]{:S(2)}) collective-permute-start(bf16[256,1024]{1,0:T(8,128)(2,1)} %get-tuple-element.33), channel_id=1, source_target_pairs={{0,2},{1,3},{2,0},{3,1},{4,6},{5,7},{6,4},{7,5},{8,10},{9,11},{10,... | collective-permute-start | bytes 1572872 | tf_op jit(solution)/shard_map/ppermute | solution.py:312
  49.0 18.6 %collective-permute-start.7 = (bf16[256,1024]{1,0:T(8,128)(2,1)S(1)}, bf16[256,1024]{1,0:T(8,128)(2,1)S(1)}, u32[]{:S(2)}, u32[]{:S(2)}) collective-permute-start(bf16[256,1024]{1,0:T(8,128)(2,1)S(1)} %pad_maximum_fusion.3), channel_id=1, source_target_pairs={{0,2},{1,3},{2,0},{3,1},{4,6},{5,7},{6,4},{7,5},{8,10},{9,11},{10,... | collective-permute-start | bytes 1572872 | tf_op jit(solution)/shard_map/ppermute | solution.py:312
  50.8 17.2 %copy-start.8 = (bf16[768,256]{1,0:T(8,128)(2,1)}, bf16[768,256]{1,0:T(8,128)(2,1)S(1)}, u32[]{:S(2)}) copy-start(bf16[768,256]{1,0:T(8,128)(2,1)S(1)} %get-tuple-element.20.refs_1_) | copy-start | bytes 1179652
  50.9 18.3 %collective-permute-start.9 = (bf16[768,256]{1,0:T(8,128)(2,1)S(1)}, bf16[768,256]{1,0:T(8,128)(2,1)S(1)}, u32[]{:S(2)}, u32[]{:S(2)}) collective-permute-start(bf16[768,256]{1,0:T(8,128)(2,1)S(1)} %get-tuple-element.24), channel_id=1, source_target_pairs={{0,1},{1,0},{2,3},{3,2},{4,5},{5,4},{6,7},{7,6},{8,9},{9,8},{10,11... | collective-permute-start | bytes 1179656 | tf_op jit(solution)/shard_map/ppermute | solution.py:312
  58.1 11.0 %collective-permute-start.10 = (bf16[768,256]{1,0:T(8,128)(2,1)S(1)}, bf16[768,256]{1,0:T(8,128)(2,1)S(1)}, u32[]{:S(2)}, u32[]{:S(2)}) collective-permute-start(bf16[768,256]{1,0:T(8,128)(2,1)S(1)} %get-tuple-element.25), channel_id=1, source_target_pairs={{0,1},{1,0},{2,3},{3,2},{4,5},{5,4},{6,7},{7,6},{8,9},{9,8},{10,11... | collective-permute-start | bytes 1179656 | tf_op jit(solution)/shard_map/ppermute | solution.py:312
  59.6 9.6 %collective-permute-start.8 = (bf16[256,256]{1,0:T(8,128)(2,1)S(1)}, bf16[256,256]{1,0:T(8,128)(2,1)S(1)}, u32[]{:S(2)}, u32[]{:S(2)}) collective-permute-start(bf16[256,256]{1,0:T(8,128)(2,1)S(1)} %get-tuple-element.23), channel_id=1, source_target_pairs={{0,1},{1,0},{2,3},{3,2},{4,5},{5,4},{6,7},{7,6},{8,9},{9,8},{10,11... | collective-permute-start | bytes 393224 | tf_op jit(solution)/shard_map/ppermute | solution.py:312
  68.1 1.9 %collective-permute-start.11 = (bf16[256,256]{1,0:T(8,128)(2,1)S(1)}, bf16[256,256]{1,0:T(8,128)(2,1)S(1)}, u32[]{:S(2)}, u32[]{:S(2)}) collective-permute-start(bf16[256,256]{1,0:T(8,128)(2,1)S(1)} %get-tuple-element.26), channel_id=1, source_target_pairs={{0,1},{1,0},{2,3},{3,2},{4,5},{5,4},{6,7},{7,6},{8,9},{9,8},{10,11... | collective-permute-start | bytes 393224 | tf_op jit(solution)/shard_map/ppermute | solution.py:312
  70.0 1.0 copy-start.9
  71.0 1.0 copy-start.11
  72.0 35.1 %copy-start.5 = (bf16[256,1024]{1,0:T(8,128)(2,1)S(1)}, bf16[256,1024]{1,0:T(8,128)(2,1)}, u32[]{:S(2)}) copy-start(bf16[256,1024]{1,0:T(8,128)(2,1)} %copy-done.4) | copy-start | bytes 1572868
  72.0 35.1 %copy-start.6 = (f32[1024]{0:T(1024)S(1)}, f32[1024]{0:T(1024)}, u32[]{:S(2)}) copy-start(f32[1024]{0:T(1024)} %param.14) | copy-start | bytes 12292
  72.0 35.1 %copy-start.7 = (s32[1,256,1]{1,2,0:T(1,128)S(1)}, s32[1,256,1]{1,2,0:T(1,128)}, u32[]{:S(2)}) copy-start(s32[1,256,1]{1,2,0:T(1,128)} %param.19) | copy-start | bytes 3076
  107.2 1.6 copy-start.3
  139.1 40.7 %copy-start.1 = (bf16[1,512,1024]{2,1,0:T(8,128)(2,1)S(1)}, bf16[1,512,1024]{2,1,0:T(8,128)(2,1)}, u32[]{:S(2)}) copy-start(bf16[1,512,1024]{2,1,0:T(8,128)(2,1)} %param.11) | copy-start | bytes 3145732
  (2 other events, 1.4 us)
Sparse Core Ops, SparseCore 0:
  9.1 40.4 all-gather.1

commit v3 on v2

v3 whole, which is shorter than its diff:
```python
import functools
import math

import jax
import jax.numpy as jnp
from jax import lax
from jax.experimental import pallas as pl
from jax.experimental.pallas import tpu as pltpu
from jax.sharding import PartitionSpec as P

HS = 64
LANES = 128
HALF = 128
SLOTS = 4
eps_norm = 1e-06
score_gain = 2.5
SCALE2 = score_gain / math.sqrt(HS) * math.log2(math.e)

A0, A1, A2, A3 = (0, 0), (1, 0), (2, 0), (3, 0)
B0, B1, B2, B3 = (0, 1), (1, 1), (2, 1), (3, 1)
EARLY = [(c, h) for c in (A0, A3, A1, B0) for h in (0, 1)]
LATE = [(A2, 0), (B3, 0), (A2, 1), (B1, 0), (B1, 1), (B3, 1), (B2, 0), (B2, 1)]
THIRD, REST = 96, 176


def params(limit):
    return pltpu.CompilerParams(vmem_limit_bytes=limit << 20)


def cost(flops, moved, exps=0):
    return pl.CostEstimate(flops=int(flops), bytes_accessed=int(moved), transcendentals=int(exps))


def dot32(a, b):
    return jnp.dot(a, b, preferred_element_type=jnp.float32)


def dot_first(a, b):
    return lax.dot_general(a, b, (((0,), (0,)), ((), ())), preferred_element_type=jnp.float32)


def iota(shape, axis):
    return lax.broadcasted_iota(jnp.int32, shape, axis)


def one_hot(flag):
    return jnp.where(flag, 1.0, 0.0).astype(jnp.bfloat16)


def rms_scale(values, gain):
    power = jnp.mean(values * values, axis=-1, keepdims=True)
    return values * lax.rsqrt(power + eps_norm) * gain


def gather_kernel(*refs):
    sources, (rows_hbm, normed_ref, w_ref), (kept, doc, gain, rows_ref, sems) = refs[:6], refs[6:9], refs[9:]
    head = sources[3].shape[0]
    targets = [kept, doc, gain] + [w_ref.at[k * head : (k + 1) * head, :] for k in range(3)]
    arrivals = [
        pltpu.make_async_copy(source, target, sems.at[k])
        for k, (source, target) in enumerate(zip(sources, targets))
    ]
    for arrival in arrivals:
        arrival.start()
    w_ref[3 * head :, :] = jnp.zeros((w_ref.shape[0] - 3 * head, w_ref.shape[1]), jnp.bfloat16)
    for arrival in arrivals:
        arrival.wait()
    length = doc.shape[0]
    spread = one_hot(iota((length, kept.shape[1]), 0) == kept[...] % length)
    rows = dot_first(spread, doc[...])
    rows_ref[...] = rows.astype(jnp.bfloat16)
    leaving = pltpu.make_async_copy(rows_ref, rows_hbm, sems.at[6])
    leaving.start()
    normed_ref[...] = rms_scale(rows, gain[...]).astype(jnp.bfloat16)
    leaving.wait()


def gather_rows(kept, document, gain, heads):
    keep, (_, width) = kept.shape[1], document.shape
    shape = jax.ShapeDtypeStruct((keep, width), jnp.bfloat16)
    vmem, hbm = pl.BlockSpec(memory_space=pltpu.VMEM), pl.BlockSpec(memory_space=pltpu.HBM)
    return pl.pallas_call(
        gather_kernel,
        in_specs=[hbm] * 6,
        out_specs=[hbm, vmem, vmem],
        out_shape=(shape, shape, jax.ShapeDtypeStruct((4 * HS, width), jnp.bfloat16)),
        scratch_shapes=[
            pltpu.VMEM(kept.shape, jnp.int32),
            pltpu.VMEM(document.shape, jnp.bfloat16),
            pltpu.VMEM(gain.shape, jnp.float32),
            pltpu.VMEM(shape.shape, jnp.bfloat16),
            pltpu.SemaphoreType.DMA((7,)),
        ],
        compiler_params=params(57),
        cost_estimate=cost(2 * keep * document.size, 2 * (document.size + 2 * keep * width)),
        name="gather_rows",
    )(kept, document, gain, *heads)


def rearrange_kernel(*refs, recipes):
    sources, outs = refs[: len(refs) - len(recipes)], refs[len(refs) - len(recipes) :]
    for out, recipe in zip(outs, recipes):
        at = 0
        for which, start, size in recipe:
            out[at : at + size, :] = sources[which][start : start + size, :]
            at += size


def rearrange(sources, recipes):
    width = sources[0].shape[1]
    rows = [sum(size for _, _, size in recipe) for recipe in recipes]
    return pl.pallas_call(
        functools.partial(rearrange_kernel, recipes=recipes),
        out_shape=[jax.ShapeDtypeStruct((count, width), jnp.bfloat16) for count in rows],
        compiler_params=params(8),
        cost_estimate=cost(0, 4 * sum(rows) * width),
        name="rearrange_rows",
    )(*sources)


def dot_last(a, b):
    return lax.dot_general(a, b, (((1,), (1,)), ((), ())), preferred_element_type=jnp.float32)


def project_kernel(*refs):
    *blocks, own_w, other_w, own_ref, other_ref = refs
    at = 0
    for block in blocks:
        here = pl.ds(at, block.shape[0])
        value = block[...]
        own_ref[here, :] = dot_last(value, own_w[...]).astype(jnp.bfloat16)
        other_ref[here, :] = dot_last(value, other_w[...]).astype(jnp.bfloat16)
        at += block.shape[0]


def project(blocks, own_w, other_w):
    count = sum(block.shape[0] for block in blocks)
    columns, depth = own_w.shape
    shape = jax.ShapeDtypeStruct((count, columns), jnp.bfloat16)
    return pl.pallas_call(
        project_kernel,
        out_shape=(shape, shape),
        compiler_params=params(8),
        cost_estimate=cost(4 * count * own_w.size, 2 * (count * depth + 2 * own_w.size)),
        name="project_rows",
    )(*blocks, own_w, other_w)


def unpack(packed, queries, keys, values):
    at = 0
    for piece in packed:
        count = piece.shape[0]
        here = pl.ds(at, count)
        pair = piece[:, :LANES].astype(jnp.float32)
        lane = iota((count, LANES), 1)
        twice = jnp.where(lane < HS, pair, pltpu.roll(pair, HS, 1)) * SCALE2
        high = twice.astype(jnp.bfloat16).astype(jnp.float32)
        queries[here, :] = jnp.where(lane < HS, high, twice - high).astype(jnp.bfloat16)
        turned = pair.T[HS:, :].astype(jnp.bfloat16)
        keys[:HS, here] = turned
        keys[HS:, here] = turned
        ones = jnp.where(lane == HS, 1.0, 0.0)
        values[here, :] = (piece[:, LANES:].astype(jnp.float32) + ones).astype(jnp.bfloat16)
        at += count


def chunks(total, size):
    return [(at, min(size, total - at)) for at in range(0, total, size)]


def online(query, top, held, stores, chunk):
    for keys, values in stores:
        for at, size in chunks(values.shape[0], chunk):
            scores = dot32(query, keys[:, at : at + size])
            newer = jnp.maximum(top, jnp.max(scores, axis=1, keepdims=True))
            weights = jnp.exp2(scores - newer).astype(jnp.bfloat16)
            held = held * jnp.exp2(top - newer) + dot32(weights, values[at : at + size, :])
            top = newer
    return top, held


def block_of(me, chip, side):
    dx, dy = chip
    x, y = me // 4, me // 2 % 2
    return (x + dx) % 4 * 4 + (1 - y if dy else y) * 2 + side


def attend_kernel(*refs, pieces, olds, last, spans):
    refs = list(refs)
    me = refs.pop(0)[0] if last else None
    packed, refs = refs[:pieces], refs[pieces:]
    stores = []
    for _ in range(olds):
        stores.append(refs[:3])
        refs = refs[3:]
    state = refs.pop(0) if olds else None
    out = refs.pop(0)
    queries, keys, values = refs[:3]
    turn = refs[3] if last else None
    unpack(packed, queries, keys, values)

    def finish(side, at, top, held, units):
        size = held.shape[0]
        if not last:
            lane = iota(held.shape, 1)
            out[pl.ds(at, size), :] = jnp.where(lane == HS + 1, top, held)
            return
        turned = held.T
        result = (turned[:HS] / turned[HS : HS + 1]).astype(jnp.bfloat16)
        core = me % 2
        side = jnp.where(side == 0, core, 1 - core)
        for k, (chip, half) in enumerate(units):
            out[block_of(me, chip, side), :, half * HALF : (half + 1) * HALF] = result[
                :, k * HALF : (k + 1) * HALF
            ]

    def each(total, size, step):
        def one(i, carry):
            step(i, pl.multiple_of(i * size, size))
            return carry

        lax.fori_loop(0, total // size, one, 0)

    for old_queries, _, _ in stores:

        def old_step(i, at):
            size = spans[0]
            held = state[pl.ds(at, size), :]
            query = old_queries[pl.ds(at, size), :]
            top = held[:, HS + 1 : HS + 2]
            finish(i, at, *online(query, top, held, [(keys, values)], 1024), EARLY)

        each(old_queries.shape[0], spans[0], old_step)
    seen = [(k, v) for _, k, v in stores] + [(keys, values)]

    def new_step(i, at):
        size = spans[-1]
        top = jnp.full((size, 1), -1e30, jnp.float32)
        held = jnp.zeros((size, LANES), jnp.float32)
        finish(i, at, *online(queries[pl.ds(at, size), :], top, held, seen, 1024), LATE)

    each(queries.shape[0], spans[-1], new_step)


def attend(packed, stores, state, spans, me=None, blocks=0):
    fresh = sum(piece.shape[0] for piece in packed)
    old = sum(store[0].shape[0] for store in stores)
    last = me is not None
    kept_shapes = [(fresh, LANES), (LANES, fresh), (fresh, LANES)]
    vmem = pl.BlockSpec(memory_space=pltpu.VMEM)
    operands = list(packed) + [value for store in stores for value in store]
    operands += [state] if stores else []
    in_specs = [vmem] * len(operands)
    if last:
        operands, in_specs = [me] + operands, [pl.BlockSpec(memory_space=pltpu.SMEM)] + in_specs
        out_shape = jax.ShapeDtypeStruct((blocks, HS, 2 * HALF), jnp.bfloat16)
        scratch = [pltpu.VMEM(shape, jnp.bfloat16) for shape in kept_shapes]
        scratch.append(pltpu.VMEM((LANES, max(spans)), jnp.float32))
        out_specs = vmem
    else:
        out_shape = [jax.ShapeDtypeStruct((old + fresh, LANES), jnp.float32)]
        out_shape += [jax.ShapeDtypeStruct(shape, jnp.bfloat16) for shape in kept_shapes]
        scratch = []
        out_specs = [vmem] * 4
    pairs = old * fresh + fresh * (old + fresh)
    return pl.pallas_call(
        functools.partial(
            attend_kernel,
            pieces=len(packed),
            olds=len(stores),
            last=last,
            spans=spans,
        ),
        in_specs=in_specs,
        out_specs=out_specs,
        out_shape=out_shape,
        scratch_shapes=scratch,
        compiler_params=params(24),
        cost_estimate=cost(16 * pairs * LANES, 16 * (old + fresh) * LANES, pairs),
        name="attend_heads",
    )(*operands)


def dispatch_kernel(
    me_ref, mixed_ref, near_ref, far_ref, rows_ref, gain_ref, label_ref, first_ref, send_ref, place_ref, mixed
):
    blocks, head, _ = mixed_ref.shape
    me = me_ref[0]
    for k in range(blocks):
        chip = (k // 2 % 4, k % 2)
        side = me % 2 if k < blocks // 2 else 1 - me % 2
        mixed[k * head : (k + 1) * head, :] = mixed_ref[block_of(me, chip, side)]
    inner = near_ref.shape[0]
    first = dot_first(mixed[:inner, :], near_ref[...]) + dot_first(mixed[inner:, :], far_ref[...])
    first = rows_ref[...].astype(jnp.float32) + first
    first_ref[...] = first
    entry = rms_scale(first, gain_ref[...]).astype(jnp.bfloat16)
    keep, width = first.shape
    label = label_ref[...].astype(jnp.float32)
    across = jnp.broadcast_to(label, (keep, keep))
    same = (across == across.T) & (iota((keep, keep), 0) < iota((keep, keep), 1))
    slot = jnp.sum(jnp.where(same, 1.0, 0.0), axis=0, keepdims=True)
    place = (label * (2 * SLOTS) + slot).astype(jnp.int32)
    place_ref[...] = place
    places = send_ref.shape[0]
    half = width // 2
    row = iota((places, keep), 0)
    send = dot32(one_hot(row == place), entry[:, :half])
    send = send + dot32(one_hot(row == place + SLOTS), entry[:, half:])
    send_ref[...] = send.astype(jnp.bfloat16)


def dispatch(me, mixed, near, far, rows, gain, label, experts):
    keep, width = rows.shape
    places = experts * 2 * SLOTS
    vmem = pl.BlockSpec(memory_space=pltpu.VMEM)
    return pl.pallas_call(
        dispatch_kernel,
        in_specs=[pl.BlockSpec(memory_space=pltpu.SMEM)] + [vmem] * 6,
        scratch_shapes=[pltpu.VMEM((mixed.shape[0] * mixed.shape[1], keep), jnp.bfloat16)],
        out_shape=(
            jax.ShapeDtypeStruct((keep, width), jnp.float32),
            jax.ShapeDtypeStruct((places, width // 2), jnp.bfloat16),
            jax.ShapeDtypeStruct((1, keep), jnp.int32),
        ),
        compiler_params=params(24),
        cost_estimate=cost(8 * keep * near.size, 4 * near.size + 10 * keep * width),
        name="dispatch_rows",
    )(me, mixed, near, far, rows, gain, label)


def expert_kernel(slots_ref, w_in_ref, w_back_ref, out_ref, entry, hidden, total):
    count, half = slots_ref.shape
    pairs = count // 16
    low_side = iota((pairs, 8, half), 1) < SLOTS
    got = slots_ref[...].astype(jnp.float32).reshape(pairs, 2, 8, half)
    even, odd = got[:, 0], got[:, 1]
    low = jnp.where(low_side, even, pltpu.roll(odd, SLOTS, 1))
    high = jnp.where(low_side, pltpu.roll(even, SLOTS, 1), odd)
    entry[:, :half] = low.reshape(count // 2, half).astype(jnp.bfloat16)
    entry[:, half:] = high.reshape(count // 2, half).astype(jnp.bfloat16)
    tile = 256
    for at in range(0, hidden.shape[1], tile):
        part = dot32(entry[...], w_in_ref[:, at : at + tile])
        hidden[:, at : at + tile] = jnp.maximum(part, 0.0).astype(jnp.bfloat16)
    for at in range(0, total.shape[1], tile):
        total[:, at : at + tile] = dot32(hidden[...], w_back_ref[:, at : at + tile])
    low = total[:, :half].reshape(pairs, 8, half)
    high = total[:, half:].reshape(pairs, 8, half)
    even = jnp.where(low_side, low, pltpu.roll(high, SLOTS, 1))
    odd = jnp.where(low_side, pltpu.roll(low, SLOTS, 1), high)
    both = jnp.concatenate([even[:, None], odd[:, None]], axis=1)
    out_ref[...] = both.reshape(count, half).astype(jnp.bfloat16)


def run_expert(slots, w_in, w_back):
    count, half = slots.shape
    width, inner = w_in.shape
    vmem = pl.BlockSpec(memory_space=pltpu.VMEM)
    return pl.pallas_call(
        expert_kernel,
        in_specs=[vmem] * 3,
        out_specs=vmem,
        out_shape=jax.ShapeDtypeStruct((count, half), jnp.bfloat16),
        scratch_shapes=[
            pltpu.VMEM((count // 2, width), jnp.bfloat16),
            pltpu.VMEM((count // 2, inner), jnp.bfloat16),
            pltpu.VMEM((count // 2, width), jnp.float32),
        ],
        compiler_params=params(16),
        cost_estimate=cost(2 * count * w_in.size, 4 * w_in.size + 4 * slots.size),
        name="run_expert",
    )(slots, w_in, w_back)


def combine_kernel(back_ref, place_ref, first_ref, kept_ref, doc_ref, out_ref):
    back = back_ref[...]
    places, half = back.shape
    place = place_ref[...]
    keep = place.shape[1]
    row = iota((places, keep), 0)
    low = dot_first(one_hot(row == place), back)
    high = dot_first(one_hot(row == place + SLOTS), back)
    taken = jnp.concatenate([low, high], axis=1)
    second = (first_ref[...] + taken).astype(jnp.bfloat16)
    length = doc_ref.shape[0]
    spread = iota((length, keep), 0) == kept_ref[...] % length
    fresh = dot32(one_hot(spread), second).astype(jnp.bfloat16)
    hit = jnp.max(jnp.where(spread, 1.0, 0.0), axis=1, keepdims=True) > 0.5
    out_ref[...] = jnp.where(hit, fresh, doc_ref[...])


def combine(back, place, first, kept, document):
    keep, width = first.shape
    return pl.pallas_call(
        combine_kernel,
        out_shape=jax.ShapeDtypeStruct(document.shape, document.dtype),
        compiler_params=params(16),
        cost_estimate=cost(2 * keep * (2 * back.size + document.size), 6 * document.size),
        name="combine_rows",
    )(back, place, first, kept, document)


def body(
    tokens, kept, gain_attn, gain_ffn, w_query, w_key, w_value, w_out, expert_ids, w_in, w_back
):
    document = tokens[0]
    width = document.shape[1]
    ctx_count = lax.axis_size("ctx")
    experts = lax.axis_size("dp") * ctx_count
    me = lax.axis_index("ctx").astype(jnp.int32)[None]
    keep = kept.shape[1]

    def along(value, step):
        pairs = [(i, (i // 4 + step) % 4 * 4 + i % 4) for i in range(ctx_count)]
        return lax.ppermute(value, "ctx", pairs)

    def flip(value, bit):
        return lax.ppermute(value, "ctx", [(i, i ^ bit) for i in range(ctx_count)])

    heads = (w_query.T, w_key.T, w_value.T)
    rows, normed, own_w = gather_rows(kept, document, gain_attn[None], heads)

    a3, a1, b0 = along(normed, 1), along(normed, 3), flip(normed, 2)
    other_w = flip(own_w, 1)

    def trade(blocks):
        mine, theirs = project(blocks, own_w, other_w)
        return mine, flip(theirs, 1)

    own0, other0 = trade([normed])
    a3, a1, b0, w_mine, own0 = lax.optimization_barrier((a3, a1, b0, w_out, own0))
    low, high, left = (0, 0, HALF), (0, HALF, HALF), (1, HALF, HALF)
    p1, p2, p3 = rearrange([a3, a1, b0], [(low, (2, 0, HALF)), (left, (2, 0, HALF)), (left, high)])
    a3, a1, b0, p1, p2, p3 = lax.optimization_barrier((a3, a1, b0, p1, p2, p3))
    r1, r2, r3 = along(p1, 1), along(p2, 3), flip(p3, 2)
    w_next = lax.ppermute(w_mine, ("dp", "ctx"), [(i, i ^ 18) for i in range(experts)])
    own1, other1 = trade([a3, a1, b0])
    state, *store = attend([own0, own1, other0, other1], [], None, (1024,))
    r1, r2, r3, w_next, state = lax.optimization_barrier((r1, r2, r3, w_next, state))
    count = w_out.shape[0]
    q1, q2, q3, w_pair = rearrange(
        [r1, r2, r3, w_mine, w_next],
        [
            ((0, HALF, THIRD),),
            ((0, THIRD, HALF - THIRD), (1, 0, REST - HALF)),
            ((2, REST - HALF, keep - REST),),
            ((3, 0, count), (4, 0, count)),
        ],
    )
    r1, r2, r3, q1, q2, q3 = lax.optimization_barrier((r1, r2, r3, q1, q2, q3))
    t1, t2, t3 = along(q1, 1), flip(q2, 2), along(q3, 3)
    own2, other2 = trade([r1, r2, r3])
    t1, t2, t3, w_pair, own2 = lax.optimization_barrier((t1, t2, t3, w_pair, own2))
    own3, other3 = trade([t1, t2, t3])
    w_steps = [along(w_pair, 3), along(w_pair, 2), along(w_pair, 1)]
    mixed = attend([own2, own3, other2, other3], [store], state, (1024, 1024), me, ctx_count)
    *w_steps, mixed = lax.optimization_barrier((*w_steps, mixed))
    (w_near,) = rearrange([w_pair, *w_steps], [tuple((k, 0, 2 * count) for k in range(4))])
    w_far = flip(w_near, 1)
    parts = lax.all_to_all(mixed, "ctx", split_axis=0, concat_axis=0, tiled=True)

    label = expert_ids[:, :, 0]
    first, send, place = dispatch(
        me, parts, w_near, w_far, rows, gain_ffn[None], label, experts
    )
    names = ("dp", "ctx")
    send = send.reshape(experts, 2 * SLOTS, width // 2)
    got = lax.all_to_all(send, names, split_axis=0, concat_axis=0, tiled=True)
    answer = run_expert(got.reshape(-1, width // 2), w_in[0], w_back[0])
    answer = answer.reshape(experts, 2 * SLOTS, width // 2)
    back = lax.all_to_all(answer, names, split_axis=0, concat_axis=0, tiled=True)
    return combine(back.reshape(-1, width // 2), place, first, kept, document)[None]


def solution(mesh):
    return jax.shard_map(
        body,
        mesh=mesh,
        in_specs=(
            P("dp", "ctx", None),
            P("dp", "ctx"),
            P(),
            P(),
            P(None, "ctx"),
            P(None, "ctx"),
            P(None, "ctx"),
            P("ctx", None),
            P("dp", "ctx", None),
            P(("dp", "ctx"), None, None),
            P(("dp", "ctx"), None, None),
        ),
        out_specs=P("dp", "ctx", None),
        check_vma=False,
    )
```

time: 189 us -> 154 us (0.81)
  waiting for transfers between devices: 31.9 us -> 16.4 us
  between operations: 13.6 us -> 0.25 us
  starting transfers between devices: 17.2 us -> 25 us
  local copies, waits for them, and re-layouts: 11 us -> 5.97 us
  Pallas kernels: 45.7 us -> 41 us
  other arithmetic: 3.3 us -> 0.01 us
    ppermute x8 -> x9, waiting for transfers between devices: 15.8 us -> 3.23 us  [flip(): return lax.ppermute(value, 'ctx', [(i, i ^ bit) for i in range(ctx_count)])]
    ppermute x4 -> x9, starting transfers between devices: 5.52 us -> 12.1 us  [along(): return lax.ppermute(value, 'ctx', pairs)]
    pallas_call x4 -> x8, Pallas kernels: 40.9 us -> 35.5 us  [the longest x2 23.8 us: attend(): pl.pallas_call(functools.partial(attend_kernel, pieces=len(packed), olds=...]
    unnamed x29 -> x36, local copies, waits for them, and re-layouts: 10.7 us -> 5.97 us
    concatenate x3 -> x0, other arithmetic: 2.62 us -> none  [the longest x1 1.31 us: body(): jnp.concatenate([w_query, w_key, w_value, jnp.zeros_like(w_value)], axis=1)]
    ppermute x4 -> x9, waiting for transfers between devices: 15.4 us -> 13.1 us  [along(): return lax.ppermute(value, 'ctx', pairs)]
    ppermute x0 -> x1, starting transfers between devices: none -> 1.9 us  [body(): lax.ppermute(w_mine, ('dp', 'ctx'), [(i, i ^ 18) for i in range(experts)])]
    ppermute x8 -> x9, starting transfers between devices: 11.7 us -> 10.9 us  [flip(): return lax.ppermute(value, 'ctx', [(i, i ^ bit) for i in range(ctx_count)])]
  transfers between devices with their start and end apart: 13 -> 19, of which waited for: 6 -> 7; matrix products, arithmetic and copies ran while one was open for 4% -> 0% of each run, Pallas kernels for 13% -> 17%
where the time goes in v3:
time: 154 us; the launch traced here: 153 us
  blocking collectives  64.8 us (42%)
  Pallas kernels  41 us (27%)
  starting transfers between devices  25 us (16%)
  waiting for transfers between devices  16.4 us (11%)
  local copies, waits for them, and re-layouts  5.97 us (4%)
    all_to_all x1, blocking collectives, body(): got = lax.all_to_all(send, names, split_axis=0, concat_axis=0, tiled=True)  28.3 us
    pallas_call x2, Pallas kernels, attend(): pl.pallas_call(functools.partial(attend_kernel, pieces=len(packed), olds=...  23.8 us
    all_to_all x1, blocking collectives, body(): lax.all_to_all(answer, names, split_axis=0, concat_axis=0, tiled=True)  23.1 us
    all_to_all x1, blocking collectives, body(): lax.all_to_all(mixed, 'ctx', split_axis=0, concat_axis=0, tiled=True)  13.5 us
    ppermute x9, waiting for transfers between devices, along(): return lax.ppermute(value, 'ctx', pairs)  13.1 us
    ppermute x9, starting transfers between devices, along(): return lax.ppermute(value, 'ctx', pairs)  12.1 us
    ppermute x9, starting transfers between devices, flip(): return lax.ppermute(value, 'ctx', [(i, i ^ bit) for i in range(ctx_count)])  10.9 us
    pallas_call x1, Pallas kernels, run_expert(): pl.pallas_call(expert_kernel, in_specs=[vmem] * 3, out_specs=vmem, out_sh...  6.2 us
  transfers between devices with their start and end apart: 19, of which 7 were waited for; matrix products, arithmetic and copies ran while one was open for 0% of the time, Pallas kernels for 17%

profile of v3, /device:TPU:1, one launch (start us, length us, event | category | flops | bytes accessed | tf_op | source)
XLA Modules:
  0.0 153.4 jit_solution(1404264008187357502)
XLA Ops:
  0.0 3.7 %gather_rows.1 = (bf16[256,1024]{1,0:T(8,128)(2,1)}, bf16[256,1024]{1,0:T(8,128)(2,1)}, bf16[256,1024]{1,0:T(8,128)(2,1)}) custom-call(s32[1,256]{1,0:T(1,128)} %kept_ref.1, bf16[512,1024]{1,0:T(8,128)(2,1)} %bitcast.15, f32[1,1024]{1,0:T(1,128)} %bitcast.32, bf16[64,1024]{1,0:T(8,128)(2,1)} %bitcast.29, bf16[64,1024]{1,0:T(8,128)(2,1)} %bitcast.30, ...), custom_call_target="tpu_custom_call" | custom-call | flops 268435456 | bytes 2097152 | tf_op jit(solution)/shard_map/gather_rows/pallas_call | solution.py:82
  3.7 1.5 collective-permute-start.3
  6.5 1.4 collective-permute-start.1
  7.9 1.4 collective-permute-start.2
  11.8 8.3 %collective-permute-done.refs_0_ = bf16[256,1024]{1,0:T(8,128)(2,1)S(1)} collective-permute-done((bf16[256,1024]{1,0:T(8,128)(2,1)}, bf16[256,1024]{1,0:T(8,128)(2,1)S(1)}, u32[]{:S(2)}, u32[]{:S(2)}) %collective-permute-start) | collective-permute-done | bytes 524320 | tf_op jit(solution)/shard_map/ppermute | solution.py:416
  23.1 1.6 %collective-permute-start.9 = (bf16[768,256]{1,0:T(8,128)(2,1)S(1)}, bf16[768,256]{1,0:T(8,128)(2,1)S(1)}, u32[]{:S(2)}, u32[]{:S(2)}) collective-permute-start(bf16[768,256]{1,0:T(8,128)(2,1)S(1)} %get-tuple-element.80), channel_id=1, source_target_pairs={{0,1},{1,0},{2,3},{3,2},{4,5},{5,4},{6,7},{7,6},{8,9},{9,8},{10,11... | collective-permute-start | bytes 1179656 | tf_op jit(solution)/shard_map/ppermute | solution.py:419
  24.8 2.6 %collective-permute-start.5 = (bf16[256,1024]{1,0:T(8,128)(2,1)S(1)}, bf16[256,1024]{1,0:T(8,128)(2,1)S(1)}, u32[]{:S(2)}, u32[]{:S(2)}) collective-permute-start(bf16[256,1024]{1,0:T(8,128)(2,1)S(1)} %get-tuple-element.71), channel_id=1, source_target_pairs={{0,12},{1,13},{2,14},{3,15},{4,0},{5,1},{6,2},{7,3},{8,4},{9,5},{1... | collective-permute-start | bytes 1572872 | tf_op jit(solution)/shard_map/ppermute | solution.py:416
  27.4 1.4 collective-permute-start.6
  28.8 1.9 %collective-permute-start.7 = (bf16[64,1024]{1,0:T(8,128)(2,1)S(1)}, bf16[64,1024]{1,0:T(8,128)(2,1)S(1)}, u32[]{:S(2)}, u32[]{:S(2)}) collective-permute-start(bf16[64,1024]{1,0:T(8,128)(2,1)S(1)} %copy-done.5), channel_id=1, source_target_pairs={{0,18},{1,19},{2,16},{3,17},{4,22},{5,23},{6,20},{7,21},{8,26},{9,... | collective-permute-start | bytes 393224 | tf_op jit(solution)/shard_map/ppermute | solution.py:437
  30.7 5.5 %attend_heads.2 = (f32[2048,128]{1,0:T(8,128)S(1)}, bf16[2048,128]{1,0:T(8,128)(2,1)S(1)}, bf16[128,2048]{1,0:T(8,128)(2,1)S(1)}, bf16[2048,128]{1,0:T(8,128)(2,1)S(1)}) custom-call(bf16[256,256]{1,0:T(8,128)(2,1)S(1)} %get-tuple-element.74.refs_0_, bf16[768,256]{1,0:T(8,128)(2,1)S(1)} %get-tuple-element.78.refs_1_, ...), custom_call_target="tpu_custom_call" | custom-call | flops 8589934592 | bytes 4194304 | tf_op jit(solution)/shard_map/attend_heads/pallas_call | solution.py:266
  36.3 2.8 %collective-permute-done.4.refs_0_ = bf16[256,1024]{1,0:T(8,128)(2,1)S(1)} collective-permute-done((bf16[256,1024]{1,0:T(8,128)(2,1)S(1)}, bf16[256,1024]{1,0:T(8,128)(2,1)S(1)}, u32[]{:S(2)}, u32[]{:S(2)}) %collective-permute-start.4) | collective-permute-done | bytes 524320 | tf_op jit(solution)/shard_map/ppermute | solution.py:416
  41.0 2.0 %collective-permute-start.16 = (bf16[768,256]{1,0:T(8,128)(2,1)S(1)}, bf16[768,256]{1,0:T(8,128)(2,1)S(1)}, u32[]{:S(2)}, u32[]{:S(2)}) collective-permute-start(bf16[768,256]{1,0:T(8,128)(2,1)S(1)} %get-tuple-element.103), channel_id=1, source_target_pairs={{0,1},{1,0},{2,3},{3,2},{4,5},{5,4},{6,7},{7,6},{8,9},{9,8},{10,11... | collective-permute-start | bytes 1179656 | tf_op jit(solution)/shard_map/ppermute | solution.py:419
  42.9 1.4 collective-permute-start.11
  44.3 2.7 %collective-permute-start.12 = (bf16[80,1024]{1,0:T(8,128)(2,1)S(1)}, bf16[80,1024]{1,0:T(8,128)(2,1)S(1)}, u32[]{:S(2)}, u32[]{:S(2)}) collective-permute-start(bf16[80,1024]{1,0:T(8,128)(2,1)S(1)} %get-tuple-element.91), channel_id=1, source_target_pairs={{0,12},{1,13},{2,14},{3,15},{4,0},{5,1},{6,2},{7,3},{8,4},{9,5},{1... | collective-permute-start | bytes 491528 | tf_op jit(solution)/shard_map/ppermute | solution.py:416
  47.0 1.6 %collective-permute-done.11.refs_1_ = bf16[80,1024]{1,0:T(8,128)(2,1)S(1)} collective-permute-done((bf16[80,1024]{1,0:T(8,128)(2,1)S(1)}, bf16[80,1024]{1,0:T(8,128)(2,1)S(1)}, u32[]{:S(2)}, u32[]{:S(2)}) %collective-permute-start.11) | collective-permute-done | bytes 163872 | tf_op jit(solution)/shard_map/ppermute | solution.py:419
  52.6 3.4 %collective-permute-start.13 = (bf16[128,1024]{1,0:T(8,128)(2,1)S(1)}, bf16[128,1024]{1,0:T(8,128)(2,1)S(1)}, u32[]{:S(2)}, u32[]{:S(2)}) collective-permute-start(bf16[128,1024]{1,0:T(8,128)(2,1)S(1)} %get-tuple-element.97.refs_0_), channel_id=1, source_target_pairs={{0,12},{1,13},{2,14},{3,15},{4,0},{5,1},{6,2},{7,3},{8,4},{9,5},{1... | collective-permute-start | bytes 786440 | tf_op jit(solution)/shard_map/ppermute | solution.py:416
  57.9 1.6 %copy-done.13 = bf16[2048,128]{1,0:T(8,128)(2,1)S(1)} copy-done((bf16[2048,128]{1,0:T(8,128)(2,1)S(1)}, bf16[2048,128]{1,0:T(8,128)(2,1)}, u32[]{:S(2)}) %copy-start.13) | copy-done | bytes 524312
  59.5 18.3 %attend_heads.3 = bf16[16,64,256]{2,1,0:T(8,128)(2,1)S(1)} custom-call(s32[1]{0:T(128)} %bitcast.refs_0_.me_ref, bf16[768,256]{1,0:T(8,128)(2,1)S(1)} %get-tuple-element.98.refs_1_, bf16[256,256]{1,0:T(8,128)(2,1)S(1)} %get-tuple-element.102.refs_2_, bf16[768,256]{1,0:T(8,128)(2,1)S(1)} %collective-permute-done.16.refs_3_, ...), custom_call_target="tpu_custom_call" | custom-call | flops 25769803776 | bytes 8388608 | tf_op jit(solution)/shard_map/attend_heads/pallas_call | solution.py:266
  78.7 13.5 %all_to_all.15.mixed_ref = bf16[16,64,256]{2,1,0:T(8,128)(2,1)S(1)} all-to-all(bf16[16,64,256]{2,1,0:T(8,128)(2,1)S(1)} %attend_heads.3), channel_id=1, replica_groups=mesh['dp'=8,'ctx'=16] {'ctx'}, dimensions={0} | all-to-all | bytes 1048576 | tf_op jit(solution)/shard_map/all_to_all | solution.py:461
  92.2 1.6 %dispatch_rows.1 = (f32[256,1024]{1,0:T(8,128)S(1)}, bf16[1024,512]{1,0:T(8,128)(2,1)S(1)}, s32[1,256]{1,0:T(1,128)S(1)}) custom-call(s32[1]{0:T(128)} %bitcast.refs_0_.me_ref, bf16[16,64,256]{2,1,0:T(8,128)(2,1)S(1)} %all_to_all.15.mixed_ref, bf16[512,1024]{1,0:T(8,128)(2,1)S(1)} %rearrange_rows.5.near_ref, ...), custom_call_target="tpu_custom_call" | custom-call | flops 1073741824 | bytes 4718592 | tf_op jit(solution)/shard_map/dispatch_rows/pallas_call | solution.py:317
  93.8 28.3 %all_to_all.16 = bf16[128,8,512]{2,1,0:T(8,128)(2,1)S(1)} all-to-all(bf16[128,8,512]{2,1,0:T(8,128)(2,1)S(1)} %bitcast.18), channel_id=1, replica_groups=mesh['dp'=8,'ctx'=16] {'dp','ctx'}, dimensions={0} | all-to-all | bytes 2097152 | tf_op jit(solution)/shard_map/all_to_all | solution.py:469
  122.1 6.2 %run_expert.1 = bf16[1024,512]{1,0:T(8,128)(2,1)S(1)} custom-call(bf16[1024,512]{1,0:T(8,128)(2,1)S(1)} %bitcast.19, bf16[1024,2816]{1,0:T(8,128)(2,1)S(1)} %bitcast.23, bf16[2816,1024]{1,0:T(8,128)(2,1)S(1)} %bitcast.26), custom_call_target="tpu_custom_call" | custom-call | flops 5905580032 | bytes 13631488 | tf_op jit(solution)/shard_map/run_expert/pallas_call | solution.py:360
  128.3 23.1 %all_to_all.17 = bf16[128,8,512]{2,1,0:T(8,128)(2,1)S(1)} all-to-all(bf16[128,8,512]{2,1,0:T(8,128)(2,1)S(1)} %bitcast.20), channel_id=1, replica_groups=mesh['dp'=8,'ctx'=16] {'dp','ctx'}, dimensions={0} | all-to-all | bytes 2097152 | tf_op jit(solution)/shard_map/all_to_all | solution.py:472
  151.4 2.0 %combine_rows.1 = bf16[512,1024]{1,0:T(8,128)(2,1)} custom-call(bf16[1024,512]{1,0:T(8,128)(2,1)S(1)} %bitcast.17, s32[1,256]{1,0:T(1,128)S(1)} %get-tuple-element.115.place_ref, f32[256,1024]{1,0:T(8,128)S(1)} %get-tuple-element.116.first_ref, s32[1,256]{1,0:T(1,128)S(1)} %copy-done.6, bf16[512,1024]{1,0:T(8,128)(2,1)S(1)} %bitcast.16), custom_call_target="tpu_custom_call" | custom-call | flops 805306368 | bytes 3145728 | tf_op jit(solution)/shard_map/combine_rows/pallas_call | solution.py:395
  (68 shorter events, 15.7 us)
Async XLA Ops:
  3.7 5.6 %collective-permute-start.3 = (bf16[256,1024]{1,0:T(8,128)(2,1)}, bf16[256,1024]{1,0:T(8,128)(2,1)S(1)}, u32[]{:S(2)}, u32[]{:S(2)}) collective-permute-start(bf16[256,1024]{1,0:T(8,128)(2,1)} %get-tuple-element.62.refs_1_.refs_3_), channel_id=1, source_target_pairs={{0,1},{1,0},{2,3},{3,2},{4,5},{5,4},{6,7},{7,6},{8,9},{9,8},{10,11... | collective-permute-start | bytes 1572872 | tf_op jit(solution)/shard_map/ppermute | solution.py:419
  5.2 14.9 %collective-permute-start = (bf16[256,1024]{1,0:T(8,128)(2,1)}, bf16[256,1024]{1,0:T(8,128)(2,1)S(1)}, u32[]{:S(2)}, u32[]{:S(2)}) collective-permute-start(bf16[256,1024]{1,0:T(8,128)(2,1)} %get-tuple-element.61.refs_0_), channel_id=1, source_target_pairs={{0,4},{1,5},{2,6},{3,7},{4,8},{5,9},{6,10},{7,11},{8,12},{9,13},{1... | collective-permute-start | bytes 1572872 | tf_op jit(solution)/shard_map/ppermute | solution.py:416
  6.5 13.6 %collective-permute-start.1 = (bf16[256,1024]{1,0:T(8,128)(2,1)}, bf16[256,1024]{1,0:T(8,128)(2,1)S(1)}, u32[]{:S(2)}, u32[]{:S(2)}) collective-permute-start(bf16[256,1024]{1,0:T(8,128)(2,1)} %get-tuple-element.61.refs_0_), channel_id=1, source_target_pairs={{0,12},{1,13},{2,14},{3,15},{4,0},{5,1},{6,2},{7,3},{8,4},{9,5},{1... | collective-permute-start | bytes 1572872 | tf_op jit(solution)/shard_map/ppermute | solution.py:416
  7.9 13.1 %collective-permute-start.2 = (bf16[256,1024]{1,0:T(8,128)(2,1)}, bf16[256,1024]{1,0:T(8,128)(2,1)S(1)}, u32[]{:S(2)}, u32[]{:S(2)}) collective-permute-start(bf16[256,1024]{1,0:T(8,128)(2,1)} %get-tuple-element.61.refs_0_), channel_id=1, source_target_pairs={{0,2},{1,3},{2,0},{3,1},{4,6},{5,7},{6,4},{7,5},{8,10},{9,11},{10,... | collective-permute-start | bytes 1572872 | tf_op jit(solution)/shard_map/ppermute | solution.py:419
  23.1 7.6 %collective-permute-start.9 = (bf16[768,256]{1,0:T(8,128)(2,1)S(1)}, bf16[768,256]{1,0:T(8,128)(2,1)S(1)}, u32[]{:S(2)}, u32[]{:S(2)}) collective-permute-start(bf16[768,256]{1,0:T(8,128)(2,1)S(1)} %get-tuple-element.80), channel_id=1, source_target_pairs={{0,1},{1,0},{2,3},{3,2},{4,5},{5,4},{6,7},{7,6},{8,9},{9,8},{10,11... | collective-permute-start | bytes 1179656 | tf_op jit(solution)/shard_map/ppermute | solution.py:419
  24.7 4.2 %collective-permute-start.8 = (bf16[256,256]{1,0:T(8,128)(2,1)S(1)}, bf16[256,256]{1,0:T(8,128)(2,1)S(1)}, u32[]{:S(2)}, u32[]{:S(2)}) collective-permute-start(bf16[256,256]{1,0:T(8,128)(2,1)S(1)} %get-tuple-element.79), channel_id=1, source_target_pairs={{0,1},{1,0},{2,3},{3,2},{4,5},{5,4},{6,7},{7,6},{8,9},{9,8},{10,11... | collective-permute-start | bytes 393224 | tf_op jit(solution)/shard_map/ppermute | solution.py:419
  24.8 14.3 %collective-permute-start.4 = (bf16[256,1024]{1,0:T(8,128)(2,1)S(1)}, bf16[256,1024]{1,0:T(8,128)(2,1)S(1)}, u32[]{:S(2)}, u32[]{:S(2)}) collective-permute-start(bf16[256,1024]{1,0:T(8,128)(2,1)S(1)} %get-tuple-element.70), channel_id=1, source_target_pairs={{0,4},{1,5},{2,6},{3,7},{4,8},{5,9},{6,10},{7,11},{8,12},{9,13},{1... | collective-permute-start | bytes 1572872 | tf_op jit(solution)/shard_map/ppermute | solution.py:416
  24.8 14.2 %collective-permute-start.5 = (bf16[256,1024]{1,0:T(8,128)(2,1)S(1)}, bf16[256,1024]{1,0:T(8,128)(2,1)S(1)}, u32[]{:S(2)}, u32[]{:S(2)}) collective-permute-start(bf16[256,1024]{1,0:T(8,128)(2,1)S(1)} %get-tuple-element.71), channel_id=1, source_target_pairs={{0,12},{1,13},{2,14},{3,15},{4,0},{5,1},{6,2},{7,3},{8,4},{9,5},{1... | collective-permute-start | bytes 1572872 | tf_op jit(solution)/shard_map/ppermute | solution.py:416
  27.4 12.4 %collective-permute-start.6 = (bf16[256,1024]{1,0:T(8,128)(2,1)S(1)}, bf16[256,1024]{1,0:T(8,128)(2,1)S(1)}, u32[]{:S(2)}, u32[]{:S(2)}) collective-permute-start(bf16[256,1024]{1,0:T(8,128)(2,1)S(1)} %get-tuple-element.72), channel_id=1, source_target_pairs={{0,2},{1,3},{2,0},{3,1},{4,6},{5,7},{6,4},{7,5},{8,10},{9,11},{10,... | collective-permute-start | bytes 1572872 | tf_op jit(solution)/shard_map/ppermute | solution.py:419
  28.8 7.4 %collective-permute-start.7 = (bf16[64,1024]{1,0:T(8,128)(2,1)S(1)}, bf16[64,1024]{1,0:T(8,128)(2,1)S(1)}, u32[]{:S(2)}, u32[]{:S(2)}) collective-permute-start(bf16[64,1024]{1,0:T(8,128)(2,1)S(1)} %copy-done.5), channel_id=1, source_target_pairs={{0,18},{1,19},{2,16},{3,17},{4,22},{5,23},{6,20},{7,21},{8,26},{9,... | collective-permute-start | bytes 393224 | tf_op jit(solution)/shard_map/ppermute | solution.py:437
  41.0 15.7 %collective-permute-start.16 = (bf16[768,256]{1,0:T(8,128)(2,1)S(1)}, bf16[768,256]{1,0:T(8,128)(2,1)S(1)}, u32[]{:S(2)}, u32[]{:S(2)}) collective-permute-start(bf16[768,256]{1,0:T(8,128)(2,1)S(1)} %get-tuple-element.103), channel_id=1, source_target_pairs={{0,1},{1,0},{2,3},{3,2},{4,5},{5,4},{6,7},{7,6},{8,9},{9,8},{10,11... | collective-permute-start | bytes 1179656 | tf_op jit(solution)/shard_map/ppermute | solution.py:419
  42.9 7.7 %collective-permute-start.10 = (bf16[96,1024]{1,0:T(8,128)(2,1)S(1)}, bf16[96,1024]{1,0:T(8,128)(2,1)S(1)}, u32[]{:S(2)}, u32[]{:S(2)}) collective-permute-start(bf16[96,1024]{1,0:T(8,128)(2,1)S(1)} %get-tuple-element.89), channel_id=1, source_target_pairs={{0,4},{1,5},{2,6},{3,7},{4,8},{5,9},{6,10},{7,11},{8,12},{9,13},{1... | collective-permute-start | bytes 589832 | tf_op jit(solution)/shard_map/ppermute | solution.py:416
  42.9 5.6 %collective-permute-start.11 = (bf16[80,1024]{1,0:T(8,128)(2,1)S(1)}, bf16[80,1024]{1,0:T(8,128)(2,1)S(1)}, u32[]{:S(2)}, u32[]{:S(2)}) collective-permute-start(bf16[80,1024]{1,0:T(8,128)(2,1)S(1)} %get-tuple-element.90), channel_id=1, source_target_pairs={{0,2},{1,3},{2,0},{3,1},{4,6},{5,7},{6,4},{7,5},{8,10},{9,11},{10,... | collective-permute-start | bytes 491528 | tf_op jit(solution)/shard_map/ppermute | solution.py:419
  44.3 5.6 %collective-permute-start.12 = (bf16[80,1024]{1,0:T(8,128)(2,1)S(1)}, bf16[80,1024]{1,0:T(8,128)(2,1)S(1)}, u32[]{:S(2)}, u32[]{:S(2)}) collective-permute-start(bf16[80,1024]{1,0:T(8,128)(2,1)S(1)} %get-tuple-element.91), channel_id=1, source_target_pairs={{0,12},{1,13},{2,14},{3,15},{4,0},{5,1},{6,2},{7,3},{8,4},{9,5},{1... | collective-permute-start | bytes 491528 | tf_op jit(solution)/shard_map/ppermute | solution.py:416
  51.7 5.0 %collective-permute-start.17 = (bf16[256,256]{1,0:T(8,128)(2,1)S(1)}, bf16[256,256]{1,0:T(8,128)(2,1)S(1)}, u32[]{:S(2)}, u32[]{:S(2)}) collective-permute-start(bf16[256,256]{1,0:T(8,128)(2,1)S(1)} %get-tuple-element.104), channel_id=1, source_target_pairs={{0,1},{1,0},{2,3},{3,2},{4,5},{5,4},{6,7},{7,6},{8,9},{9,8},{10,11... | collective-permute-start | bytes 393224 | tf_op jit(solution)/shard_map/ppermute | solution.py:419
  52.6 25.2 %collective-permute-start.13 = (bf16[128,1024]{1,0:T(8,128)(2,1)S(1)}, bf16[128,1024]{1,0:T(8,128)(2,1)S(1)}, u32[]{:S(2)}, u32[]{:S(2)}) collective-permute-start(bf16[128,1024]{1,0:T(8,128)(2,1)S(1)} %get-tuple-element.97.refs_0_), channel_id=1, source_target_pairs={{0,12},{1,13},{2,14},{3,15},{4,0},{5,1},{6,2},{7,3},{8,4},{9,5},{1... | collective-permute-start | bytes 786440 | tf_op jit(solution)/shard_map/ppermute | solution.py:416
  56.0 21.8 %collective-permute-start.14 = (bf16[128,1024]{1,0:T(8,128)(2,1)S(1)}, bf16[128,1024]{1,0:T(8,128)(2,1)S(1)}, u32[]{:S(2)}, u32[]{:S(2)}) collective-permute-start(bf16[128,1024]{1,0:T(8,128)(2,1)S(1)} %get-tuple-element.97.refs_0_), channel_id=1, source_target_pairs={{0,8},{1,9},{2,10},{3,11},{4,12},{5,13},{6,14},{7,15},{8,0},{9,1},... | collective-permute-start | bytes 786440 | tf_op jit(solution)/shard_map/ppermute | solution.py:416
  56.0 21.9 %collective-permute-start.15 = (bf16[128,1024]{1,0:T(8,128)(2,1)S(1)}, bf16[128,1024]{1,0:T(8,128)(2,1)S(1)}, u32[]{:S(2)}, u32[]{:S(2)}) collective-permute-start(bf16[128,1024]{1,0:T(8,128)(2,1)S(1)} %get-tuple-element.97.refs_0_), channel_id=1, source_target_pairs={{0,4},{1,5},{2,6},{3,7},{4,8},{5,9},{6,10},{7,11},{8,12},{9,13},{1... | collective-permute-start | bytes 786440 | tf_op jit(solution)/shard_map/ppermute | solution.py:416
  56.7 65.3 %slice-start = ((s8[5767168]{0:T(1024)(128)(4,1)}), s8[4194304]{0:T(1024)(128)(4,1)S(1)}, s32[]{:S(2)}) async-start(s8[5767168]{0:T(1024)(128)(4,1)} %bitcast.21), calls=%async_computation.3 | async-start | bytes 8388608
  56.7 65.3 %slice-start.2 = ((s8[5767168]{0:T(1024)(128)(4,1)}), s8[4194304]{0:T(1024)(128)(4,1)S(1)}, s32[]{:S(2)}) async-start(s8[5767168]{0:T(1024)(128)(4,1)} %bitcast.24), calls=%async_computation.5 | async-start | bytes 8388608
  59.5 32.7 %copy-start.9 = (s32[1,256,1]{1,2,0:T(1,128)S(1)}, s32[1,256,1]{1,2,0:T(1,128)}, u32[]{:S(2)}) copy-start(s32[1,256,1]{1,2,0:T(1,128)} %param.19) | copy-start | bytes 3076
  59.5 62.5 %slice-start.1 = ((s8[5767168]{0:T(1024)(128)(4,1)}), s8[1572864]{0:T(1024)(128)(4,1)S(1)}, s32[]{:S(2)}) async-start(s8[5767168]{0:T(1024)(128)(4,1)} %bitcast.21), calls=%async_computation.4 | async-start | bytes 3145728
  59.5 62.5 %slice-start.3 = ((s8[5767168]{0:T(1024)(128)(4,1)}), s8[1572864]{0:T(1024)(128)(4,1)S(1)}, s32[]{:S(2)}) async-start(s8[5767168]{0:T(1024)(128)(4,1)} %bitcast.24), calls=%async_computation.6 | async-start | bytes 3145728
  78.0 14.2 %collective-permute-start.18 = (bf16[512,1024]{1,0:T(8,128)(2,1)S(1)}, bf16[512,1024]{1,0:T(8,128)(2,1)S(1)}, u32[]{:S(2)}, u32[]{:S(2)}) collective-permute-start(bf16[512,1024]{1,0:T(8,128)(2,1)S(1)} %rearrange_rows.5.near_ref), channel_id=1, source_target_pairs={{0,1},{1,0},{2,3},{3,2},{4,5},{5,4},{6,7},{7,6},{8,9},{9,8},{10,11... | collective-permute-start | bytes 3145736 | tf_op jit(solution)/shard_map/ppermute | solution.py:419
  (13 other events, 200.7 us)

commit v4 on v3

--- a/solution.py
+++ b/solution.py
@@ -20,11 +20,11 @@
 B0, B1, B2, B3 = (0, 1), (1, 1), (2, 1), (3, 1)
 EARLY = [(c, h) for c in (A0, A3, A1, B0) for h in (0, 1)]
 LATE = [(A2, 0), (B3, 0), (A2, 1), (B1, 0), (B1, 1), (B3, 1), (B2, 0), (B2, 1)]
-THIRD, REST = 96, 176
+THIRD, REST = 48, 208
 
 
 def params(limit):
-    return pltpu.CompilerParams(vmem_limit_bytes=limit << 20)
+    return pltpu.CompilerParams(vmem_limit_bytes=int(limit * 2**20))
 
 
 def cost(flops, moved, exps=0):
@@ -53,9 +53,9 @@
 
 
 def gather_kernel(*refs):
-    sources, (rows_hbm, normed_ref, w_ref), (kept, doc, gain, rows_ref, sems) = refs[:6], refs[6:9], refs[9:]
+    sources, (rows_hbm, normed_ref, w_ref, out_ref), (kept, doc, gain, rows_ref, sems) = refs[:7], refs[7:11], refs[11:]
     head = sources[3].shape[0]
-    targets = [kept, doc, gain] + [w_ref.at[k * head : (k + 1) * head, :] for k in range(3)]
+    targets = [kept, doc, gain] + [w_ref.at[k * head : (k + 1) * head, :] for k in range(3)] + [out_ref]
     arrivals = [
         pltpu.make_async_copy(source, target, sems.at[k])
         for k, (source, target) in enumerate(zip(sources, targets))
@@ -69,7 +69,7 @@
     spread = one_hot(iota((length, kept.shape[1]), 0) == kept[...] % length)
     rows = dot_first(spread, doc[...])
     rows_ref[...] = rows.astype(jnp.bfloat16)
-    leaving = pltpu.make_async_copy(rows_ref, rows_hbm, sems.at[6])
+    leaving = pltpu.make_async_copy(rows_ref, rows_hbm, sems.at[7])
     leaving.start()
     normed_ref[...] = rms_scale(rows, gain[...]).astype(jnp.bfloat16)
     leaving.wait()
@@ -81,17 +81,22 @@
     vmem, hbm = pl.BlockSpec(memory_space=pltpu.VMEM), pl.BlockSpec(memory_space=pltpu.HBM)
     return pl.pallas_call(
         gather_kernel,
-        in_specs=[hbm] * 6,
-        out_specs=[hbm, vmem, vmem],
-        out_shape=(shape, shape, jax.ShapeDtypeStruct((4 * HS, width), jnp.bfloat16)),
+        in_specs=[hbm] * 7,
+        out_specs=[hbm, vmem, vmem, vmem],
+        out_shape=(
+            shape,
+            pltpu.VMEM(shape.shape, jnp.bfloat16),
+            pltpu.VMEM((4 * HS, width), jnp.bfloat16),
+            pltpu.VMEM(heads[3].shape, jnp.bfloat16),
+        ),
         scratch_shapes=[
             pltpu.VMEM(kept.shape, jnp.int32),
             pltpu.VMEM(document.shape, jnp.bfloat16),
             pltpu.VMEM(gain.shape, jnp.float32),
             pltpu.VMEM(shape.shape, jnp.bfloat16),
-            pltpu.SemaphoreType.DMA((7,)),
+            pltpu.SemaphoreType.DMA((8,)),
         ],
-        compiler_params=params(57),
+        compiler_params=params(62.5),
         cost_estimate=cost(2 * keep * document.size, 2 * (document.size + 2 * keep * width)),
         name="gather_rows",
     )(kept, document, gain, *heads)
@@ -135,13 +140,13 @@
 
 def project(blocks, own_w, other_w):
     count = sum(block.shape[0] for block in blocks)
-    columns, depth = own_w.shape
+    columns = own_w.shape[0]
     shape = jax.ShapeDtypeStruct((count, columns), jnp.bfloat16)
     return pl.pallas_call(
         project_kernel,
         out_shape=(shape, shape),
         compiler_params=params(8),
-        cost_estimate=cost(4 * count * own_w.size, 2 * (count * depth + 2 * own_w.size)),
+        cost_estimate=cost(1, 1),
         name="project_rows",
     )(*blocks, own_w, other_w)
 
@@ -246,6 +251,7 @@
     fresh = sum(piece.shape[0] for piece in packed)
     old = sum(store[0].shape[0] for store in stores)
     last = me is not None
+    total = old + fresh
     kept_shapes = [(fresh, LANES), (LANES, fresh), (fresh, LANES)]
     vmem = pl.BlockSpec(memory_space=pltpu.VMEM)
     operands = list(packed) + [value for store in stores for value in store]
@@ -262,7 +268,6 @@
         out_shape += [jax.ShapeDtypeStruct(shape, jnp.bfloat16) for shape in kept_shapes]
         scratch = []
         out_specs = [vmem] * 4
-    pairs = old * fresh + fresh * (old + fresh)
     return pl.pallas_call(
         functools.partial(
             attend_kernel,
@@ -276,7 +281,7 @@
         out_shape=out_shape,
         scratch_shapes=scratch,
         compiler_params=params(24),
-        cost_estimate=cost(16 * pairs * LANES, 16 * (old + fresh) * LANES, pairs),
+        cost_estimate=cost(32 * total * total * LANES, 16 * total * LANES) if last else cost(1, 1),
         name="attend_heads",
     )(*operands)
 
@@ -286,10 +291,13 @@
 ):
     blocks, head, _ = mixed_ref.shape
     me = me_ref[0]
+    x, y = me // 4, me // 2 % 2
+    other = jnp.where(x % 2 == 0, x + 1, x - 1)
+    columns = (x, other, 3 - x, 3 - other)
     for k in range(blocks):
-        chip = (k // 2 % 4, k % 2)
         side = me % 2 if k < blocks // 2 else 1 - me % 2
-        mixed[k * head : (k + 1) * head, :] = mixed_ref[block_of(me, chip, side)]
+        block = columns[k // 2 % 4] * 4 + (1 - y if k % 2 else y) * 2 + side
+        mixed[k * head : (k + 1) * head, :] = mixed_ref[block]
     inner = near_ref.shape[0]
     first = dot_first(mixed[:inner, :], near_ref[...]) + dot_first(mixed[inner:, :], far_ref[...])
     first = rows_ref[...].astype(jnp.float32) + first
@@ -418,8 +426,9 @@
     def flip(value, bit):
         return lax.ppermute(value, "ctx", [(i, i ^ bit) for i in range(ctx_count)])
 
-    heads = (w_query.T, w_key.T, w_value.T)
-    rows, normed, own_w = gather_rows(kept, document, gain_attn[None], heads)
+    heads = (w_query.T, w_key.T, w_value.T, w_out)
+    me, kept = lax.optimization_barrier((me, kept))
+    rows, normed, own_w, w_mine = gather_rows(kept, document, gain_attn[None], heads)
 
     a3, a1, b0 = along(normed, 1), along(normed, 3), flip(normed, 2)
     other_w = flip(own_w, 1)
@@ -429,34 +438,40 @@
         return mine, flip(theirs, 1)
 
     own0, other0 = trade([normed])
-    a3, a1, b0, w_mine, own0 = lax.optimization_barrier((a3, a1, b0, w_out, own0))
+    w_mine, own0 = lax.optimization_barrier((w_mine, own0))
+    w_next = lax.ppermute(w_mine, ("dp", "ctx"), [(i, i ^ 18) for i in range(experts)])
+    a3, a1, b0, w_next = lax.optimization_barrier((a3, a1, b0, w_next))
     low, high, left = (0, 0, HALF), (0, HALF, HALF), (1, HALF, HALF)
-    p1, p2, p3 = rearrange([a3, a1, b0], [(low, (2, 0, HALF)), (left, (2, 0, HALF)), (left, high)])
+    count = w_out.shape[0]
+    p1, p2, p3, w_pair = rearrange(
+        [a3, a1, b0, w_mine, w_next],
+        [(low, (2, 0, HALF)), (left, (2, 0, HALF)), (left, high), ((3, 0, count), (4, 0, count))],
+    )
     a3, a1, b0, p1, p2, p3 = lax.optimization_barrier((a3, a1, b0, p1, p2, p3))
     r1, r2, r3 = along(p1, 1), along(p2, 3), flip(p3, 2)
-    w_next = lax.ppermute(w_mine, ("dp", "ctx"), [(i, i ^ 18) for i in range(experts)])
     own1, other1 = trade([a3, a1, b0])
     state, *store = attend([own0, own1, other0, other1], [], None, (1024,))
-    r1, r2, r3, w_next, state = lax.optimization_barrier((r1, r2, r3, w_next, state))
-    count = w_out.shape[0]
-    q1, q2, q3, w_pair = rearrange(
-        [r1, r2, r3, w_mine, w_next],
+    r1, r2, r3, state = lax.optimization_barrier((r1, r2, r3, state))
+    q1, q2, q3 = rearrange(
+        [r1, r2, r3],
         [
             ((0, HALF, THIRD),),
             ((0, THIRD, HALF - THIRD), (1, 0, REST - HALF)),
             ((2, REST - HALF, keep - REST),),
-            ((3, 0, count), (4, 0, count)),
         ],
     )
     r1, r2, r3, q1, q2, q3 = lax.optimization_barrier((r1, r2, r3, q1, q2, q3))
     t1, t2, t3 = along(q1, 1), flip(q2, 2), along(q3, 3)
     own2, other2 = trade([r1, r2, r3])
-    t1, t2, t3, w_pair, own2 = lax.optimization_barrier((t1, t2, t3, w_pair, own2))
+    w_pair, own2 = lax.optimization_barrier((w_pair, own2))
+    w_side = lax.ppermute(w_pair, "ctx", [(i, i ^ 4) for i in range(ctx_count)])
+    t1, t2, t3, w_side = lax.optimization_barrier((t1, t2, t3, w_side))
     own3, other3 = trade([t1, t2, t3])
-    w_steps = [along(w_pair, 3), along(w_pair, 2), along(w_pair, 1)]
+    (w_quad,) = rearrange([w_pair, w_side], [((0, 0, 2 * count), (1, 0, 2 * count))])
+    w_rest = lax.ppermute(w_quad, "ctx", [(i, i ^ 12) for i in range(ctx_count)])
     mixed = attend([own2, own3, other2, other3], [store], state, (1024, 1024), me, ctx_count)
-    *w_steps, mixed = lax.optimization_barrier((*w_steps, mixed))
-    (w_near,) = rearrange([w_pair, *w_steps], [tuple((k, 0, 2 * count) for k in range(4))])
+    w_quad, w_rest, mixed = lax.optimization_barrier((w_quad, w_rest, mixed))
+    (w_near,) = rearrange([w_quad, w_rest], [((0, 0, 4 * count), (1, 0, 4 * count))])
     w_far = flip(w_near, 1)
     parts = lax.all_to_all(mixed, "ctx", split_axis=0, concat_axis=0, tiled=True)
 

time: 154 us -> 146 us (0.948)
  local copies, waits for them, and re-layouts: 5.97 us -> 0.05 us
  starting transfers between devices: 25 us -> 22.8 us
    ppermute x9, waiting for transfers between devices: 3.23 us -> 9.28 us  [flip(): return lax.ppermute(value, 'ctx', [(i, i ^ bit) for i in range(ctx_count)])]
    unnamed x36 -> x18, local copies, waits for them, and re-layouts: 5.97 us -> 0.05 us
    ppermute x9 -> x6, waiting for transfers between devices: 13.1 us -> 8.25 us  [along(): return lax.ppermute(value, 'ctx', pairs)]
    ppermute x9 -> x6, starting transfers between devices: 12.1 us -> 7.91 us  [along(): return lax.ppermute(value, 'ctx', pairs)]
  transfers between devices with their start and end apart: 19 -> 18, of which waited for: 7 -> 7; matrix products, arithmetic and copies ran while one was open for 0% -> 0% of each run, Pallas kernels for 17% -> 19%
where the time goes in v4:
time: 146 us
  blocking collectives  65.1 us (45%)
  Pallas kernels  40.1 us (27%)
  starting transfers between devices  22.8 us (16%)
  waiting for transfers between devices  17.5 us (12%)
    all_to_all x1, blocking collectives, body(): got = lax.all_to_all(send, names, split_axis=0, concat_axis=0, tiled=True)  28.1 us
    pallas_call x2, Pallas kernels, attend(): pl.pallas_call(functools.partial(attend_kernel, pieces=len(packed), olds=...  23.8 us
    all_to_all x1, blocking collectives, body(): lax.all_to_all(answer, names, split_axis=0, concat_axis=0, tiled=True)  23.1 us
    all_to_all x1, blocking collectives, body(): lax.all_to_all(mixed, 'ctx', split_axis=0, concat_axis=0, tiled=True)  13.8 us
    ppermute x9, starting transfers between devices, flip(): return lax.ppermute(value, 'ctx', [(i, i ^ bit) for i in range(ctx_count)])  11.5 us
    ppermute x9, waiting for transfers between devices, flip(): return lax.ppermute(value, 'ctx', [(i, i ^ bit) for i in range(ctx_count)])  9.28 us
    ppermute x6, waiting for transfers between devices, along(): return lax.ppermute(value, 'ctx', pairs)  8.25 us
    ppermute x6, starting transfers between devices, along(): return lax.ppermute(value, 'ctx', pairs)  7.91 us
  transfers between devices with their start and end apart: 18, of which 7 were waited for; matrix products, arithmetic and copies ran while one was open for 0% of the time, Pallas kernels for 19%

profile of v4, /device:TPU:1, one launch (start us, length us, event | category | flops | bytes accessed | tf_op | source)
XLA Modules:
  0.0 145.8 jit_solution(10885635164973613843)
XLA Ops:
  0.0 2.7 %gather_rows.1 = (bf16[256,1024]{1,0:T(8,128)(2,1)}, bf16[256,1024]{1,0:T(8,128)(2,1)S(1)}, bf16[256,1024]{1,0:T(8,128)(2,1)S(1)}, bf16[64,1024]{1,0:T(8,128)(2,1)S(1)}) custom-call(s32[1,256]{1,0:T(1,128)} %kept_ref, bf16[512,1024]{1,0:T(8,128)(2,1)} %bitcast.15, f32[1,1024]{1,0:T(1,128)} %bitcast.32, bf16[64,1024]{1,0:T(8,128)(2,1)} %bitcast.29, ...), custom_call_target="tpu_custom_call" | custom-call | flops 268435456 | bytes 2097152 | tf_op jit(solution)/shard_map/gather_rows/pallas_call | solution.py:82
  2.7 1.5 %collective-permute-start.3 = (bf16[256,1024]{1,0:T(8,128)(2,1)S(1)}, bf16[256,1024]{1,0:T(8,128)(2,1)S(1)}, u32[]{:S(2)}, u32[]{:S(2)}) collective-permute-start(bf16[256,1024]{1,0:T(8,128)(2,1)S(1)} %get-tuple-element.68.refs_1_.refs_3_), channel_id=1, source_target_pairs={{0,1},{1,0},{2,3},{3,2},{4,5},{5,4},{6,7},{7,6},{8,9},{9,8},{10,11... | collective-permute-start | bytes 1572872 | tf_op jit(solution)/shard_map/ppermute | solution.py:427
  4.2 1.4 collective-permute-start.2
  5.6 2.5 %collective-permute-start.1 = (bf16[256,1024]{1,0:T(8,128)(2,1)S(1)}, bf16[256,1024]{1,0:T(8,128)(2,1)S(1)}, u32[]{:S(2)}, u32[]{:S(2)}) collective-permute-start(bf16[256,1024]{1,0:T(8,128)(2,1)S(1)} %get-tuple-element.66.refs_0_), channel_id=1, source_target_pairs={{0,12},{1,13},{2,14},{3,15},{4,0},{5,1},{6,2},{7,3},{8,4},{9,5},{1... | collective-permute-start | bytes 1572872 | tf_op jit(solution)/shard_map/ppermute | solution.py:424
  8.6 2.0 %collective-permute-start.4 = (bf16[64,1024]{1,0:T(8,128)(2,1)S(1)}, bf16[64,1024]{1,0:T(8,128)(2,1)S(1)}, u32[]{:S(2)}, u32[]{:S(2)}) collective-permute-start(bf16[64,1024]{1,0:T(8,128)(2,1)S(1)} %get-tuple-element.70.refs_3_), channel_id=1, source_target_pairs={{0,18},{1,19},{2,16},{3,17},{4,22},{5,23},{6,20},{7,21},{8,26},{9,... | collective-permute-start | bytes 393224 | tf_op jit(solution)/shard_map/ppermute | solution.py:442
  10.5 7.1 %collective-permute-done.2.refs_2_ = bf16[256,1024]{1,0:T(8,128)(2,1)S(1)} collective-permute-done((bf16[256,1024]{1,0:T(8,128)(2,1)S(1)}, bf16[256,1024]{1,0:T(8,128)(2,1)S(1)}, u32[]{:S(2)}, u32[]{:S(2)}) %collective-permute-start.2) | collective-permute-done | bytes 524320 | tf_op jit(solution)/shard_map/ppermute | solution.py:427
  17.7 1.3 collective-permute-done.1.refs_1_
  19.0 3.1 %collective-permute-done.refs_0_ = bf16[256,1024]{1,0:T(8,128)(2,1)S(1)} collective-permute-done((bf16[256,1024]{1,0:T(8,128)(2,1)S(1)}, bf16[256,1024]{1,0:T(8,128)(2,1)S(1)}, u32[]{:S(2)}, u32[]{:S(2)}) %collective-permute-start) | collective-permute-done | bytes 524320 | tf_op jit(solution)/shard_map/ppermute | solution.py:424
  22.3 2.7 %collective-permute-start.6 = (bf16[256,1024]{1,0:T(8,128)(2,1)S(1)}, bf16[256,1024]{1,0:T(8,128)(2,1)S(1)}, u32[]{:S(2)}, u32[]{:S(2)}) collective-permute-start(bf16[256,1024]{1,0:T(8,128)(2,1)S(1)} %get-tuple-element.80), channel_id=1, source_target_pairs={{0,12},{1,13},{2,14},{3,15},{4,0},{5,1},{6,2},{7,3},{8,4},{9,5},{1... | collective-permute-start | bytes 1572872 | tf_op jit(solution)/shard_map/ppermute | solution.py:424
  26.2 2.4 %collective-permute-start.9 = (bf16[768,256]{1,0:T(8,128)(2,1)S(1)}, bf16[768,256]{1,0:T(8,128)(2,1)S(1)}, u32[]{:S(2)}, u32[]{:S(2)}) collective-permute-start(bf16[768,256]{1,0:T(8,128)(2,1)S(1)} %get-tuple-element.88), channel_id=1, source_target_pairs={{0,1},{1,0},{2,3},{3,2},{4,5},{5,4},{6,7},{7,6},{8,9},{9,8},{10,11... | collective-permute-start | bytes 1179656 | tf_op jit(solution)/shard_map/ppermute | solution.py:427
  28.7 1.4 collective-permute-done.8.refs_2_
  30.2 5.5 %attend_heads.2 = (f32[2048,128]{1,0:T(8,128)S(1)}, bf16[2048,128]{1,0:T(8,128)(2,1)S(1)}, bf16[128,2048]{1,0:T(8,128)(2,1)S(1)}, bf16[2048,128]{1,0:T(8,128)(2,1)S(1)}) custom-call(bf16[256,256]{1,0:T(8,128)(2,1)S(1)} %get-tuple-element.82.refs_0_, bf16[768,256]{1,0:T(8,128)(2,1)S(1)} %get-tuple-element.86.refs_1_, ...), custom_call_target="tpu_custom_call" | custom-call | flops 1 | bytes 1 | tf_op jit(solution)/shard_map/attend_heads/pallas_call | solution.py:271
  38.2 2.9 %collective-permute-start.15 = (bf16[768,256]{1,0:T(8,128)(2,1)S(1)}, bf16[768,256]{1,0:T(8,128)(2,1)S(1)}, u32[]{:S(2)}, u32[]{:S(2)}) collective-permute-start(bf16[768,256]{1,0:T(8,128)(2,1)S(1)} %get-tuple-element.110), channel_id=1, source_target_pairs={{0,1},{1,0},{2,3},{3,2},{4,5},{5,4},{6,7},{7,6},{8,9},{9,8},{10,11... | collective-permute-start | bytes 1179656 | tf_op jit(solution)/shard_map/ppermute | solution.py:427
  41.1 1.7 %collective-permute-start.10 = (bf16[48,1024]{1,0:T(8,128)(2,1)S(1)}, bf16[48,1024]{1,0:T(8,128)(2,1)S(1)}, u32[]{:S(2)}, u32[]{:S(2)}) collective-permute-start(bf16[48,1024]{1,0:T(8,128)(2,1)S(1)} %get-tuple-element.101), channel_id=1, source_target_pairs={{0,4},{1,5},{2,6},{3,7},{4,8},{5,9},{6,10},{7,11},{8,12},{9,13},{1... | collective-permute-start | bytes 294920 | tf_op jit(solution)/shard_map/ppermute | solution.py:424
  43.8 2.9 %collective-permute-done.10.refs_0_ = bf16[48,1024]{1,0:T(8,128)(2,1)S(1)} collective-permute-done((bf16[48,1024]{1,0:T(8,128)(2,1)S(1)}, bf16[48,1024]{1,0:T(8,128)(2,1)S(1)}, u32[]{:S(2)}, u32[]{:S(2)}) %collective-permute-start.10) | collective-permute-done | bytes 98336 | tf_op jit(solution)/shard_map/ppermute | solution.py:424
  48.7 2.0 %collective-permute-start.16 = (bf16[256,256]{1,0:T(8,128)(2,1)S(1)}, bf16[256,256]{1,0:T(8,128)(2,1)S(1)}, u32[]{:S(2)}, u32[]{:S(2)}) collective-permute-start(bf16[256,256]{1,0:T(8,128)(2,1)S(1)} %get-tuple-element.111), channel_id=1, source_target_pairs={{0,1},{1,0},{2,3},{3,2},{4,5},{5,4},{6,7},{7,6},{8,9},{9,8},{10,11... | collective-permute-start | bytes 393224 | tf_op jit(solution)/shard_map/ppermute | solution.py:427
  50.7 1.3 collective-permute-start.14
  52.1 18.3 %attend_heads.3 = bf16[16,64,256]{2,1,0:T(8,128)(2,1)S(1)} custom-call(s32[1]{0:T(128)} %bitcast.refs_0_.me_ref, bf16[768,256]{1,0:T(8,128)(2,1)S(1)} %get-tuple-element.105.refs_1_, bf16[256,256]{1,0:T(8,128)(2,1)S(1)} %get-tuple-element.109.refs_2_, bf16[768,256]{1,0:T(8,128)(2,1)S(1)} %collective-permute-done.15.refs_3_, ...), custom_call_target="tpu_custom_call" | custom-call | flops 68719476736 | bytes 8388608 | tf_op jit(solution)/shard_map/attend_heads/pallas_call | solution.py:271
  70.8 13.8 %all_to_all.15.mixed_ref = bf16[16,64,256]{2,1,0:T(8,128)(2,1)S(1)} all-to-all(bf16[16,64,256]{2,1,0:T(8,128)(2,1)S(1)} %attend_heads.3), channel_id=1, replica_groups=mesh['dp'=8,'ctx'=16] {'ctx'}, dimensions={0} | all-to-all | bytes 1048576 | tf_op jit(solution)/shard_map/all_to_all | solution.py:476
  84.7 1.6 %dispatch_rows.1 = (f32[256,1024]{1,0:T(8,128)S(1)}, bf16[1024,512]{1,0:T(8,128)(2,1)S(1)}, s32[1,256]{1,0:T(1,128)S(1)}) custom-call(s32[1]{0:T(128)} %bitcast.refs_0_.me_ref, bf16[16,64,256]{2,1,0:T(8,128)(2,1)S(1)} %all_to_all.15.mixed_ref, bf16[512,1024]{1,0:T(8,128)(2,1)S(1)} %rearrange_rows.7.near_ref, ...), custom_call_target="tpu_custom_call" | custom-call | flops 1073741824 | bytes 4718592 | tf_op jit(solution)/shard_map/dispatch_rows/pallas_call | solution.py:325
  86.3 28.1 %all_to_all.16 = bf16[128,8,512]{2,1,0:T(8,128)(2,1)S(1)} all-to-all(bf16[128,8,512]{2,1,0:T(8,128)(2,1)S(1)} %bitcast.18), channel_id=1, replica_groups=mesh['dp'=8,'ctx'=16] {'dp','ctx'}, dimensions={0} | all-to-all | bytes 2097152 | tf_op jit(solution)/shard_map/all_to_all | solution.py:484
  114.5 6.2 %run_expert.1 = bf16[1024,512]{1,0:T(8,128)(2,1)S(1)} custom-call(bf16[1024,512]{1,0:T(8,128)(2,1)S(1)} %bitcast.19, bf16[1024,2816]{1,0:T(8,128)(2,1)S(1)} %bitcast.23, bf16[2816,1024]{1,0:T(8,128)(2,1)S(1)} %bitcast.26), custom_call_target="tpu_custom_call" | custom-call | flops 5905580032 | bytes 13631488 | tf_op jit(solution)/shard_map/run_expert/pallas_call | solution.py:368
  120.7 23.1 %all_to_all.17 = bf16[128,8,512]{2,1,0:T(8,128)(2,1)S(1)} all-to-all(bf16[128,8,512]{2,1,0:T(8,128)(2,1)S(1)} %bitcast.20), channel_id=1, replica_groups=mesh['dp'=8,'ctx'=16] {'dp','ctx'}, dimensions={0} | all-to-all | bytes 2097152 | tf_op jit(solution)/shard_map/all_to_all | solution.py:487
  143.8 2.0 %combine_rows.1 = bf16[512,1024]{1,0:T(8,128)(2,1)} custom-call(bf16[1024,512]{1,0:T(8,128)(2,1)S(1)} %bitcast.17, s32[1,256]{1,0:T(1,128)S(1)} %get-tuple-element.121.place_ref, f32[256,1024]{1,0:T(8,128)S(1)} %get-tuple-element.122.first_ref, s32[1,256]{1,0:T(1,128)S(1)} %copy-done.1, bf16[512,1024]{1,0:T(8,128)(2,1)S(1)} %bitcast.16), custom_call_target="tpu_custom_call" | custom-call | flops 805306368 | bytes 3145728 | tf_op jit(solution)/shard_map/combine_rows/pallas_call | solution.py:403
  (49 shorter events, 8.1 us)
Async XLA Ops:
  2.7 5.4 %collective-permute-start.3 = (bf16[256,1024]{1,0:T(8,128)(2,1)S(1)}, bf16[256,1024]{1,0:T(8,128)(2,1)S(1)}, u32[]{:S(2)}, u32[]{:S(2)}) collective-permute-start(bf16[256,1024]{1,0:T(8,128)(2,1)S(1)} %get-tuple-element.68.refs_1_.refs_3_), channel_id=1, source_target_pairs={{0,1},{1,0},{2,3},{3,2},{4,5},{5,4},{6,7},{7,6},{8,9},{9,8},{10,11... | collective-permute-start | bytes 1572872 | tf_op jit(solution)/shard_map/ppermute | solution.py:427
  4.2 13.5 %collective-permute-start.2 = (bf16[256,1024]{1,0:T(8,128)(2,1)S(1)}, bf16[256,1024]{1,0:T(8,128)(2,1)S(1)}, u32[]{:S(2)}, u32[]{:S(2)}) collective-permute-start(bf16[256,1024]{1,0:T(8,128)(2,1)S(1)} %get-tuple-element.66.refs_0_), channel_id=1, source_target_pairs={{0,2},{1,3},{2,0},{3,1},{4,6},{5,7},{6,4},{7,5},{8,10},{9,11},{10,... | collective-permute-start | bytes 1572872 | tf_op jit(solution)/shard_map/ppermute | solution.py:427
  5.6 13.4 %collective-permute-start.1 = (bf16[256,1024]{1,0:T(8,128)(2,1)S(1)}, bf16[256,1024]{1,0:T(8,128)(2,1)S(1)}, u32[]{:S(2)}, u32[]{:S(2)}) collective-permute-start(bf16[256,1024]{1,0:T(8,128)(2,1)S(1)} %get-tuple-element.66.refs_0_), channel_id=1, source_target_pairs={{0,12},{1,13},{2,14},{3,15},{4,0},{5,1},{6,2},{7,3},{8,4},{9,5},{1... | collective-permute-start | bytes 1572872 | tf_op jit(solution)/shard_map/ppermute | solution.py:424
  8.1 14.0 %collective-permute-start = (bf16[256,1024]{1,0:T(8,128)(2,1)S(1)}, bf16[256,1024]{1,0:T(8,128)(2,1)S(1)}, u32[]{:S(2)}, u32[]{:S(2)}) collective-permute-start(bf16[256,1024]{1,0:T(8,128)(2,1)S(1)} %get-tuple-element.66.refs_0_), channel_id=1, source_target_pairs={{0,4},{1,5},{2,6},{3,7},{4,8},{5,9},{6,10},{7,11},{8,12},{9,13},{1... | collective-permute-start | bytes 1572872 | tf_op jit(solution)/shard_map/ppermute | solution.py:424
  8.6 13.6 %collective-permute-start.4 = (bf16[64,1024]{1,0:T(8,128)(2,1)S(1)}, bf16[64,1024]{1,0:T(8,128)(2,1)S(1)}, u32[]{:S(2)}, u32[]{:S(2)}) collective-permute-start(bf16[64,1024]{1,0:T(8,128)(2,1)S(1)} %get-tuple-element.70.refs_3_), channel_id=1, source_target_pairs={{0,18},{1,19},{2,16},{3,17},{4,22},{5,23},{6,20},{7,21},{8,26},{9,... | collective-permute-start | bytes 393224 | tf_op jit(solution)/shard_map/ppermute | solution.py:442
  22.3 13.4 %collective-permute-start.5 = (bf16[256,1024]{1,0:T(8,128)(2,1)S(1)}, bf16[256,1024]{1,0:T(8,128)(2,1)S(1)}, u32[]{:S(2)}, u32[]{:S(2)}) collective-permute-start(bf16[256,1024]{1,0:T(8,128)(2,1)S(1)} %get-tuple-element.79), channel_id=1, source_target_pairs={{0,4},{1,5},{2,6},{3,7},{4,8},{5,9},{6,10},{7,11},{8,12},{9,13},{1... | collective-permute-start | bytes 1572872 | tf_op jit(solution)/shard_map/ppermute | solution.py:424
  22.3 13.3 %collective-permute-start.6 = (bf16[256,1024]{1,0:T(8,128)(2,1)S(1)}, bf16[256,1024]{1,0:T(8,128)(2,1)S(1)}, u32[]{:S(2)}, u32[]{:S(2)}) collective-permute-start(bf16[256,1024]{1,0:T(8,128)(2,1)S(1)} %get-tuple-element.80), channel_id=1, source_target_pairs={{0,12},{1,13},{2,14},{3,15},{4,0},{5,1},{6,2},{7,3},{8,4},{9,5},{1... | collective-permute-start | bytes 1572872 | tf_op jit(solution)/shard_map/ppermute | solution.py:424
  25.0 11.3 %collective-permute-start.7 = (bf16[256,1024]{1,0:T(8,128)(2,1)S(1)}, bf16[256,1024]{1,0:T(8,128)(2,1)S(1)}, u32[]{:S(2)}, u32[]{:S(2)}) collective-permute-start(bf16[256,1024]{1,0:T(8,128)(2,1)S(1)} %get-tuple-element.81), channel_id=1, source_target_pairs={{0,2},{1,3},{2,0},{3,1},{4,6},{5,7},{6,4},{7,5},{8,10},{9,11},{10,... | collective-permute-start | bytes 1572872 | tf_op jit(solution)/shard_map/ppermute | solution.py:427
  26.2 4.0 %collective-permute-start.9 = (bf16[768,256]{1,0:T(8,128)(2,1)S(1)}, bf16[768,256]{1,0:T(8,128)(2,1)S(1)}, u32[]{:S(2)}, u32[]{:S(2)}) collective-permute-start(bf16[768,256]{1,0:T(8,128)(2,1)S(1)} %get-tuple-element.88), channel_id=1, source_target_pairs={{0,1},{1,0},{2,3},{3,2},{4,5},{5,4},{6,7},{7,6},{8,9},{9,8},{10,11... | collective-permute-start | bytes 1179656 | tf_op jit(solution)/shard_map/ppermute | solution.py:427
  28.6 1.5 %collective-permute-start.8 = (bf16[256,256]{1,0:T(8,128)(2,1)S(1)}, bf16[256,256]{1,0:T(8,128)(2,1)S(1)}, u32[]{:S(2)}, u32[]{:S(2)}) collective-permute-start(bf16[256,256]{1,0:T(8,128)(2,1)S(1)} %get-tuple-element.87), channel_id=1, source_target_pairs={{0,1},{1,0},{2,3},{3,2},{4,5},{5,4},{6,7},{7,6},{8,9},{9,8},{10,11... | collective-permute-start | bytes 393224 | tf_op jit(solution)/shard_map/ppermute | solution.py:427
  36.4 11.2 %collective-permute-start.11 = (bf16[160,1024]{1,0:T(8,128)(2,1)S(1)}, bf16[160,1024]{1,0:T(8,128)(2,1)S(1)}, u32[]{:S(2)}, u32[]{:S(2)}) collective-permute-start(bf16[160,1024]{1,0:T(8,128)(2,1)S(1)} %get-tuple-element.102), channel_id=1, source_target_pairs={{0,2},{1,3},{2,0},{3,1},{4,6},{5,7},{6,4},{7,5},{8,10},{9,11},{10,... | collective-permute-start | bytes 983048 | tf_op jit(solution)/shard_map/ppermute | solution.py:427
  38.1 9.5 %collective-permute-start.13 = (bf16[128,1024]{1,0:T(8,128)(2,1)S(1)}, bf16[128,1024]{1,0:T(8,128)(2,1)S(1)}, u32[]{:S(2)}, u32[]{:S(2)}) collective-permute-start(bf16[128,1024]{1,0:T(8,128)(2,1)S(1)} %get-tuple-element.100.refs_0_), channel_id=1, source_target_pairs={{0,4},{1,5},{2,6},{3,7},{4,0},{5,1},{6,2},{7,3},{8,12},{9,13},{10,... | collective-permute-start | bytes 786440 | tf_op jit(solution)/shard_map/ppermute | solution.py:467
  38.2 13.8 %collective-permute-start.15 = (bf16[768,256]{1,0:T(8,128)(2,1)S(1)}, bf16[768,256]{1,0:T(8,128)(2,1)S(1)}, u32[]{:S(2)}, u32[]{:S(2)}) collective-permute-start(bf16[768,256]{1,0:T(8,128)(2,1)S(1)} %get-tuple-element.110), channel_id=1, source_target_pairs={{0,1},{1,0},{2,3},{3,2},{4,5},{5,4},{6,7},{7,6},{8,9},{9,8},{10,11... | collective-permute-start | bytes 1179656 | tf_op jit(solution)/shard_map/ppermute | solution.py:427
  41.1 5.6 %collective-permute-start.10 = (bf16[48,1024]{1,0:T(8,128)(2,1)S(1)}, bf16[48,1024]{1,0:T(8,128)(2,1)S(1)}, u32[]{:S(2)}, u32[]{:S(2)}) collective-permute-start(bf16[48,1024]{1,0:T(8,128)(2,1)S(1)} %get-tuple-element.101), channel_id=1, source_target_pairs={{0,4},{1,5},{2,6},{3,7},{4,8},{5,9},{6,10},{7,11},{8,12},{9,13},{1... | collective-permute-start | bytes 294920 | tf_op jit(solution)/shard_map/ppermute | solution.py:424
  42.7 4.8 %collective-permute-start.12 = (bf16[48,1024]{1,0:T(8,128)(2,1)S(1)}, bf16[48,1024]{1,0:T(8,128)(2,1)S(1)}, u32[]{:S(2)}, u32[]{:S(2)}) collective-permute-start(bf16[48,1024]{1,0:T(8,128)(2,1)S(1)} %get-tuple-element.103), channel_id=1, source_target_pairs={{0,12},{1,13},{2,14},{3,15},{4,0},{5,1},{6,2},{7,3},{8,4},{9,5},{1... | collective-permute-start | bytes 294920 | tf_op jit(solution)/shard_map/ppermute | solution.py:424
  48.7 3.3 %collective-permute-start.16 = (bf16[256,256]{1,0:T(8,128)(2,1)S(1)}, bf16[256,256]{1,0:T(8,128)(2,1)S(1)}, u32[]{:S(2)}, u32[]{:S(2)}) collective-permute-start(bf16[256,256]{1,0:T(8,128)(2,1)S(1)} %get-tuple-element.111), channel_id=1, source_target_pairs={{0,1},{1,0},{2,3},{3,2},{4,5},{5,4},{6,7},{7,6},{8,9},{9,8},{10,11... | collective-permute-start | bytes 393224 | tf_op jit(solution)/shard_map/ppermute | solution.py:427
  50.7 19.7 %collective-permute-start.14 = (bf16[256,1024]{1,0:T(8,128)(2,1)S(1)}, bf16[256,1024]{1,0:T(8,128)(2,1)S(1)}, u32[]{:S(2)}, u32[]{:S(2)}) collective-permute-start(bf16[256,1024]{1,0:T(8,128)(2,1)S(1)} %rearrange_rows.6.refs_0_), channel_id=1, source_target_pairs={{0,12},{1,13},{2,14},{3,15},{4,8},{5,9},{6,10},{7,11},{8,4},{9,5},... | collective-permute-start | bytes 1572872 | tf_op jit(solution)/shard_map/ppermute | solution.py:471
  52.0 62.4 %slice-start = ((s8[5767168]{0:T(1024)(128)(4,1)}), s8[4194304]{0:T(1024)(128)(4,1)S(1)}, s32[]{:S(2)}) async-start(s8[5767168]{0:T(1024)(128)(4,1)} %bitcast.21), calls=%async_computation.3 | async-start | bytes 8388608
  52.0 62.4 %slice-start.2 = ((s8[5767168]{0:T(1024)(128)(4,1)}), s8[4194304]{0:T(1024)(128)(4,1)S(1)}, s32[]{:S(2)}) async-start(s8[5767168]{0:T(1024)(128)(4,1)} %bitcast.24), calls=%async_computation.5 | async-start | bytes 8388608
  52.0 32.6 %copy-start.2 = (bf16[256,1024]{1,0:T(8,128)(2,1)S(1)}, bf16[256,1024]{1,0:T(8,128)(2,1)}, u32[]{:S(2)}) copy-start(bf16[256,1024]{1,0:T(8,128)(2,1)} %get-tuple-element.119.rows_ref) | copy-start | bytes 1572868
  52.0 32.6 %copy-start.3 = (f32[1024]{0:T(1024)S(1)}, f32[1024]{0:T(1024)}, u32[]{:S(2)}) copy-start(f32[1024]{0:T(1024)} %param.14) | copy-start | bytes 12292
  52.1 62.4 %slice-start.1 = ((s8[5767168]{0:T(1024)(128)(4,1)}), s8[1572864]{0:T(1024)(128)(4,1)S(1)}, s32[]{:S(2)}) async-start(s8[5767168]{0:T(1024)(128)(4,1)} %bitcast.21), calls=%async_computation.4 | async-start | bytes 3145728
  52.1 62.4 %slice-start.3 = ((s8[5767168]{0:T(1024)(128)(4,1)}), s8[1572864]{0:T(1024)(128)(4,1)S(1)}, s32[]{:S(2)}) async-start(s8[5767168]{0:T(1024)(128)(4,1)} %bitcast.24), calls=%async_computation.6 | async-start | bytes 3145728
  70.5 14.2 %collective-permute-start.17 = (bf16[512,1024]{1,0:T(8,128)(2,1)S(1)}, bf16[512,1024]{1,0:T(8,128)(2,1)S(1)}, u32[]{:S(2)}, u32[]{:S(2)}) collective-permute-start(bf16[512,1024]{1,0:T(8,128)(2,1)S(1)} %rearrange_rows.7.near_ref), channel_id=1, source_target_pairs={{0,1},{1,0},{2,3},{3,2},{4,5},{5,4},{6,7},{7,6},{8,9},{9,8},{10,11... | collective-permute-start | bytes 3145736 | tf_op jit(solution)/shard_map/ppermute | solution.py:427
  (3 other events, 91.3 us)

commit v5 on v4

--- a/solution.py
+++ b/solution.py
@@ -170,6 +170,7 @@
 
 
 def chunks(total, size):
+    size = total if total < 1600 else size
     return [(at, min(size, total - at)) for at in range(0, total, size)]
 
 
@@ -190,7 +191,7 @@
     return (x + dx) % 4 * 4 + (1 - y if dy else y) * 2 + side
 
 
-def attend_kernel(*refs, pieces, olds, last, spans):
+def attend_kernel(*refs, pieces, olds, last, span):
     refs = list(refs)
     me = refs.pop(0)[0] if last else None
     packed, refs = refs[:pieces], refs[pieces:]
@@ -201,14 +202,12 @@
     state = refs.pop(0) if olds else None
     out = refs.pop(0)
     queries, keys, values = refs[:3]
-    turn = refs[3] if last else None
     unpack(packed, queries, keys, values)
 
     def finish(side, at, top, held, units):
-        size = held.shape[0]
         if not last:
             lane = iota(held.shape, 1)
-            out[pl.ds(at, size), :] = jnp.where(lane == HS + 1, top, held)
+            out[pl.ds(at, span), :] = jnp.where(lane == HS + 1, top, held)
             return
         turned = held.T
         result = (turned[:HS] / turned[HS : HS + 1]).astype(jnp.bfloat16)
@@ -219,39 +218,51 @@
                 :, k * HALF : (k + 1) * HALF
             ]
 
-    def each(total, size, step):
+    def each(total, step):
         def one(i, carry):
-            step(i, pl.multiple_of(i * size, size))
+            step(i, pl.multiple_of(i * span, span))
             return carry
 
-        lax.fori_loop(0, total // size, one, 0)
-
-    for old_queries, _, _ in stores:
+        if last:
+            for i in range(total // span):
+                step(i, i * span)
+        else:
+            lax.fori_loop(0, total // span, one, 0)
+
+    if stores:
 
         def old_step(i, at):
-            size = spans[0]
-            held = state[pl.ds(at, size), :]
-            query = old_queries[pl.ds(at, size), :]
+            held = state[pl.ds(at, span), :]
+            query = stores[0][0][pl.ds(at, span), :]
             top = held[:, HS + 1 : HS + 2]
             finish(i, at, *online(query, top, held, [(keys, values)], 1024), EARLY)
 
-        each(old_queries.shape[0], spans[0], old_step)
-    seen = [(k, v) for _, k, v in stores] + [(keys, values)]
-
-    def new_step(i, at):
-        size = spans[-1]
-        top = jnp.full((size, 1), -1e30, jnp.float32)
-        held = jnp.zeros((size, LANES), jnp.float32)
-        finish(i, at, *online(queries[pl.ds(at, size), :], top, held, seen, 1024), LATE)
-
-    each(queries.shape[0], spans[-1], new_step)
-
-
-def attend(packed, stores, state, spans, me=None, blocks=0):
+        each(stores[0][0].shape[0], old_step)
+    if last:
+        late, at = refs[3], 0
+        for side in range(2):
+            for source in (stores[1][0], queries):
+                count = source.shape[0] // 2
+                late[at : at + count, :] = source[side * count : (side + 1) * count, :]
+                at += count
+    if last or not stores:
+        seen = [(k, v) for _, k, v in stores] + [(keys, values)]
+        fresh = late if last else queries
+
+        def new_step(i, at):
+            top = jnp.full((span, 1), -1e30, jnp.float32)
+            held = jnp.zeros((span, LANES), jnp.float32)
+            finish(i, at, *online(fresh[pl.ds(at, span), :], top, held, seen, 1024), LATE)
+
+        each(fresh.shape[0], new_step)
+
+
+def attend(packed, stores=(), state=None, me=None, blocks=0):
     fresh = sum(piece.shape[0] for piece in packed)
     old = sum(store[0].shape[0] for store in stores)
     last = me is not None
     total = old + fresh
+    span = 1024
     kept_shapes = [(fresh, LANES), (LANES, fresh), (fresh, LANES)]
     vmem = pl.BlockSpec(memory_space=pltpu.VMEM)
     operands = list(packed) + [value for store in stores for value in store]
@@ -261,20 +272,16 @@
         operands, in_specs = [me] + operands, [pl.BlockSpec(memory_space=pltpu.SMEM)] + in_specs
         out_shape = jax.ShapeDtypeStruct((blocks, HS, 2 * HALF), jnp.bfloat16)
         scratch = [pltpu.VMEM(shape, jnp.bfloat16) for shape in kept_shapes]
-        scratch.append(pltpu.VMEM((LANES, max(spans)), jnp.float32))
+        scratch.append(pltpu.VMEM((total - stores[0][0].shape[0], LANES), jnp.bfloat16))
         out_specs = vmem
     else:
-        out_shape = [jax.ShapeDtypeStruct((old + fresh, LANES), jnp.float32)]
+        out_shape = [jax.ShapeDtypeStruct((old if stores else fresh, LANES), jnp.float32)]
         out_shape += [jax.ShapeDtypeStruct(shape, jnp.bfloat16) for shape in kept_shapes]
         scratch = []
         out_specs = [vmem] * 4
     return pl.pallas_call(
         functools.partial(
-            attend_kernel,
-            pieces=len(packed),
-            olds=len(stores),
-            last=last,
-            spans=spans,
+            attend_kernel, pieces=len(packed), olds=len(stores), last=last, span=span
         ),
         in_specs=in_specs,
         out_specs=out_specs,
@@ -430,7 +437,7 @@
     me, kept = lax.optimization_barrier((me, kept))
     rows, normed, own_w, w_mine = gather_rows(kept, document, gain_attn[None], heads)
 
-    a3, a1, b0 = along(normed, 1), along(normed, 3), flip(normed, 2)
+    b0, a1, a3 = flip(normed, 2), along(normed, 3), along(normed, 1)
     other_w = flip(own_w, 1)
 
     def trade(blocks):
@@ -450,7 +457,7 @@
     a3, a1, b0, p1, p2, p3 = lax.optimization_barrier((a3, a1, b0, p1, p2, p3))
     r1, r2, r3 = along(p1, 1), along(p2, 3), flip(p3, 2)
     own1, other1 = trade([a3, a1, b0])
-    state, *store = attend([own0, own1, other0, other1], [], None, (1024,))
+    state, *store = attend([own0, own1, other0, other1])
     r1, r2, r3, state = lax.optimization_barrier((r1, r2, r3, state))
     q1, q2, q3 = rearrange(
         [r1, r2, r3],
@@ -465,11 +472,12 @@
     own2, other2 = trade([r1, r2, r3])
     w_pair, own2 = lax.optimization_barrier((w_pair, own2))
     w_side = lax.ppermute(w_pair, "ctx", [(i, i ^ 4) for i in range(ctx_count)])
-    t1, t2, t3, w_side = lax.optimization_barrier((t1, t2, t3, w_side))
+    state, *later = attend([own2, other2], [store], state)
+    t1, t2, t3, w_side, state = lax.optimization_barrier((t1, t2, t3, w_side, state))
     own3, other3 = trade([t1, t2, t3])
     (w_quad,) = rearrange([w_pair, w_side], [((0, 0, 2 * count), (1, 0, 2 * count))])
     w_rest = lax.ppermute(w_quad, "ctx", [(i, i ^ 12) for i in range(ctx_count)])
-    mixed = attend([own2, own3, other2, other3], [store], state, (1024, 1024), me, ctx_count)
+    mixed = attend([own3, other3], [store, later], state, me, ctx_count)
     w_quad, w_rest, mixed = lax.optimization_barrier((w_quad, w_rest, mixed))
     (w_near,) = rearrange([w_quad, w_rest], [((0, 0, 4 * count), (1, 0, 4 * count))])
     w_far = flip(w_near, 1)

time: 146 us -> 141 us (0.966)
  waiting for transfers between devices: 17.5 us -> 12.6 us
    ppermute x9, waiting for transfers between devices: 9.28 us -> 2.29 us  [flip(): return lax.ppermute(value, 'ctx', [(i, i ^ bit) for i in range(ctx_count)])]
    ppermute x1, waiting for transfers between devices: 0.01 us -> 1.84 us  [body(): lax.ppermute(w_quad, 'ctx', [(i, i ^ 12) for i in range(ctx_count)])]
    all_to_all x1, blocking collectives: 13.8 us -> 12.4 us  [body(): lax.all_to_all(mixed, 'ctx', split_axis=0, concat_axis=0, tiled=True)]
    pallas_call x2 -> x3, Pallas kernels: 23.8 us -> 23.7 us  [attend(): pl.pallas_call(functools.partial(attend_kernel, pieces=len(packed), olds=...]
  transfers between devices with their start and end apart: 18 -> 18, of which waited for: 7 -> 5; matrix products, arithmetic and copies ran while one was open for 0% -> 0% of each run, Pallas kernels for 19% -> 18%
where the time goes in v5:
time: 141 us
  blocking collectives  63.7 us (45%)
  Pallas kernels  40 us (28%)
  starting transfers between devices  24.2 us (17%)
  waiting for transfers between devices  12.6 us (9%)
    all_to_all x1, blocking collectives, body(): got = lax.all_to_all(send, names, split_axis=0, concat_axis=0, tiled=True)  28.3 us
    pallas_call x3, Pallas kernels, attend(): pl.pallas_call(functools.partial(attend_kernel, pieces=len(packed), olds=...  23.7 us
    all_to_all x1, blocking collectives, body(): lax.all_to_all(answer, names, split_axis=0, concat_axis=0, tiled=True)  23.1 us
    ppermute x9, starting transfers between devices, flip(): return lax.ppermute(value, 'ctx', [(i, i ^ bit) for i in range(ctx_count)])  12.8 us
    all_to_all x1, blocking collectives, body(): lax.all_to_all(mixed, 'ctx', split_axis=0, concat_axis=0, tiled=True)  12.4 us
    ppermute x6, waiting for transfers between devices, along(): return lax.ppermute(value, 'ctx', pairs)  8.49 us
    ppermute x6, starting transfers between devices, along(): return lax.ppermute(value, 'ctx', pairs)  8.11 us
    pallas_call x1, Pallas kernels, run_expert(): pl.pallas_call(expert_kernel, in_specs=[vmem] * 3, out_specs=vmem, out_sh...  6.16 us
  transfers between devices with their start and end apart: 18, of which 5 were waited for; matrix products, arithmetic and copies ran while one was open for 0% of the time, Pallas kernels for 18%

profile of v5, /device:TPU:1, one launch (start us, length us, event | category | flops | bytes accessed | tf_op | source)
XLA Modules:
  0.0 140.9 jit_solution(13843135885430404408)
XLA Ops:
  0.0 2.7 %gather_rows.1 = (bf16[256,1024]{1,0:T(8,128)(2,1)}, bf16[256,1024]{1,0:T(8,128)(2,1)S(1)}, bf16[256,1024]{1,0:T(8,128)(2,1)S(1)}, bf16[64,1024]{1,0:T(8,128)(2,1)S(1)}) custom-call(s32[1,256]{1,0:T(1,128)} %kept_ref, bf16[512,1024]{1,0:T(8,128)(2,1)} %bitcast.15, f32[1,1024]{1,0:T(1,128)} %bitcast.32, bf16[64,1024]{1,0:T(8,128)(2,1)} %bitcast.29, ...), custom_call_target="tpu_custom_call" | custom-call | flops 268435456 | bytes 2097152 | tf_op jit(solution)/shard_map/gather_rows/pallas_call | solution.py:82
  2.7 1.5 %collective-permute-start.3 = (bf16[256,1024]{1,0:T(8,128)(2,1)S(1)}, bf16[256,1024]{1,0:T(8,128)(2,1)S(1)}, u32[]{:S(2)}, u32[]{:S(2)}) collective-permute-start(bf16[256,1024]{1,0:T(8,128)(2,1)S(1)} %get-tuple-element.73.refs_1_.refs_3_), channel_id=1, source_target_pairs={{0,1},{1,0},{2,3},{3,2},{4,5},{5,4},{6,7},{7,6},{8,9},{9,8},{10,11... | collective-permute-start | bytes 1572872 | tf_op jit(solution)/shard_map/ppermute | solution.py:434
  4.2 1.3 collective-permute-start
  5.5 1.4 collective-permute-start.1
  6.9 1.4 collective-permute-start.2
  8.8 2.0 %collective-permute-start.4 = (bf16[64,1024]{1,0:T(8,128)(2,1)S(1)}, bf16[64,1024]{1,0:T(8,128)(2,1)S(1)}, u32[]{:S(2)}, u32[]{:S(2)}) collective-permute-start(bf16[64,1024]{1,0:T(8,128)(2,1)S(1)} %get-tuple-element.75.refs_3_), channel_id=1, source_target_pairs={{0,18},{1,19},{2,16},{3,17},{4,22},{5,23},{6,20},{7,21},{8,26},{9,... | collective-permute-start | bytes 393224 | tf_op jit(solution)/shard_map/ppermute | solution.py:449
  10.7 8.2 %collective-permute-done.refs_0_ = bf16[256,1024]{1,0:T(8,128)(2,1)S(1)} collective-permute-done((bf16[256,1024]{1,0:T(8,128)(2,1)S(1)}, bf16[256,1024]{1,0:T(8,128)(2,1)S(1)}, u32[]{:S(2)}, u32[]{:S(2)}) %collective-permute-start) | collective-permute-done | bytes 524320 | tf_op jit(solution)/shard_map/ppermute | solution.py:431
  20.1 2.5 %collective-permute-start.6 = (bf16[256,1024]{1,0:T(8,128)(2,1)S(1)}, bf16[256,1024]{1,0:T(8,128)(2,1)S(1)}, u32[]{:S(2)}, u32[]{:S(2)}) collective-permute-start(bf16[256,1024]{1,0:T(8,128)(2,1)S(1)} %get-tuple-element.85), channel_id=1, source_target_pairs={{0,12},{1,13},{2,14},{3,15},{4,0},{5,1},{6,2},{7,3},{8,4},{9,5},{1... | collective-permute-start | bytes 1572872 | tf_op jit(solution)/shard_map/ppermute | solution.py:431
  22.6 1.4 collective-permute-start.7
  25.0 2.4 %collective-permute-start.9 = (bf16[768,256]{1,0:T(8,128)(2,1)S(1)}, bf16[768,256]{1,0:T(8,128)(2,1)S(1)}, u32[]{:S(2)}, u32[]{:S(2)}) collective-permute-start(bf16[768,256]{1,0:T(8,128)(2,1)S(1)} %get-tuple-element.93), channel_id=1, source_target_pairs={{0,1},{1,0},{2,3},{3,2},{4,5},{5,4},{6,7},{7,6},{8,9},{9,8},{10,11... | collective-permute-start | bytes 1179656 | tf_op jit(solution)/shard_map/ppermute | solution.py:434
  27.5 1.4 %collective-permute-done.8.refs_2_ = bf16[256,256]{1,0:T(8,128)(2,1)S(1)} collective-permute-done((bf16[256,256]{1,0:T(8,128)(2,1)S(1)}, bf16[256,256]{1,0:T(8,128)(2,1)S(1)}, u32[]{:S(2)}, u32[]{:S(2)}) %collective-permute-start.8) | collective-permute-done | bytes 131104 | tf_op jit(solution)/shard_map/ppermute | solution.py:434
  29.0 5.5 %attend_heads.3 = (f32[2048,128]{1,0:T(8,128)S(1)}, bf16[2048,128]{1,0:T(8,128)(2,1)S(1)}, bf16[128,2048]{1,0:T(8,128)(2,1)S(1)}, bf16[2048,128]{1,0:T(8,128)(2,1)S(1)}) custom-call(bf16[256,256]{1,0:T(8,128)(2,1)S(1)} %get-tuple-element.87.refs_0_, bf16[768,256]{1,0:T(8,128)(2,1)S(1)} %get-tuple-element.91.refs_1_, ...), custom_call_target="tpu_custom_call" | custom-call | flops 1 | bytes 1 | tf_op jit(solution)/shard_map/attend_heads/pallas_call | solution.py:282
  35.6 2.5 %collective-permute-start.14 = (bf16[768,256]{1,0:T(8,128)(2,1)S(1)}, bf16[768,256]{1,0:T(8,128)(2,1)S(1)}, u32[]{:S(2)}, u32[]{:S(2)}) collective-permute-start(bf16[768,256]{1,0:T(8,128)(2,1)S(1)} %get-tuple-element.110), channel_id=1, source_target_pairs={{0,1},{1,0},{2,3},{3,2},{4,5},{5,4},{6,7},{7,6},{8,9},{9,8},{10,11... | collective-permute-start | bytes 1179656 | tf_op jit(solution)/shard_map/ppermute | solution.py:434
  38.1 1.4 collective-permute-start.11
  39.5 1.5 %collective-permute-start.10 = (bf16[48,1024]{1,0:T(8,128)(2,1)S(1)}, bf16[48,1024]{1,0:T(8,128)(2,1)S(1)}, u32[]{:S(2)}, u32[]{:S(2)}) collective-permute-start(bf16[48,1024]{1,0:T(8,128)(2,1)S(1)} %get-tuple-element.106), channel_id=1, source_target_pairs={{0,4},{1,5},{2,6},{3,7},{4,8},{5,9},{6,10},{7,11},{8,12},{9,13},{1... | collective-permute-start | bytes 294920 | tf_op jit(solution)/shard_map/ppermute | solution.py:431
  42.2 6.6 %attend_heads.4 = (f32[2048,128]{1,0:T(8,128)S(1)}, bf16[1536,128]{1,0:T(8,128)(2,1)S(1)}, bf16[128,1536]{1,0:T(8,128)(2,1)S(1)}, bf16[1536,128]{1,0:T(8,128)(2,1)S(1)}) custom-call(bf16[768,256]{1,0:T(8,128)(2,1)S(1)} %get-tuple-element.109.refs_0_, bf16[768,256]{1,0:T(8,128)(2,1)S(1)} %collective-permute-done.14.refs_1_, ...), custom_call_target="tpu_custom_call" | custom-call | flops 1 | bytes 1 | tf_op jit(solution)/shard_map/attend_heads/pallas_call | solution.py:282
  52.9 11.6 %attend_heads.5 = bf16[16,64,256]{2,1,0:T(8,128)(2,1)S(1)} custom-call(s32[1]{0:T(128)} %bitcast.refs_0_.me_ref, bf16[256,256]{1,0:T(8,128)(2,1)S(1)} %get-tuple-element.120.refs_1_, bf16[256,256]{1,0:T(8,128)(2,1)S(1)} %collective-permute-done.16.refs_2_, bf16[2048,128]{1,0:T(8,128)(2,1)S(1)} %get-tuple-element.111.refs_2_.refs_3_, ...), custom_call_target="tpu_custom_call" | custom-call | flops 68719476736 | bytes 8388608 | tf_op jit(solution)/shard_map/attend_heads/pallas_call | solution.py:282
  64.5 1.8 %collective-permute-done.15.refs_1_ = bf16[256,1024]{1,0:T(8,128)(2,1)S(1)} collective-permute-done((bf16[256,1024]{1,0:T(8,128)(2,1)S(1)}, bf16[256,1024]{1,0:T(8,128)(2,1)S(1)}, u32[]{:S(2)}, u32[]{:S(2)}) %collective-permute-start.15) | collective-permute-done | bytes 524320 | tf_op jit(solution)/shard_map/ppermute | solution.py:479
  67.3 12.4 %all_to_all.15.mixed_ref = bf16[16,64,256]{2,1,0:T(8,128)(2,1)S(1)} all-to-all(bf16[16,64,256]{2,1,0:T(8,128)(2,1)S(1)} %attend_heads.5), channel_id=1, replica_groups=mesh['dp'=8,'ctx'=16] {'ctx'}, dimensions={0} | all-to-all | bytes 1048576 | tf_op jit(solution)/shard_map/all_to_all | solution.py:484
  79.7 1.6 %dispatch_rows.1 = (f32[256,1024]{1,0:T(8,128)S(1)}, bf16[1024,512]{1,0:T(8,128)(2,1)S(1)}, s32[1,256]{1,0:T(1,128)S(1)}) custom-call(s32[1]{0:T(128)} %bitcast.refs_0_.me_ref, bf16[16,64,256]{2,1,0:T(8,128)(2,1)S(1)} %all_to_all.15.mixed_ref, bf16[512,1024]{1,0:T(8,128)(2,1)S(1)} %rearrange_rows.7.near_ref, ...), custom_call_target="tpu_custom_call" | custom-call | flops 1073741824 | bytes 4718592 | tf_op jit(solution)/shard_map/dispatch_rows/pallas_call | solution.py:332
  81.3 28.3 %all_to_all.16 = bf16[128,8,512]{2,1,0:T(8,128)(2,1)S(1)} all-to-all(bf16[128,8,512]{2,1,0:T(8,128)(2,1)S(1)} %bitcast.18), channel_id=1, replica_groups=mesh['dp'=8,'ctx'=16] {'dp','ctx'}, dimensions={0} | all-to-all | bytes 2097152 | tf_op jit(solution)/shard_map/all_to_all | solution.py:492
  109.6 6.2 %run_expert.1 = bf16[1024,512]{1,0:T(8,128)(2,1)S(1)} custom-call(bf16[1024,512]{1,0:T(8,128)(2,1)S(1)} %bitcast.19, bf16[1024,2816]{1,0:T(8,128)(2,1)S(1)} %bitcast.23, bf16[2816,1024]{1,0:T(8,128)(2,1)S(1)} %bitcast.26), custom_call_target="tpu_custom_call" | custom-call | flops 5905580032 | bytes 13631488 | tf_op jit(solution)/shard_map/run_expert/pallas_call | solution.py:375
  115.8 23.1 %all_to_all.17 = bf16[128,8,512]{2,1,0:T(8,128)(2,1)S(1)} all-to-all(bf16[128,8,512]{2,1,0:T(8,128)(2,1)S(1)} %bitcast.20), channel_id=1, replica_groups=mesh['dp'=8,'ctx'=16] {'dp','ctx'}, dimensions={0} | all-to-all | bytes 2097152 | tf_op jit(solution)/shard_map/all_to_all | solution.py:495
  138.9 2.0 %combine_rows.1 = bf16[512,1024]{1,0:T(8,128)(2,1)} custom-call(bf16[1024,512]{1,0:T(8,128)(2,1)S(1)} %bitcast.17, s32[1,256]{1,0:T(1,128)S(1)} %get-tuple-element.131.place_ref, f32[256,1024]{1,0:T(8,128)S(1)} %get-tuple-element.132.first_ref, s32[1,256]{1,0:T(1,128)S(1)} %copy-done.1, bf16[512,1024]{1,0:T(8,128)(2,1)S(1)} %bitcast.16), custom_call_target="tpu_custom_call" | custom-call | flops 805306368 | bytes 3145728 | tf_op jit(solution)/shard_map/combine_rows/pallas_call | solution.py:410
  (50 shorter events, 10.0 us)
Async XLA Ops:
  2.7 5.6 %collective-permute-start.3 = (bf16[256,1024]{1,0:T(8,128)(2,1)S(1)}, bf16[256,1024]{1,0:T(8,128)(2,1)S(1)}, u32[]{:S(2)}, u32[]{:S(2)}) collective-permute-start(bf16[256,1024]{1,0:T(8,128)(2,1)S(1)} %get-tuple-element.73.refs_1_.refs_3_), channel_id=1, source_target_pairs={{0,1},{1,0},{2,3},{3,2},{4,5},{5,4},{6,7},{7,6},{8,9},{9,8},{10,11... | collective-permute-start | bytes 1572872 | tf_op jit(solution)/shard_map/ppermute | solution.py:434
  4.2 14.7 %collective-permute-start = (bf16[256,1024]{1,0:T(8,128)(2,1)S(1)}, bf16[256,1024]{1,0:T(8,128)(2,1)S(1)}, u32[]{:S(2)}, u32[]{:S(2)}) collective-permute-start(bf16[256,1024]{1,0:T(8,128)(2,1)S(1)} %get-tuple-element.71.refs_0_), channel_id=1, source_target_pairs={{0,4},{1,5},{2,6},{3,7},{4,8},{5,9},{6,10},{7,11},{8,12},{9,13},{1... | collective-permute-start | bytes 1572872 | tf_op jit(solution)/shard_map/ppermute | solution.py:431
  5.5 13.4 %collective-permute-start.1 = (bf16[256,1024]{1,0:T(8,128)(2,1)S(1)}, bf16[256,1024]{1,0:T(8,128)(2,1)S(1)}, u32[]{:S(2)}, u32[]{:S(2)}) collective-permute-start(bf16[256,1024]{1,0:T(8,128)(2,1)S(1)} %get-tuple-element.71.refs_0_), channel_id=1, source_target_pairs={{0,12},{1,13},{2,14},{3,15},{4,0},{5,1},{6,2},{7,3},{8,4},{9,5},{1... | collective-permute-start | bytes 1572872 | tf_op jit(solution)/shard_map/ppermute | solution.py:431
  6.9 12.8 %collective-permute-start.2 = (bf16[256,1024]{1,0:T(8,128)(2,1)S(1)}, bf16[256,1024]{1,0:T(8,128)(2,1)S(1)}, u32[]{:S(2)}, u32[]{:S(2)}) collective-permute-start(bf16[256,1024]{1,0:T(8,128)(2,1)S(1)} %get-tuple-element.71.refs_0_), channel_id=1, source_target_pairs={{0,2},{1,3},{2,0},{3,1},{4,6},{5,7},{6,4},{7,5},{8,10},{9,11},{10,... | collective-permute-start | bytes 1572872 | tf_op jit(solution)/shard_map/ppermute | solution.py:434
  8.8 11.0 %collective-permute-start.4 = (bf16[64,1024]{1,0:T(8,128)(2,1)S(1)}, bf16[64,1024]{1,0:T(8,128)(2,1)S(1)}, u32[]{:S(2)}, u32[]{:S(2)}) collective-permute-start(bf16[64,1024]{1,0:T(8,128)(2,1)S(1)} %get-tuple-element.75.refs_3_), channel_id=1, source_target_pairs={{0,18},{1,19},{2,16},{3,17},{4,22},{5,23},{6,20},{7,21},{8,26},{9,... | collective-permute-start | bytes 393224 | tf_op jit(solution)/shard_map/ppermute | solution.py:449
  19.9 14.6 %collective-permute-start.5 = (bf16[256,1024]{1,0:T(8,128)(2,1)S(1)}, bf16[256,1024]{1,0:T(8,128)(2,1)S(1)}, u32[]{:S(2)}, u32[]{:S(2)}) collective-permute-start(bf16[256,1024]{1,0:T(8,128)(2,1)S(1)} %get-tuple-element.84), channel_id=1, source_target_pairs={{0,4},{1,5},{2,6},{3,7},{4,8},{5,9},{6,10},{7,11},{8,12},{9,13},{1... | collective-permute-start | bytes 1572872 | tf_op jit(solution)/shard_map/ppermute | solution.py:431
  20.1 14.4 %collective-permute-start.6 = (bf16[256,1024]{1,0:T(8,128)(2,1)S(1)}, bf16[256,1024]{1,0:T(8,128)(2,1)S(1)}, u32[]{:S(2)}, u32[]{:S(2)}) collective-permute-start(bf16[256,1024]{1,0:T(8,128)(2,1)S(1)} %get-tuple-element.85), channel_id=1, source_target_pairs={{0,12},{1,13},{2,14},{3,15},{4,0},{5,1},{6,2},{7,3},{8,4},{9,5},{1... | collective-permute-start | bytes 1572872 | tf_op jit(solution)/shard_map/ppermute | solution.py:431
  22.6 11.9 %collective-permute-start.7 = (bf16[256,1024]{1,0:T(8,128)(2,1)S(1)}, bf16[256,1024]{1,0:T(8,128)(2,1)S(1)}, u32[]{:S(2)}, u32[]{:S(2)}) collective-permute-start(bf16[256,1024]{1,0:T(8,128)(2,1)S(1)} %get-tuple-element.86), channel_id=1, source_target_pairs={{0,2},{1,3},{2,0},{3,1},{4,6},{5,7},{6,4},{7,5},{8,10},{9,11},{10,... | collective-permute-start | bytes 1572872 | tf_op jit(solution)/shard_map/ppermute | solution.py:434
  25.0 4.0 %collective-permute-start.9 = (bf16[768,256]{1,0:T(8,128)(2,1)S(1)}, bf16[768,256]{1,0:T(8,128)(2,1)S(1)}, u32[]{:S(2)}, u32[]{:S(2)}) collective-permute-start(bf16[768,256]{1,0:T(8,128)(2,1)S(1)} %get-tuple-element.93), channel_id=1, source_target_pairs={{0,1},{1,0},{2,3},{3,2},{4,5},{5,4},{6,7},{7,6},{8,9},{9,8},{10,11... | collective-permute-start | bytes 1179656 | tf_op jit(solution)/shard_map/ppermute | solution.py:434
  27.4 1.5 %collective-permute-start.8 = (bf16[256,256]{1,0:T(8,128)(2,1)S(1)}, bf16[256,256]{1,0:T(8,128)(2,1)S(1)}, u32[]{:S(2)}, u32[]{:S(2)}) collective-permute-start(bf16[256,256]{1,0:T(8,128)(2,1)S(1)} %get-tuple-element.92), channel_id=1, source_target_pairs={{0,1},{1,0},{2,3},{3,2},{4,5},{5,4},{6,7},{7,6},{8,9},{9,8},{10,11... | collective-permute-start | bytes 393224 | tf_op jit(solution)/shard_map/ppermute | solution.py:434
  35.6 6.6 %collective-permute-start.14 = (bf16[768,256]{1,0:T(8,128)(2,1)S(1)}, bf16[768,256]{1,0:T(8,128)(2,1)S(1)}, u32[]{:S(2)}, u32[]{:S(2)}) collective-permute-start(bf16[768,256]{1,0:T(8,128)(2,1)S(1)} %get-tuple-element.110), channel_id=1, source_target_pairs={{0,1},{1,0},{2,3},{3,2},{4,5},{5,4},{6,7},{7,6},{8,9},{9,8},{10,11... | collective-permute-start | bytes 1179656 | tf_op jit(solution)/shard_map/ppermute | solution.py:434
  38.1 11.0 %collective-permute-start.11 = (bf16[160,1024]{1,0:T(8,128)(2,1)S(1)}, bf16[160,1024]{1,0:T(8,128)(2,1)S(1)}, u32[]{:S(2)}, u32[]{:S(2)}) collective-permute-start(bf16[160,1024]{1,0:T(8,128)(2,1)S(1)} %get-tuple-element.107), channel_id=1, source_target_pairs={{0,2},{1,3},{2,0},{3,1},{4,6},{5,7},{6,4},{7,5},{8,10},{9,11},{10,... | collective-permute-start | bytes 983048 | tf_op jit(solution)/shard_map/ppermute | solution.py:434
  39.5 9.6 %collective-permute-start.13 = (bf16[128,1024]{1,0:T(8,128)(2,1)S(1)}, bf16[128,1024]{1,0:T(8,128)(2,1)S(1)}, u32[]{:S(2)}, u32[]{:S(2)}) collective-permute-start(bf16[128,1024]{1,0:T(8,128)(2,1)S(1)} %get-tuple-element.105.refs_0_), channel_id=1, source_target_pairs={{0,4},{1,5},{2,6},{3,7},{4,0},{5,1},{6,2},{7,3},{8,12},{9,13},{10,... | collective-permute-start | bytes 786440 | tf_op jit(solution)/shard_map/ppermute | solution.py:474
  39.5 9.3 %collective-permute-start.10 = (bf16[48,1024]{1,0:T(8,128)(2,1)S(1)}, bf16[48,1024]{1,0:T(8,128)(2,1)S(1)}, u32[]{:S(2)}, u32[]{:S(2)}) collective-permute-start(bf16[48,1024]{1,0:T(8,128)(2,1)S(1)} %get-tuple-element.106), channel_id=1, source_target_pairs={{0,4},{1,5},{2,6},{3,7},{4,8},{5,9},{6,10},{7,11},{8,12},{9,13},{1... | collective-permute-start | bytes 294920 | tf_op jit(solution)/shard_map/ppermute | solution.py:431
  41.0 8.2 %collective-permute-start.12 = (bf16[48,1024]{1,0:T(8,128)(2,1)S(1)}, bf16[48,1024]{1,0:T(8,128)(2,1)S(1)}, u32[]{:S(2)}, u32[]{:S(2)}) collective-permute-start(bf16[48,1024]{1,0:T(8,128)(2,1)S(1)} %get-tuple-element.108), channel_id=1, source_target_pairs={{0,12},{1,13},{2,14},{3,15},{4,0},{5,1},{6,2},{7,3},{8,4},{9,5},{1... | collective-permute-start | bytes 294920 | tf_op jit(solution)/shard_map/ppermute | solution.py:431
  50.2 2.6 %collective-permute-start.16 = (bf16[256,256]{1,0:T(8,128)(2,1)S(1)}, bf16[256,256]{1,0:T(8,128)(2,1)S(1)}, u32[]{:S(2)}, u32[]{:S(2)}) collective-permute-start(bf16[256,256]{1,0:T(8,128)(2,1)S(1)} %get-tuple-element.121), channel_id=1, source_target_pairs={{0,1},{1,0},{2,3},{3,2},{4,5},{5,4},{6,7},{7,6},{8,9},{9,8},{10,11... | collective-permute-start | bytes 393224 | tf_op jit(solution)/shard_map/ppermute | solution.py:434
  51.5 14.8 %collective-permute-start.15 = (bf16[256,1024]{1,0:T(8,128)(2,1)S(1)}, bf16[256,1024]{1,0:T(8,128)(2,1)S(1)}, u32[]{:S(2)}, u32[]{:S(2)}) collective-permute-start(bf16[256,1024]{1,0:T(8,128)(2,1)S(1)} %rearrange_rows.6.refs_0_), channel_id=1, source_target_pairs={{0,12},{1,13},{2,14},{3,15},{4,8},{5,9},{6,10},{7,11},{8,4},{9,5},... | collective-permute-start | bytes 1572872 | tf_op jit(solution)/shard_map/ppermute | solution.py:479
  52.8 56.7 %slice-start = ((s8[5767168]{0:T(1024)(128)(4,1)}), s8[4194304]{0:T(1024)(128)(4,1)S(1)}, s32[]{:S(2)}) async-start(s8[5767168]{0:T(1024)(128)(4,1)} %bitcast.21), calls=%async_computation.3 | async-start | bytes 8388608
  52.8 56.7 %slice-start.2 = ((s8[5767168]{0:T(1024)(128)(4,1)}), s8[4194304]{0:T(1024)(128)(4,1)S(1)}, s32[]{:S(2)}) async-start(s8[5767168]{0:T(1024)(128)(4,1)} %bitcast.24), calls=%async_computation.5 | async-start | bytes 8388608
  52.9 56.7 %slice-start.1 = ((s8[5767168]{0:T(1024)(128)(4,1)}), s8[1572864]{0:T(1024)(128)(4,1)S(1)}, s32[]{:S(2)}) async-start(s8[5767168]{0:T(1024)(128)(4,1)} %bitcast.21), calls=%async_computation.4 | async-start | bytes 3145728
  52.9 56.7 %slice-start.3 = ((s8[5767168]{0:T(1024)(128)(4,1)}), s8[1572864]{0:T(1024)(128)(4,1)S(1)}, s32[]{:S(2)}) async-start(s8[5767168]{0:T(1024)(128)(4,1)} %bitcast.24), calls=%async_computation.6 | async-start | bytes 3145728
  66.4 13.2 %collective-permute-start.17 = (bf16[512,1024]{1,0:T(8,128)(2,1)S(1)}, bf16[512,1024]{1,0:T(8,128)(2,1)S(1)}, u32[]{:S(2)}, u32[]{:S(2)}) collective-permute-start(bf16[512,1024]{1,0:T(8,128)(2,1)S(1)} %rearrange_rows.7.near_ref), channel_id=1, source_target_pairs={{0,1},{1,0},{2,3},{3,2},{4,5},{5,4},{6,7},{7,6},{8,9},{9,8},{10,11... | collective-permute-start | bytes 3145736 | tf_op jit(solution)/shard_map/ppermute | solution.py:434
  109.6 29.3 %copy-start = (bf16[1,512,1024]{2,1,0:T(8,128)(2,1)S(1)}, bf16[1,512,1024]{2,1,0:T(8,128)(2,1)}, u32[]{:S(2)}) copy-start(bf16[1,512,1024]{2,1,0:T(8,128)(2,1)} %param.11) | copy-start | bytes 3145732
  109.6 29.3 %copy-start.1 = (s32[1,256]{1,0:T(1,128)S(1)}, s32[1,256]{1,0:T(1,128)}, u32[]{:S(2)}) copy-start(s32[1,256]{1,0:T(1,128)} %kept_ref) | copy-start | bytes 3076
  (3 other events, 80.5 us)

commit v6 on v5

--- a/solution.py
+++ b/solution.py
@@ -20,7 +20,7 @@
 B0, B1, B2, B3 = (0, 1), (1, 1), (2, 1), (3, 1)
 EARLY = [(c, h) for c in (A0, A3, A1, B0) for h in (0, 1)]
 LATE = [(A2, 0), (B3, 0), (A2, 1), (B1, 0), (B1, 1), (B3, 1), (B2, 0), (B2, 1)]
-THIRD, REST = 48, 208
+PART = 96
 
 
 def params(limit):
@@ -459,22 +459,15 @@
     own1, other1 = trade([a3, a1, b0])
     state, *store = attend([own0, own1, other0, other1])
     r1, r2, r3, state = lax.optimization_barrier((r1, r2, r3, state))
-    q1, q2, q3 = rearrange(
-        [r1, r2, r3],
-        [
-            ((0, HALF, THIRD),),
-            ((0, THIRD, HALF - THIRD), (1, 0, REST - HALF)),
-            ((2, REST - HALF, keep - REST),),
-        ],
-    )
-    r1, r2, r3, q1, q2, q3 = lax.optimization_barrier((r1, r2, r3, q1, q2, q3))
-    t1, t2, t3 = along(q1, 1), flip(q2, 2), along(q3, 3)
+    q1, q2 = rearrange([r1, r2], [((0, HALF, PART),), ((0, PART, HALF - PART), (1, 0, HALF))])
+    r1, r2, r3, q1, q2 = lax.optimization_barrier((r1, r2, r3, q1, q2))
+    t1, t2 = along(q1, 1), flip(q2, 2)
     own2, other2 = trade([r1, r2, r3])
     w_pair, own2 = lax.optimization_barrier((w_pair, own2))
     w_side = lax.ppermute(w_pair, "ctx", [(i, i ^ 4) for i in range(ctx_count)])
     state, *later = attend([own2, other2], [store], state)
-    t1, t2, t3, w_side, state = lax.optimization_barrier((t1, t2, t3, w_side, state))
-    own3, other3 = trade([t1, t2, t3])
+    t1, t2, w_side, state = lax.optimization_barrier((t1, t2, w_side, state))
+    own3, other3 = trade([t1, t2])
     (w_quad,) = rearrange([w_pair, w_side], [((0, 0, 2 * count), (1, 0, 2 * count))])
     w_rest = lax.ppermute(w_quad, "ctx", [(i, i ^ 12) for i in range(ctx_count)])
     mixed = attend([own3, other3], [store, later], state, me, ctx_count)

time: 141 us -> 143 us (1.014)
  blocking collectives: 63.7 us -> 65.2 us
    ppermute x1, starting transfers between devices: 1.3 us -> 3.49 us  [body(): lax.ppermute(w_quad, 'ctx', [(i, i ^ 12) for i in range(ctx_count)])]
    ppermute x6 -> x5, waiting for transfers between devices: 8.49 us -> 9.95 us  [along(): return lax.ppermute(value, 'ctx', pairs)]
    ppermute x6 -> x5, starting transfers between devices: 8.11 us -> 6.9 us  [along(): return lax.ppermute(value, 'ctx', pairs)]
  transfers between devices with their start and end apart: 18 -> 17, of which waited for: 5 -> 5; matrix products, arithmetic and copies ran while one was open for 0% -> 0% of each run, Pallas kernels for 18% -> 18%
where the time goes in v6:
time: 143 us
  blocking collectives  65.2 us (46%)
  Pallas kernels  39.7 us (28%)
  starting transfers between devices  24.7 us (17%)
  waiting for transfers between devices  12.8 us (9%)
    all_to_all x1, blocking collectives, body(): got = lax.all_to_all(send, names, split_axis=0, concat_axis=0, tiled=True)  28.3 us
    pallas_call x3, Pallas kernels, attend(): pl.pallas_call(functools.partial(attend_kernel, pieces=len(packed), olds=...  23.7 us
    all_to_all x1, blocking collectives, body(): lax.all_to_all(answer, names, split_axis=0, concat_axis=0, tiled=True)  23.1 us
    all_to_all x1, blocking collectives, body(): lax.all_to_all(mixed, 'ctx', split_axis=0, concat_axis=0, tiled=True)  13.8 us
    ppermute x9, starting transfers between devices, flip(): return lax.ppermute(value, 'ctx', [(i, i ^ bit) for i in range(ctx_count)])  12.3 us
    ppermute x5, waiting for transfers between devices, along(): return lax.ppermute(value, 'ctx', pairs)  9.95 us
    ppermute x5, starting transfers between devices, along(): return lax.ppermute(value, 'ctx', pairs)  6.9 us
    pallas_call x1, Pallas kernels, run_expert(): pl.pallas_call(expert_kernel, in_specs=[vmem] * 3, out_specs=vmem, out_sh...  6.16 us
  transfers between devices with their start and end apart: 17, of which 5 were waited for; matrix products, arithmetic and copies ran while one was open for 0% of the time, Pallas kernels for 18%

profile of v6, /device:TPU:1, one launch (start us, length us, event | category | flops | bytes accessed | tf_op | source)
XLA Modules:
  0.0 142.7 jit_solution(2765377265334662579)
XLA Ops:
  0.0 2.7 %gather_rows.1 = (bf16[256,1024]{1,0:T(8,128)(2,1)}, bf16[256,1024]{1,0:T(8,128)(2,1)S(1)}, bf16[256,1024]{1,0:T(8,128)(2,1)S(1)}, bf16[64,1024]{1,0:T(8,128)(2,1)S(1)}) custom-call(s32[1,256]{1,0:T(1,128)} %kept_ref, bf16[512,1024]{1,0:T(8,128)(2,1)} %bitcast.15, f32[1,1024]{1,0:T(1,128)} %bitcast.32, bf16[64,1024]{1,0:T(8,128)(2,1)} %bitcast.29, ...), custom_call_target="tpu_custom_call" | custom-call | flops 268435456 | bytes 2097152 | tf_op jit(solution)/shard_map/gather_rows/pallas_call | solution.py:82
  2.7 1.5 %collective-permute-start.3 = (bf16[256,1024]{1,0:T(8,128)(2,1)S(1)}, bf16[256,1024]{1,0:T(8,128)(2,1)S(1)}, u32[]{:S(2)}, u32[]{:S(2)}) collective-permute-start(bf16[256,1024]{1,0:T(8,128)(2,1)S(1)} %get-tuple-element.70.refs_1_.refs_3_.refs_2_), channel_id=1, source_target_pairs={{0,1},{1,0},{2,3},{3,2},{4,5},{5,4},{6,7},{7,6},{8,9},{9,8},{10,11... | collective-permute-start | bytes 1572872 | tf_op jit(solution)/shard_map/ppermute | solution.py:434
  5.5 1.4 collective-permute-start.1
  6.9 1.4 collective-permute-start.2
  8.8 2.0 %collective-permute-start.4 = (bf16[64,1024]{1,0:T(8,128)(2,1)S(1)}, bf16[64,1024]{1,0:T(8,128)(2,1)S(1)}, u32[]{:S(2)}, u32[]{:S(2)}) collective-permute-start(bf16[64,1024]{1,0:T(8,128)(2,1)S(1)} %get-tuple-element.72.refs_3_), channel_id=1, source_target_pairs={{0,18},{1,19},{2,16},{3,17},{4,22},{5,23},{6,20},{7,21},{8,26},{9,... | collective-permute-start | bytes 393224 | tf_op jit(solution)/shard_map/ppermute | solution.py:449
  10.7 8.2 %collective-permute-done.refs_0_ = bf16[256,1024]{1,0:T(8,128)(2,1)S(1)} collective-permute-done((bf16[256,1024]{1,0:T(8,128)(2,1)S(1)}, bf16[256,1024]{1,0:T(8,128)(2,1)S(1)}, u32[]{:S(2)}, u32[]{:S(2)}) %collective-permute-start) | collective-permute-done | bytes 524320 | tf_op jit(solution)/shard_map/ppermute | solution.py:431
  20.1 2.5 %collective-permute-start.6 = (bf16[256,1024]{1,0:T(8,128)(2,1)S(1)}, bf16[256,1024]{1,0:T(8,128)(2,1)S(1)}, u32[]{:S(2)}, u32[]{:S(2)}) collective-permute-start(bf16[256,1024]{1,0:T(8,128)(2,1)S(1)} %get-tuple-element.82), channel_id=1, source_target_pairs={{0,12},{1,13},{2,14},{3,15},{4,0},{5,1},{6,2},{7,3},{8,4},{9,5},{1... | collective-permute-start | bytes 1572872 | tf_op jit(solution)/shard_map/ppermute | solution.py:431
  22.6 1.4 collective-permute-start.7
  25.0 2.4 %collective-permute-start.9 = (bf16[768,256]{1,0:T(8,128)(2,1)S(1)}, bf16[768,256]{1,0:T(8,128)(2,1)S(1)}, u32[]{:S(2)}, u32[]{:S(2)}) collective-permute-start(bf16[768,256]{1,0:T(8,128)(2,1)S(1)} %get-tuple-element.90), channel_id=1, source_target_pairs={{0,1},{1,0},{2,3},{3,2},{4,5},{5,4},{6,7},{7,6},{8,9},{9,8},{10,11... | collective-permute-start | bytes 1179656 | tf_op jit(solution)/shard_map/ppermute | solution.py:434
  27.5 1.4 %collective-permute-done.8.refs_2_ = bf16[256,256]{1,0:T(8,128)(2,1)S(1)} collective-permute-done((bf16[256,256]{1,0:T(8,128)(2,1)S(1)}, bf16[256,256]{1,0:T(8,128)(2,1)S(1)}, u32[]{:S(2)}, u32[]{:S(2)}) %collective-permute-start.8) | collective-permute-done | bytes 131104 | tf_op jit(solution)/shard_map/ppermute | solution.py:434
  29.0 5.5 %attend_heads.3 = (f32[2048,128]{1,0:T(8,128)S(1)}, bf16[2048,128]{1,0:T(8,128)(2,1)S(1)}, bf16[128,2048]{1,0:T(8,128)(2,1)S(1)}, bf16[2048,128]{1,0:T(8,128)(2,1)S(1)}) custom-call(bf16[256,256]{1,0:T(8,128)(2,1)S(1)} %get-tuple-element.84.refs_0_, bf16[768,256]{1,0:T(8,128)(2,1)S(1)} %get-tuple-element.88.refs_1_, ...), custom_call_target="tpu_custom_call" | custom-call | flops 1 | bytes 1 | tf_op jit(solution)/shard_map/attend_heads/pallas_call | solution.py:282
  35.6 2.5 %collective-permute-start.13 = (bf16[768,256]{1,0:T(8,128)(2,1)S(1)}, bf16[768,256]{1,0:T(8,128)(2,1)S(1)}, u32[]{:S(2)}, u32[]{:S(2)}) collective-permute-start(bf16[768,256]{1,0:T(8,128)(2,1)S(1)} %get-tuple-element.105), channel_id=1, source_target_pairs={{0,1},{1,0},{2,3},{3,2},{4,5},{5,4},{6,7},{7,6},{8,9},{9,8},{10,11... | collective-permute-start | bytes 1179656 | tf_op jit(solution)/shard_map/ppermute | solution.py:434
  38.1 1.4 collective-permute-start.11
  39.5 1.5 %collective-permute-start.10 = (bf16[96,1024]{1,0:T(8,128)(2,1)S(1)}, bf16[96,1024]{1,0:T(8,128)(2,1)S(1)}, u32[]{:S(2)}, u32[]{:S(2)}) collective-permute-start(bf16[96,1024]{1,0:T(8,128)(2,1)S(1)} %get-tuple-element.102), channel_id=1, source_target_pairs={{0,4},{1,5},{2,6},{3,7},{4,8},{5,9},{6,10},{7,11},{8,12},{9,13},{1... | collective-permute-start | bytes 589832 | tf_op jit(solution)/shard_map/ppermute | solution.py:431
  41.0 6.6 %attend_heads.4 = (f32[2048,128]{1,0:T(8,128)S(1)}, bf16[1536,128]{1,0:T(8,128)(2,1)S(1)}, bf16[128,1536]{1,0:T(8,128)(2,1)S(1)}, bf16[1536,128]{1,0:T(8,128)(2,1)S(1)}) custom-call(bf16[768,256]{1,0:T(8,128)(2,1)S(1)} %get-tuple-element.104.refs_0_, bf16[768,256]{1,0:T(8,128)(2,1)S(1)} %collective-permute-done.13.refs_1_, ...), custom_call_target="tpu_custom_call" | custom-call | flops 1 | bytes 1 | tf_op jit(solution)/shard_map/attend_heads/pallas_call | solution.py:282
  47.6 1.8 %collective-permute-done.10.refs_0_ = bf16[96,1024]{1,0:T(8,128)(2,1)S(1)} collective-permute-done((bf16[96,1024]{1,0:T(8,128)(2,1)S(1)}, bf16[96,1024]{1,0:T(8,128)(2,1)S(1)}, u32[]{:S(2)}, u32[]{:S(2)}) %collective-permute-start.10) | collective-permute-done | bytes 196640 | tf_op jit(solution)/shard_map/ppermute | solution.py:431
  51.2 3.5 %collective-permute-start.14 = (bf16[256,1024]{1,0:T(8,128)(2,1)S(1)}, bf16[256,1024]{1,0:T(8,128)(2,1)S(1)}, u32[]{:S(2)}, u32[]{:S(2)}) collective-permute-start(bf16[256,1024]{1,0:T(8,128)(2,1)S(1)} %rearrange_rows.6.refs_0_), channel_id=1, source_target_pairs={{0,12},{1,13},{2,14},{3,15},{4,8},{5,9},{6,10},{7,11},{8,4},{9,5},... | collective-permute-start | bytes 1572872 | tf_op jit(solution)/shard_map/ppermute | solution.py:472
  54.7 11.6 %attend_heads.5 = bf16[16,64,256]{2,1,0:T(8,128)(2,1)S(1)} custom-call(s32[1]{0:T(128)} %bitcast.refs_0_.me_ref, bf16[256,256]{1,0:T(8,128)(2,1)S(1)} %get-tuple-element.114.refs_1_, bf16[256,256]{1,0:T(8,128)(2,1)S(1)} %collective-permute-done.15.refs_2_, bf16[2048,128]{1,0:T(8,128)(2,1)S(1)} %get-tuple-element.106.refs_2_.refs_3_, ...), custom_call_target="tpu_custom_call" | custom-call | flops 68719476736 | bytes 8388608 | tf_op jit(solution)/shard_map/attend_heads/pallas_call | solution.py:282
  67.7 13.8 %all_to_all.15.mixed_ref = bf16[16,64,256]{2,1,0:T(8,128)(2,1)S(1)} all-to-all(bf16[16,64,256]{2,1,0:T(8,128)(2,1)S(1)} %attend_heads.5), channel_id=1, replica_groups=mesh['dp'=8,'ctx'=16] {'ctx'}, dimensions={0} | all-to-all | bytes 1048576 | tf_op jit(solution)/shard_map/all_to_all | solution.py:477
  81.5 1.6 %dispatch_rows.1 = (f32[256,1024]{1,0:T(8,128)S(1)}, bf16[1024,512]{1,0:T(8,128)(2,1)S(1)}, s32[1,256]{1,0:T(1,128)S(1)}) custom-call(s32[1]{0:T(128)} %bitcast.refs_0_.me_ref, bf16[16,64,256]{2,1,0:T(8,128)(2,1)S(1)} %all_to_all.15.mixed_ref, bf16[512,1024]{1,0:T(8,128)(2,1)S(1)} %rearrange_rows.7.near_ref, ...), custom_call_target="tpu_custom_call" | custom-call | flops 1073741824 | bytes 4718592 | tf_op jit(solution)/shard_map/dispatch_rows/pallas_call | solution.py:332
  83.1 28.3 %all_to_all.16 = bf16[128,8,512]{2,1,0:T(8,128)(2,1)S(1)} all-to-all(bf16[128,8,512]{2,1,0:T(8,128)(2,1)S(1)} %bitcast.18), channel_id=1, replica_groups=mesh['dp'=8,'ctx'=16] {'dp','ctx'}, dimensions={0} | all-to-all | bytes 2097152 | tf_op jit(solution)/shard_map/all_to_all | solution.py:485
  111.5 6.2 %run_expert.1 = bf16[1024,512]{1,0:T(8,128)(2,1)S(1)} custom-call(bf16[1024,512]{1,0:T(8,128)(2,1)S(1)} %bitcast.19, bf16[1024,2816]{1,0:T(8,128)(2,1)S(1)} %bitcast.23, bf16[2816,1024]{1,0:T(8,128)(2,1)S(1)} %bitcast.26), custom_call_target="tpu_custom_call" | custom-call | flops 5905580032 | bytes 13631488 | tf_op jit(solution)/shard_map/run_expert/pallas_call | solution.py:375
  117.6 23.1 %all_to_all.17 = bf16[128,8,512]{2,1,0:T(8,128)(2,1)S(1)} all-to-all(bf16[128,8,512]{2,1,0:T(8,128)(2,1)S(1)} %bitcast.20), channel_id=1, replica_groups=mesh['dp'=8,'ctx'=16] {'dp','ctx'}, dimensions={0} | all-to-all | bytes 2097152 | tf_op jit(solution)/shard_map/all_to_all | solution.py:488
  140.7 2.0 %combine_rows.1 = bf16[512,1024]{1,0:T(8,128)(2,1)} custom-call(bf16[1024,512]{1,0:T(8,128)(2,1)S(1)} %bitcast.17, s32[1,256]{1,0:T(1,128)S(1)} %get-tuple-element.125.place_ref, f32[256,1024]{1,0:T(8,128)S(1)} %get-tuple-element.126.first_ref, s32[1,256]{1,0:T(1,128)S(1)} %copy-done.1, bf16[512,1024]{1,0:T(8,128)(2,1)S(1)} %bitcast.16), custom_call_target="tpu_custom_call" | custom-call | flops 805306368 | bytes 3145728 | tf_op jit(solution)/shard_map/combine_rows/pallas_call | solution.py:410
  (48 shorter events, 8.3 us)
Async XLA Ops:
  2.7 5.6 %collective-permute-start.3 = (bf16[256,1024]{1,0:T(8,128)(2,1)S(1)}, bf16[256,1024]{1,0:T(8,128)(2,1)S(1)}, u32[]{:S(2)}, u32[]{:S(2)}) collective-permute-start(bf16[256,1024]{1,0:T(8,128)(2,1)S(1)} %get-tuple-element.70.refs_1_.refs_3_.refs_2_), channel_id=1, source_target_pairs={{0,1},{1,0},{2,3},{3,2},{4,5},{5,4},{6,7},{7,6},{8,9},{9,8},{10,11... | collective-permute-start | bytes 1572872 | tf_op jit(solution)/shard_map/ppermute | solution.py:434
  4.2 14.7 %collective-permute-start = (bf16[256,1024]{1,0:T(8,128)(2,1)S(1)}, bf16[256,1024]{1,0:T(8,128)(2,1)S(1)}, u32[]{:S(2)}, u32[]{:S(2)}) collective-permute-start(bf16[256,1024]{1,0:T(8,128)(2,1)S(1)} %get-tuple-element.68.refs_0_), channel_id=1, source_target_pairs={{0,4},{1,5},{2,6},{3,7},{4,8},{5,9},{6,10},{7,11},{8,12},{9,13},{1... | collective-permute-start | bytes 1572872 | tf_op jit(solution)/shard_map/ppermute | solution.py:431
  5.5 13.4 %collective-permute-start.1 = (bf16[256,1024]{1,0:T(8,128)(2,1)S(1)}, bf16[256,1024]{1,0:T(8,128)(2,1)S(1)}, u32[]{:S(2)}, u32[]{:S(2)}) collective-permute-start(bf16[256,1024]{1,0:T(8,128)(2,1)S(1)} %get-tuple-element.68.refs_0_), channel_id=1, source_target_pairs={{0,12},{1,13},{2,14},{3,15},{4,0},{5,1},{6,2},{7,3},{8,4},{9,5},{1... | collective-permute-start | bytes 1572872 | tf_op jit(solution)/shard_map/ppermute | solution.py:431
  6.9 12.8 %collective-permute-start.2 = (bf16[256,1024]{1,0:T(8,128)(2,1)S(1)}, bf16[256,1024]{1,0:T(8,128)(2,1)S(1)}, u32[]{:S(2)}, u32[]{:S(2)}) collective-permute-start(bf16[256,1024]{1,0:T(8,128)(2,1)S(1)} %get-tuple-element.68.refs_0_), channel_id=1, source_target_pairs={{0,2},{1,3},{2,0},{3,1},{4,6},{5,7},{6,4},{7,5},{8,10},{9,11},{10,... | collective-permute-start | bytes 1572872 | tf_op jit(solution)/shard_map/ppermute | solution.py:434
  8.8 11.0 %collective-permute-start.4 = (bf16[64,1024]{1,0:T(8,128)(2,1)S(1)}, bf16[64,1024]{1,0:T(8,128)(2,1)S(1)}, u32[]{:S(2)}, u32[]{:S(2)}) collective-permute-start(bf16[64,1024]{1,0:T(8,128)(2,1)S(1)} %get-tuple-element.72.refs_3_), channel_id=1, source_target_pairs={{0,18},{1,19},{2,16},{3,17},{4,22},{5,23},{6,20},{7,21},{8,26},{9,... | collective-permute-start | bytes 393224 | tf_op jit(solution)/shard_map/ppermute | solution.py:449
  19.9 14.6 %collective-permute-start.5 = (bf16[256,1024]{1,0:T(8,128)(2,1)S(1)}, bf16[256,1024]{1,0:T(8,128)(2,1)S(1)}, u32[]{:S(2)}, u32[]{:S(2)}) collective-permute-start(bf16[256,1024]{1,0:T(8,128)(2,1)S(1)} %get-tuple-element.81), channel_id=1, source_target_pairs={{0,4},{1,5},{2,6},{3,7},{4,8},{5,9},{6,10},{7,11},{8,12},{9,13},{1... | collective-permute-start | bytes 1572872 | tf_op jit(solution)/shard_map/ppermute | solution.py:431
  20.1 14.4 %collective-permute-start.6 = (bf16[256,1024]{1,0:T(8,128)(2,1)S(1)}, bf16[256,1024]{1,0:T(8,128)(2,1)S(1)}, u32[]{:S(2)}, u32[]{:S(2)}) collective-permute-start(bf16[256,1024]{1,0:T(8,128)(2,1)S(1)} %get-tuple-element.82), channel_id=1, source_target_pairs={{0,12},{1,13},{2,14},{3,15},{4,0},{5,1},{6,2},{7,3},{8,4},{9,5},{1... | collective-permute-start | bytes 1572872 | tf_op jit(solution)/shard_map/ppermute | solution.py:431
  22.6 11.9 %collective-permute-start.7 = (bf16[256,1024]{1,0:T(8,128)(2,1)S(1)}, bf16[256,1024]{1,0:T(8,128)(2,1)S(1)}, u32[]{:S(2)}, u32[]{:S(2)}) collective-permute-start(bf16[256,1024]{1,0:T(8,128)(2,1)S(1)} %get-tuple-element.83), channel_id=1, source_target_pairs={{0,2},{1,3},{2,0},{3,1},{4,6},{5,7},{6,4},{7,5},{8,10},{9,11},{10,... | collective-permute-start | bytes 1572872 | tf_op jit(solution)/shard_map/ppermute | solution.py:434
  25.0 4.0 %collective-permute-start.9 = (bf16[768,256]{1,0:T(8,128)(2,1)S(1)}, bf16[768,256]{1,0:T(8,128)(2,1)S(1)}, u32[]{:S(2)}, u32[]{:S(2)}) collective-permute-start(bf16[768,256]{1,0:T(8,128)(2,1)S(1)} %get-tuple-element.90), channel_id=1, source_target_pairs={{0,1},{1,0},{2,3},{3,2},{4,5},{5,4},{6,7},{7,6},{8,9},{9,8},{10,11... | collective-permute-start | bytes 1179656 | tf_op jit(solution)/shard_map/ppermute | solution.py:434
  27.4 1.5 %collective-permute-start.8 = (bf16[256,256]{1,0:T(8,128)(2,1)S(1)}, bf16[256,256]{1,0:T(8,128)(2,1)S(1)}, u32[]{:S(2)}, u32[]{:S(2)}) collective-permute-start(bf16[256,256]{1,0:T(8,128)(2,1)S(1)} %get-tuple-element.89), channel_id=1, source_target_pairs={{0,1},{1,0},{2,3},{3,2},{4,5},{5,4},{6,7},{7,6},{8,9},{9,8},{10,11... | collective-permute-start | bytes 393224 | tf_op jit(solution)/shard_map/ppermute | solution.py:434
  35.6 5.4 %collective-permute-start.13 = (bf16[768,256]{1,0:T(8,128)(2,1)S(1)}, bf16[768,256]{1,0:T(8,128)(2,1)S(1)}, u32[]{:S(2)}, u32[]{:S(2)}) collective-permute-start(bf16[768,256]{1,0:T(8,128)(2,1)S(1)} %get-tuple-element.105), channel_id=1, source_target_pairs={{0,1},{1,0},{2,3},{3,2},{4,5},{5,4},{6,7},{7,6},{8,9},{9,8},{10,11... | collective-permute-start | bytes 1179656 | tf_op jit(solution)/shard_map/ppermute | solution.py:434
  38.1 11.3 %collective-permute-start.11 = (bf16[160,1024]{1,0:T(8,128)(2,1)S(1)}, bf16[160,1024]{1,0:T(8,128)(2,1)S(1)}, u32[]{:S(2)}, u32[]{:S(2)}) collective-permute-start(bf16[160,1024]{1,0:T(8,128)(2,1)S(1)} %get-tuple-element.103), channel_id=1, source_target_pairs={{0,2},{1,3},{2,0},{3,1},{4,6},{5,7},{6,4},{7,5},{8,10},{9,11},{10,... | collective-permute-start | bytes 983048 | tf_op jit(solution)/shard_map/ppermute | solution.py:434
  39.5 9.9 %collective-permute-start.12 = (bf16[128,1024]{1,0:T(8,128)(2,1)S(1)}, bf16[128,1024]{1,0:T(8,128)(2,1)S(1)}, u32[]{:S(2)}, u32[]{:S(2)}) collective-permute-start(bf16[128,1024]{1,0:T(8,128)(2,1)S(1)} %get-tuple-element.101.refs_0_), channel_id=1, source_target_pairs={{0,4},{1,5},{2,6},{3,7},{4,0},{5,1},{6,2},{7,3},{8,12},{9,13},{10,... | collective-permute-start | bytes 786440 | tf_op jit(solution)/shard_map/ppermute | solution.py:467
  39.5 9.9 %collective-permute-start.10 = (bf16[96,1024]{1,0:T(8,128)(2,1)S(1)}, bf16[96,1024]{1,0:T(8,128)(2,1)S(1)}, u32[]{:S(2)}, u32[]{:S(2)}) collective-permute-start(bf16[96,1024]{1,0:T(8,128)(2,1)S(1)} %get-tuple-element.102), channel_id=1, source_target_pairs={{0,4},{1,5},{2,6},{3,7},{4,8},{5,9},{6,10},{7,11},{8,12},{9,13},{1... | collective-permute-start | bytes 589832 | tf_op jit(solution)/shard_map/ppermute | solution.py:431
  50.2 4.5 %collective-permute-start.15 = (bf16[256,256]{1,0:T(8,128)(2,1)S(1)}, bf16[256,256]{1,0:T(8,128)(2,1)S(1)}, u32[]{:S(2)}, u32[]{:S(2)}) collective-permute-start(bf16[256,256]{1,0:T(8,128)(2,1)S(1)} %get-tuple-element.115), channel_id=1, source_target_pairs={{0,1},{1,0},{2,3},{3,2},{4,5},{5,4},{6,7},{7,6},{8,9},{9,8},{10,11... | collective-permute-start | bytes 393224 | tf_op jit(solution)/shard_map/ppermute | solution.py:434
  51.2 15.8 %collective-permute-start.14 = (bf16[256,1024]{1,0:T(8,128)(2,1)S(1)}, bf16[256,1024]{1,0:T(8,128)(2,1)S(1)}, u32[]{:S(2)}, u32[]{:S(2)}) collective-permute-start(bf16[256,1024]{1,0:T(8,128)(2,1)S(1)} %rearrange_rows.6.refs_0_), channel_id=1, source_target_pairs={{0,12},{1,13},{2,14},{3,15},{4,8},{5,9},{6,10},{7,11},{8,4},{9,5},... | collective-permute-start | bytes 1572872 | tf_op jit(solution)/shard_map/ppermute | solution.py:472
  54.7 56.7 %slice-start = ((s8[5767168]{0:T(1024)(128)(4,1)}), s8[4194304]{0:T(1024)(128)(4,1)S(1)}, s32[]{:S(2)}) async-start(s8[5767168]{0:T(1024)(128)(4,1)} %bitcast.21), calls=%async_computation.3 | async-start | bytes 8388608
  54.7 56.7 %slice-start.2 = ((s8[5767168]{0:T(1024)(128)(4,1)}), s8[4194304]{0:T(1024)(128)(4,1)S(1)}, s32[]{:S(2)}) async-start(s8[5767168]{0:T(1024)(128)(4,1)} %bitcast.24), calls=%async_computation.5 | async-start | bytes 8388608
  54.7 26.8 %copy-start.2 = (bf16[256,1024]{1,0:T(8,128)(2,1)S(1)}, bf16[256,1024]{1,0:T(8,128)(2,1)}, u32[]{:S(2)}) copy-start(bf16[256,1024]{1,0:T(8,128)(2,1)} %get-tuple-element.123.rows_ref) | copy-start | bytes 1572868
  54.7 56.7 %slice-start.1 = ((s8[5767168]{0:T(1024)(128)(4,1)}), s8[1572864]{0:T(1024)(128)(4,1)S(1)}, s32[]{:S(2)}) async-start(s8[5767168]{0:T(1024)(128)(4,1)} %bitcast.21), calls=%async_computation.4 | async-start | bytes 3145728
  54.7 56.7 %slice-start.3 = ((s8[5767168]{0:T(1024)(128)(4,1)}), s8[1572864]{0:T(1024)(128)(4,1)S(1)}, s32[]{:S(2)}) async-start(s8[5767168]{0:T(1024)(128)(4,1)} %bitcast.24), calls=%async_computation.6 | async-start | bytes 3145728
  67.0 14.4 %collective-permute-start.16 = (bf16[512,1024]{1,0:T(8,128)(2,1)S(1)}, bf16[512,1024]{1,0:T(8,128)(2,1)S(1)}, u32[]{:S(2)}, u32[]{:S(2)}) collective-permute-start(bf16[512,1024]{1,0:T(8,128)(2,1)S(1)} %rearrange_rows.7.near_ref), channel_id=1, source_target_pairs={{0,1},{1,0},{2,3},{3,2},{4,5},{5,4},{6,7},{7,6},{8,9},{9,8},{10,11... | collective-permute-start | bytes 3145736 | tf_op jit(solution)/shard_map/ppermute | solution.py:434
  111.4 29.3 %copy-start = (bf16[1,512,1024]{2,1,0:T(8,128)(2,1)S(1)}, bf16[1,512,1024]{2,1,0:T(8,128)(2,1)}, u32[]{:S(2)}) copy-start(bf16[1,512,1024]{2,1,0:T(8,128)(2,1)} %param.11) | copy-start | bytes 3145732
  111.4 29.3 %copy-start.1 = (s32[1,256]{1,0:T(1,128)S(1)}, s32[1,256]{1,0:T(1,128)}, u32[]{:S(2)}) copy-start(s32[1,256]{1,0:T(1,128)} %kept_ref) | copy-start | bytes 3076
  (2 other events, 53.6 us)

commit v7 on v5

--- a/solution.py
+++ b/solution.py
@@ -447,7 +447,7 @@
     own0, other0 = trade([normed])
     w_mine, own0 = lax.optimization_barrier((w_mine, own0))
     w_next = lax.ppermute(w_mine, ("dp", "ctx"), [(i, i ^ 18) for i in range(experts)])
-    a3, a1, b0, w_next = lax.optimization_barrier((a3, a1, b0, w_next))
+    a3, a1, b0, w_next, other0 = lax.optimization_barrier((a3, a1, b0, w_next, other0))
     low, high, left = (0, 0, HALF), (0, HALF, HALF), (1, HALF, HALF)
     count = w_out.shape[0]
     p1, p2, p3, w_pair = rearrange(

time: 141 us -> 141 us (level)
  no operation moved by 1% of the time
where the time goes in v7:
time: 141 us
  blocking collectives  63.8 us (45%)
  Pallas kernels  40 us (28%)
  starting transfers between devices  25.5 us (18%)
  waiting for transfers between devices  11.3 us (8%)
    all_to_all x1, blocking collectives, body(): got = lax.all_to_all(send, names, split_axis=0, concat_axis=0, tiled=True)  28.3 us
    pallas_call x3, Pallas kernels, attend(): pl.pallas_call(functools.partial(attend_kernel, pieces=len(packed), olds=...  23.8 us
    all_to_all x1, blocking collectives, body(): lax.all_to_all(answer, names, split_axis=0, concat_axis=0, tiled=True)  23.1 us
    ppermute x9, starting transfers between devices, flip(): return lax.ppermute(value, 'ctx', [(i, i ^ bit) for i in range(ctx_count)])  14.1 us
    all_to_all x1, blocking collectives, body(): lax.all_to_all(mixed, 'ctx', split_axis=0, concat_axis=0, tiled=True)  12.4 us
    ppermute x6, starting transfers between devices, along(): return lax.ppermute(value, 'ctx', pairs)  8.11 us
    ppermute x6, waiting for transfers between devices, along(): return lax.ppermute(value, 'ctx', pairs)  7.3 us
    pallas_call x1, Pallas kernels, run_expert(): pl.pallas_call(expert_kernel, in_specs=[vmem] * 3, out_specs=vmem, out_sh...  6.16 us
  transfers between devices with their start and end apart: 18, of which 5 were waited for; matrix products, arithmetic and copies ran while one was open for 0% of the time, Pallas kernels for 18%

profile of v7, /device:TPU:1, one launch (start us, length us, event | category | flops | bytes accessed | tf_op | source)
XLA Modules:
  0.0 140.9 jit_solution(10635475231226452621)
XLA Ops:
  0.0 2.7 %gather_rows.1 = (bf16[256,1024]{1,0:T(8,128)(2,1)}, bf16[256,1024]{1,0:T(8,128)(2,1)S(1)}, bf16[256,1024]{1,0:T(8,128)(2,1)S(1)}, bf16[64,1024]{1,0:T(8,128)(2,1)S(1)}) custom-call(s32[1,256]{1,0:T(1,128)} %kept_ref, bf16[512,1024]{1,0:T(8,128)(2,1)} %bitcast.15, f32[1,1024]{1,0:T(1,128)} %bitcast.32, bf16[64,1024]{1,0:T(8,128)(2,1)} %bitcast.29, ...), custom_call_target="tpu_custom_call" | custom-call | flops 268435456 | bytes 2097152 | tf_op jit(solution)/shard_map/gather_rows/pallas_call | solution.py:82
  2.7 1.5 %collective-permute-start.3 = (bf16[256,1024]{1,0:T(8,128)(2,1)S(1)}, bf16[256,1024]{1,0:T(8,128)(2,1)S(1)}, u32[]{:S(2)}, u32[]{:S(2)}) collective-permute-start(bf16[256,1024]{1,0:T(8,128)(2,1)S(1)} %get-tuple-element.74.refs_1_.refs_3_), channel_id=1, source_target_pairs={{0,1},{1,0},{2,3},{3,2},{4,5},{5,4},{6,7},{7,6},{8,9},{9,8},{10,11... | collective-permute-start | bytes 1572872 | tf_op jit(solution)/shard_map/ppermute | solution.py:434
  4.2 1.3 collective-permute-start
  5.5 1.4 collective-permute-start.1
  6.9 1.4 collective-permute-start.2
  8.8 2.0 %collective-permute-start.4 = (bf16[64,1024]{1,0:T(8,128)(2,1)S(1)}, bf16[64,1024]{1,0:T(8,128)(2,1)S(1)}, u32[]{:S(2)}, u32[]{:S(2)}) collective-permute-start(bf16[64,1024]{1,0:T(8,128)(2,1)S(1)} %get-tuple-element.76.refs_3_), channel_id=1, source_target_pairs={{0,18},{1,19},{2,16},{3,17},{4,22},{5,23},{6,20},{7,21},{8,26},{9,... | collective-permute-start | bytes 393224 | tf_op jit(solution)/shard_map/ppermute | solution.py:449
  11.9 7.0 %collective-permute-done.refs_0_ = bf16[256,1024]{1,0:T(8,128)(2,1)S(1)} collective-permute-done((bf16[256,1024]{1,0:T(8,128)(2,1)S(1)}, bf16[256,1024]{1,0:T(8,128)(2,1)S(1)}, u32[]{:S(2)}, u32[]{:S(2)}) %collective-permute-start) | collective-permute-done | bytes 524320 | tf_op jit(solution)/shard_map/ppermute | solution.py:431
  20.1 2.5 %collective-permute-start.7 = (bf16[256,1024]{1,0:T(8,128)(2,1)S(1)}, bf16[256,1024]{1,0:T(8,128)(2,1)S(1)}, u32[]{:S(2)}, u32[]{:S(2)}) collective-permute-start(bf16[256,1024]{1,0:T(8,128)(2,1)S(1)} %get-tuple-element.87), channel_id=1, source_target_pairs={{0,12},{1,13},{2,14},{3,15},{4,0},{5,1},{6,2},{7,3},{8,4},{9,5},{1... | collective-permute-start | bytes 1572872 | tf_op jit(solution)/shard_map/ppermute | solution.py:431
  22.6 1.4 collective-permute-start.8
  25.0 2.4 %collective-permute-start.9 = (bf16[768,256]{1,0:T(8,128)(2,1)S(1)}, bf16[768,256]{1,0:T(8,128)(2,1)S(1)}, u32[]{:S(2)}, u32[]{:S(2)}) collective-permute-start(bf16[768,256]{1,0:T(8,128)(2,1)S(1)} %get-tuple-element.95), channel_id=1, source_target_pairs={{0,1},{1,0},{2,3},{3,2},{4,5},{5,4},{6,7},{7,6},{8,9},{9,8},{10,11... | collective-permute-start | bytes 1179656 | tf_op jit(solution)/shard_map/ppermute | solution.py:434
  27.4 1.3 collective-permute-done.9.refs_3_
  28.8 5.5 %attend_heads.3 = (f32[2048,128]{1,0:T(8,128)S(1)}, bf16[2048,128]{1,0:T(8,128)(2,1)S(1)}, bf16[128,2048]{1,0:T(8,128)(2,1)S(1)}, bf16[2048,128]{1,0:T(8,128)(2,1)S(1)}) custom-call(bf16[256,256]{1,0:T(8,128)(2,1)S(1)} %get-tuple-element.89.refs_0_, bf16[768,256]{1,0:T(8,128)(2,1)S(1)} %get-tuple-element.93.refs_1_, ...), custom_call_target="tpu_custom_call" | custom-call | flops 1 | bytes 1 | tf_op jit(solution)/shard_map/attend_heads/pallas_call | solution.py:282
  35.4 2.7 %collective-permute-start.14 = (bf16[768,256]{1,0:T(8,128)(2,1)S(1)}, bf16[768,256]{1,0:T(8,128)(2,1)S(1)}, u32[]{:S(2)}, u32[]{:S(2)}) collective-permute-start(bf16[768,256]{1,0:T(8,128)(2,1)S(1)} %get-tuple-element.112), channel_id=1, source_target_pairs={{0,1},{1,0},{2,3},{3,2},{4,5},{5,4},{6,7},{7,6},{8,9},{9,8},{10,11... | collective-permute-start | bytes 1179656 | tf_op jit(solution)/shard_map/ppermute | solution.py:434
  38.1 1.4 collective-permute-start.11
  39.5 1.5 %collective-permute-start.10 = (bf16[48,1024]{1,0:T(8,128)(2,1)S(1)}, bf16[48,1024]{1,0:T(8,128)(2,1)S(1)}, u32[]{:S(2)}, u32[]{:S(2)}) collective-permute-start(bf16[48,1024]{1,0:T(8,128)(2,1)S(1)} %get-tuple-element.108), channel_id=1, source_target_pairs={{0,4},{1,5},{2,6},{3,7},{4,8},{5,9},{6,10},{7,11},{8,12},{9,13},{1... | collective-permute-start | bytes 294920 | tf_op jit(solution)/shard_map/ppermute | solution.py:431
  42.2 6.6 %attend_heads.4 = (f32[2048,128]{1,0:T(8,128)S(1)}, bf16[1536,128]{1,0:T(8,128)(2,1)S(1)}, bf16[128,1536]{1,0:T(8,128)(2,1)S(1)}, bf16[1536,128]{1,0:T(8,128)(2,1)S(1)}) custom-call(bf16[768,256]{1,0:T(8,128)(2,1)S(1)} %get-tuple-element.111.refs_0_, bf16[768,256]{1,0:T(8,128)(2,1)S(1)} %collective-permute-done.14.refs_1_, ...), custom_call_target="tpu_custom_call" | custom-call | flops 1 | bytes 1 | tf_op jit(solution)/shard_map/attend_heads/pallas_call | solution.py:282
  52.9 11.6 %attend_heads.5 = bf16[16,64,256]{2,1,0:T(8,128)(2,1)S(1)} custom-call(s32[1]{0:T(128)} %bitcast.refs_0_.me_ref, bf16[256,256]{1,0:T(8,128)(2,1)S(1)} %get-tuple-element.122.refs_1_, bf16[256,256]{1,0:T(8,128)(2,1)S(1)} %collective-permute-done.16.refs_2_, bf16[2048,128]{1,0:T(8,128)(2,1)S(1)} %get-tuple-element.113.refs_2_.refs_3_, ...), custom_call_target="tpu_custom_call" | custom-call | flops 68719476736 | bytes 8388608 | tf_op jit(solution)/shard_map/attend_heads/pallas_call | solution.py:282
  64.5 1.8 %collective-permute-done.15.refs_1_ = bf16[256,1024]{1,0:T(8,128)(2,1)S(1)} collective-permute-done((bf16[256,1024]{1,0:T(8,128)(2,1)S(1)}, bf16[256,1024]{1,0:T(8,128)(2,1)S(1)}, u32[]{:S(2)}, u32[]{:S(2)}) %collective-permute-start.15) | collective-permute-done | bytes 524320 | tf_op jit(solution)/shard_map/ppermute | solution.py:479
  67.3 12.4 %all_to_all.15.mixed_ref = bf16[16,64,256]{2,1,0:T(8,128)(2,1)S(1)} all-to-all(bf16[16,64,256]{2,1,0:T(8,128)(2,1)S(1)} %attend_heads.5), channel_id=1, replica_groups=mesh['dp'=8,'ctx'=16] {'ctx'}, dimensions={0} | all-to-all | bytes 1048576 | tf_op jit(solution)/shard_map/all_to_all | solution.py:484
  79.7 1.6 %dispatch_rows.1 = (f32[256,1024]{1,0:T(8,128)S(1)}, bf16[1024,512]{1,0:T(8,128)(2,1)S(1)}, s32[1,256]{1,0:T(1,128)S(1)}) custom-call(s32[1]{0:T(128)} %bitcast.refs_0_.me_ref, bf16[16,64,256]{2,1,0:T(8,128)(2,1)S(1)} %all_to_all.15.mixed_ref, bf16[512,1024]{1,0:T(8,128)(2,1)S(1)} %rearrange_rows.7.near_ref, ...), custom_call_target="tpu_custom_call" | custom-call | flops 1073741824 | bytes 4718592 | tf_op jit(solution)/shard_map/dispatch_rows/pallas_call | solution.py:332
  81.3 28.3 %all_to_all.16 = bf16[128,8,512]{2,1,0:T(8,128)(2,1)S(1)} all-to-all(bf16[128,8,512]{2,1,0:T(8,128)(2,1)S(1)} %bitcast.18), channel_id=1, replica_groups=mesh['dp'=8,'ctx'=16] {'dp','ctx'}, dimensions={0} | all-to-all | bytes 2097152 | tf_op jit(solution)/shard_map/all_to_all | solution.py:492
  109.6 6.2 %run_expert.1 = bf16[1024,512]{1,0:T(8,128)(2,1)S(1)} custom-call(bf16[1024,512]{1,0:T(8,128)(2,1)S(1)} %bitcast.19, bf16[1024,2816]{1,0:T(8,128)(2,1)S(1)} %bitcast.23, bf16[2816,1024]{1,0:T(8,128)(2,1)S(1)} %bitcast.26), custom_call_target="tpu_custom_call" | custom-call | flops 5905580032 | bytes 13631488 | tf_op jit(solution)/shard_map/run_expert/pallas_call | solution.py:375
  115.8 23.1 %all_to_all.17 = bf16[128,8,512]{2,1,0:T(8,128)(2,1)S(1)} all-to-all(bf16[128,8,512]{2,1,0:T(8,128)(2,1)S(1)} %bitcast.20), channel_id=1, replica_groups=mesh['dp'=8,'ctx'=16] {'dp','ctx'}, dimensions={0} | all-to-all | bytes 2097152 | tf_op jit(solution)/shard_map/all_to_all | solution.py:495
  138.9 2.0 %combine_rows.1 = bf16[512,1024]{1,0:T(8,128)(2,1)} custom-call(bf16[1024,512]{1,0:T(8,128)(2,1)S(1)} %bitcast.17, s32[1,256]{1,0:T(1,128)S(1)} %get-tuple-element.133.place_ref, f32[256,1024]{1,0:T(8,128)S(1)} %get-tuple-element.134.first_ref, s32[1,256]{1,0:T(1,128)S(1)} %copy-done.1, bf16[512,1024]{1,0:T(8,128)(2,1)S(1)} %bitcast.16), custom_call_target="tpu_custom_call" | custom-call | flops 805306368 | bytes 3145728 | tf_op jit(solution)/shard_map/combine_rows/pallas_call | solution.py:410
  (50 shorter events, 11.1 us)
Async XLA Ops:
  2.7 5.6 %collective-permute-start.3 = (bf16[256,1024]{1,0:T(8,128)(2,1)S(1)}, bf16[256,1024]{1,0:T(8,128)(2,1)S(1)}, u32[]{:S(2)}, u32[]{:S(2)}) collective-permute-start(bf16[256,1024]{1,0:T(8,128)(2,1)S(1)} %get-tuple-element.74.refs_1_.refs_3_), channel_id=1, source_target_pairs={{0,1},{1,0},{2,3},{3,2},{4,5},{5,4},{6,7},{7,6},{8,9},{9,8},{10,11... | collective-permute-start | bytes 1572872 | tf_op jit(solution)/shard_map/ppermute | solution.py:434
  4.2 14.7 %collective-permute-start = (bf16[256,1024]{1,0:T(8,128)(2,1)S(1)}, bf16[256,1024]{1,0:T(8,128)(2,1)S(1)}, u32[]{:S(2)}, u32[]{:S(2)}) collective-permute-start(bf16[256,1024]{1,0:T(8,128)(2,1)S(1)} %get-tuple-element.72.refs_0_), channel_id=1, source_target_pairs={{0,4},{1,5},{2,6},{3,7},{4,8},{5,9},{6,10},{7,11},{8,12},{9,13},{1... | collective-permute-start | bytes 1572872 | tf_op jit(solution)/shard_map/ppermute | solution.py:431
  5.5 13.4 %collective-permute-start.1 = (bf16[256,1024]{1,0:T(8,128)(2,1)S(1)}, bf16[256,1024]{1,0:T(8,128)(2,1)S(1)}, u32[]{:S(2)}, u32[]{:S(2)}) collective-permute-start(bf16[256,1024]{1,0:T(8,128)(2,1)S(1)} %get-tuple-element.72.refs_0_), channel_id=1, source_target_pairs={{0,12},{1,13},{2,14},{3,15},{4,0},{5,1},{6,2},{7,3},{8,4},{9,5},{1... | collective-permute-start | bytes 1572872 | tf_op jit(solution)/shard_map/ppermute | solution.py:431
  6.9 12.8 %collective-permute-start.2 = (bf16[256,1024]{1,0:T(8,128)(2,1)S(1)}, bf16[256,1024]{1,0:T(8,128)(2,1)S(1)}, u32[]{:S(2)}, u32[]{:S(2)}) collective-permute-start(bf16[256,1024]{1,0:T(8,128)(2,1)S(1)} %get-tuple-element.72.refs_0_), channel_id=1, source_target_pairs={{0,2},{1,3},{2,0},{3,1},{4,6},{5,7},{6,4},{7,5},{8,10},{9,11},{10,... | collective-permute-start | bytes 1572872 | tf_op jit(solution)/shard_map/ppermute | solution.py:434
  8.8 11.0 %collective-permute-start.4 = (bf16[64,1024]{1,0:T(8,128)(2,1)S(1)}, bf16[64,1024]{1,0:T(8,128)(2,1)S(1)}, u32[]{:S(2)}, u32[]{:S(2)}) collective-permute-start(bf16[64,1024]{1,0:T(8,128)(2,1)S(1)} %get-tuple-element.76.refs_3_), channel_id=1, source_target_pairs={{0,18},{1,19},{2,16},{3,17},{4,22},{5,23},{6,20},{7,21},{8,26},{9,... | collective-permute-start | bytes 393224 | tf_op jit(solution)/shard_map/ppermute | solution.py:449
  10.7 9.0 %collective-permute-start.5 = (bf16[256,256]{1,0:T(8,128)(2,1)S(1)}, bf16[256,256]{1,0:T(8,128)(2,1)S(1)}, u32[]{:S(2)}, u32[]{:S(2)}) collective-permute-start(bf16[256,256]{1,0:T(8,128)(2,1)S(1)} %get-tuple-element.77), channel_id=1, source_target_pairs={{0,1},{1,0},{2,3},{3,2},{4,5},{5,4},{6,7},{7,6},{8,9},{9,8},{10,11... | collective-permute-start | bytes 393224 | tf_op jit(solution)/shard_map/ppermute | solution.py:434
  19.9 14.4 %collective-permute-start.6 = (bf16[256,1024]{1,0:T(8,128)(2,1)S(1)}, bf16[256,1024]{1,0:T(8,128)(2,1)S(1)}, u32[]{:S(2)}, u32[]{:S(2)}) collective-permute-start(bf16[256,1024]{1,0:T(8,128)(2,1)S(1)} %get-tuple-element.86), channel_id=1, source_target_pairs={{0,4},{1,5},{2,6},{3,7},{4,8},{5,9},{6,10},{7,11},{8,12},{9,13},{1... | collective-permute-start | bytes 1572872 | tf_op jit(solution)/shard_map/ppermute | solution.py:431
  20.1 14.2 %collective-permute-start.7 = (bf16[256,1024]{1,0:T(8,128)(2,1)S(1)}, bf16[256,1024]{1,0:T(8,128)(2,1)S(1)}, u32[]{:S(2)}, u32[]{:S(2)}) collective-permute-start(bf16[256,1024]{1,0:T(8,128)(2,1)S(1)} %get-tuple-element.87), channel_id=1, source_target_pairs={{0,12},{1,13},{2,14},{3,15},{4,0},{5,1},{6,2},{7,3},{8,4},{9,5},{1... | collective-permute-start | bytes 1572872 | tf_op jit(solution)/shard_map/ppermute | solution.py:431
  22.6 11.7 %collective-permute-start.8 = (bf16[256,1024]{1,0:T(8,128)(2,1)S(1)}, bf16[256,1024]{1,0:T(8,128)(2,1)S(1)}, u32[]{:S(2)}, u32[]{:S(2)}) collective-permute-start(bf16[256,1024]{1,0:T(8,128)(2,1)S(1)} %get-tuple-element.88), channel_id=1, source_target_pairs={{0,2},{1,3},{2,0},{3,1},{4,6},{5,7},{6,4},{7,5},{8,10},{9,11},{10,... | collective-permute-start | bytes 1572872 | tf_op jit(solution)/shard_map/ppermute | solution.py:434
  25.0 3.8 %collective-permute-start.9 = (bf16[768,256]{1,0:T(8,128)(2,1)S(1)}, bf16[768,256]{1,0:T(8,128)(2,1)S(1)}, u32[]{:S(2)}, u32[]{:S(2)}) collective-permute-start(bf16[768,256]{1,0:T(8,128)(2,1)S(1)} %get-tuple-element.95), channel_id=1, source_target_pairs={{0,1},{1,0},{2,3},{3,2},{4,5},{5,4},{6,7},{7,6},{8,9},{9,8},{10,11... | collective-permute-start | bytes 1179656 | tf_op jit(solution)/shard_map/ppermute | solution.py:434
  35.4 6.8 %collective-permute-start.14 = (bf16[768,256]{1,0:T(8,128)(2,1)S(1)}, bf16[768,256]{1,0:T(8,128)(2,1)S(1)}, u32[]{:S(2)}, u32[]{:S(2)}) collective-permute-start(bf16[768,256]{1,0:T(8,128)(2,1)S(1)} %get-tuple-element.112), channel_id=1, source_target_pairs={{0,1},{1,0},{2,3},{3,2},{4,5},{5,4},{6,7},{7,6},{8,9},{9,8},{10,11... | collective-permute-start | bytes 1179656 | tf_op jit(solution)/shard_map/ppermute | solution.py:434
  38.1 11.0 %collective-permute-start.11 = (bf16[160,1024]{1,0:T(8,128)(2,1)S(1)}, bf16[160,1024]{1,0:T(8,128)(2,1)S(1)}, u32[]{:S(2)}, u32[]{:S(2)}) collective-permute-start(bf16[160,1024]{1,0:T(8,128)(2,1)S(1)} %get-tuple-element.109), channel_id=1, source_target_pairs={{0,2},{1,3},{2,0},{3,1},{4,6},{5,7},{6,4},{7,5},{8,10},{9,11},{10,... | collective-permute-start | bytes 983048 | tf_op jit(solution)/shard_map/ppermute | solution.py:434
  39.5 9.6 %collective-permute-start.13 = (bf16[128,1024]{1,0:T(8,128)(2,1)S(1)}, bf16[128,1024]{1,0:T(8,128)(2,1)S(1)}, u32[]{:S(2)}, u32[]{:S(2)}) collective-permute-start(bf16[128,1024]{1,0:T(8,128)(2,1)S(1)} %get-tuple-element.107.refs_0_), channel_id=1, source_target_pairs={{0,4},{1,5},{2,6},{3,7},{4,0},{5,1},{6,2},{7,3},{8,12},{9,13},{10,... | collective-permute-start | bytes 786440 | tf_op jit(solution)/shard_map/ppermute | solution.py:474
  39.5 9.3 %collective-permute-start.10 = (bf16[48,1024]{1,0:T(8,128)(2,1)S(1)}, bf16[48,1024]{1,0:T(8,128)(2,1)S(1)}, u32[]{:S(2)}, u32[]{:S(2)}) collective-permute-start(bf16[48,1024]{1,0:T(8,128)(2,1)S(1)} %get-tuple-element.108), channel_id=1, source_target_pairs={{0,4},{1,5},{2,6},{3,7},{4,8},{5,9},{6,10},{7,11},{8,12},{9,13},{1... | collective-permute-start | bytes 294920 | tf_op jit(solution)/shard_map/ppermute | solution.py:431
  41.0 8.2 %collective-permute-start.12 = (bf16[48,1024]{1,0:T(8,128)(2,1)S(1)}, bf16[48,1024]{1,0:T(8,128)(2,1)S(1)}, u32[]{:S(2)}, u32[]{:S(2)}) collective-permute-start(bf16[48,1024]{1,0:T(8,128)(2,1)S(1)} %get-tuple-element.110), channel_id=1, source_target_pairs={{0,12},{1,13},{2,14},{3,15},{4,0},{5,1},{6,2},{7,3},{8,4},{9,5},{1... | collective-permute-start | bytes 294920 | tf_op jit(solution)/shard_map/ppermute | solution.py:431
  50.2 2.6 %collective-permute-start.16 = (bf16[256,256]{1,0:T(8,128)(2,1)S(1)}, bf16[256,256]{1,0:T(8,128)(2,1)S(1)}, u32[]{:S(2)}, u32[]{:S(2)}) collective-permute-start(bf16[256,256]{1,0:T(8,128)(2,1)S(1)} %get-tuple-element.123), channel_id=1, source_target_pairs={{0,1},{1,0},{2,3},{3,2},{4,5},{5,4},{6,7},{7,6},{8,9},{9,8},{10,11... | collective-permute-start | bytes 393224 | tf_op jit(solution)/shard_map/ppermute | solution.py:434
  51.5 14.8 %collective-permute-start.15 = (bf16[256,1024]{1,0:T(8,128)(2,1)S(1)}, bf16[256,1024]{1,0:T(8,128)(2,1)S(1)}, u32[]{:S(2)}, u32[]{:S(2)}) collective-permute-start(bf16[256,1024]{1,0:T(8,128)(2,1)S(1)} %rearrange_rows.6.refs_0_), channel_id=1, source_target_pairs={{0,12},{1,13},{2,14},{3,15},{4,8},{5,9},{6,10},{7,11},{8,4},{9,5},... | collective-permute-start | bytes 1572872 | tf_op jit(solution)/shard_map/ppermute | solution.py:479
  52.8 56.7 %slice-start = ((s8[5767168]{0:T(1024)(128)(4,1)}), s8[4194304]{0:T(1024)(128)(4,1)S(1)}, s32[]{:S(2)}) async-start(s8[5767168]{0:T(1024)(128)(4,1)} %bitcast.21), calls=%async_computation.3 | async-start | bytes 8388608
  52.8 56.7 %slice-start.2 = ((s8[5767168]{0:T(1024)(128)(4,1)}), s8[4194304]{0:T(1024)(128)(4,1)S(1)}, s32[]{:S(2)}) async-start(s8[5767168]{0:T(1024)(128)(4,1)} %bitcast.24), calls=%async_computation.5 | async-start | bytes 8388608
  52.9 56.7 %slice-start.1 = ((s8[5767168]{0:T(1024)(128)(4,1)}), s8[1572864]{0:T(1024)(128)(4,1)S(1)}, s32[]{:S(2)}) async-start(s8[5767168]{0:T(1024)(128)(4,1)} %bitcast.21), calls=%async_computation.4 | async-start | bytes 3145728
  52.9 56.7 %slice-start.3 = ((s8[5767168]{0:T(1024)(128)(4,1)}), s8[1572864]{0:T(1024)(128)(4,1)S(1)}, s32[]{:S(2)}) async-start(s8[5767168]{0:T(1024)(128)(4,1)} %bitcast.24), calls=%async_computation.6 | async-start | bytes 3145728
  66.4 13.2 %collective-permute-start.17 = (bf16[512,1024]{1,0:T(8,128)(2,1)S(1)}, bf16[512,1024]{1,0:T(8,128)(2,1)S(1)}, u32[]{:S(2)}, u32[]{:S(2)}) collective-permute-start(bf16[512,1024]{1,0:T(8,128)(2,1)S(1)} %rearrange_rows.7.near_ref), channel_id=1, source_target_pairs={{0,1},{1,0},{2,3},{3,2},{4,5},{5,4},{6,7},{7,6},{8,9},{9,8},{10,11... | collective-permute-start | bytes 3145736 | tf_op jit(solution)/shard_map/ppermute | solution.py:434
  109.6 29.3 %copy-start = (bf16[1,512,1024]{2,1,0:T(8,128)(2,1)S(1)}, bf16[1,512,1024]{2,1,0:T(8,128)(2,1)}, u32[]{:S(2)}) copy-start(bf16[1,512,1024]{2,1,0:T(8,128)(2,1)} %param.11) | copy-start | bytes 3145732
  109.6 29.3 %copy-start.1 = (s32[1,256]{1,0:T(1,128)S(1)}, s32[1,256]{1,0:T(1,128)}, u32[]{:S(2)}) copy-start(s32[1,256]{1,0:T(1,128)} %kept_ref) | copy-start | bytes 3076
  (3 other events, 80.5 us)
